TPU v7x, 32 devices: a whole 2x2x4 slice. The times are simulated.
32 devices in a mesh: dp: 8 (over z, x), ctx: 4 (over y, core).
Axes of the slice: x: 2, y: 2, z: 4, core: 2. Of those that a mesh axis runs over, the one named last changes fastest.
Arguments:
- hidden: bfloat16 [8, 1024, 768], P('dp', 'ctx'), may hold values from -6 to 6
- teacher: bfloat16 [8, 1024, 768], P('dp', 'ctx'), may hold values from -12 to 12
- lengths: int32 [8], P('dp'), may hold values from 256 to 1024, as said below
- w_qkv: bfloat16 [768, 2304], P('dp'), may hold values from -0.21875 to 0.21875
- w_out: bfloat16 [768, 768], P('dp'), may hold values from -0.375 to 0.375
- w_up: bfloat16 [768, 3072], P('dp'), may hold values from -0.375 to 0.375
- w_down: bfloat16 [3072, 768], P('dp'), may hold values from -0.1875 to 0.1875
- norm_gain: bfloat16 [768, 3], P('dp'), may hold values from 0.099609375 to 1.8984375
- norm_shift: bfloat16 [768, 3], P('dp'), may hold values from -3 to 3
- proj_bias: bfloat16 [768, 4], P('dp'), may hold values from -3 to 3
- mid_gain: bfloat16 [3072], P('dp'), may hold values from 0.099609375 to 1.8984375
- mid_shift: bfloat16 [3072], P('dp'), may hold values from -3 to 3
- up_bias: bfloat16 [3072], P('dp'), may hold values from -3 to 3
Outputs:
- layer_output: bfloat16 [8, 1024, 768], P('dp', 'ctx')
- loss: float32 [], replicated
- hidden_grad: float32 [8, 1024, 768], P('dp', 'ctx')
- qkv_grad: float32 [768, 2304], P('dp')
- out_grad: float32 [768, 768], P('dp')
- up_grad: float32 [768, 3072], P('dp')
- down_grad: float32 [3072, 768], P('dp')
- gain_grad: float32 [768, 3], P('dp')
- shift_grad: float32 [768, 3], P('dp')
- bias_grad: float32 [768, 4], P('dp')
- mid_gain_grad: float32 [3072], P('dp')
- mid_shift_grad: float32 [3072], P('dp')
- up_bias_grad: float32 [3072], P('dp')
Inputs may be any that keep to these rules, and one draw needn't show every extreme that they name: Sequence s has valid tokens at positions 0 to lengths[s] - 1 and padding after them; some sequence has exactly 1024 and some exactly 256 valid tokens.
All inputs are finite; a program needn't handle non-finite values.
Results may differ from a plain program's by a relative error of at most 0.013.
Values may be sent and summed in bfloat16 or wider, within the bound.
No kernel may reach another device: no remote copies, remote signals or barrier semaphores. Data moves between devices by JAX's collectives and lax.ppermute only.
A program may use at most 192 MiB of HBM per device.

v0:
```python
import math

import jax
import jax.numpy as jnp
from jax import lax
from jax.sharding import PartitionSpec as P

HEADS = 12
HEAD_DIM = 64


EPSILON = 1e-05
NEGATIVE = -1e30


def passed_along(value, axis, steps):
    count = lax.axis_size(axis)
    pairs = [(source, (source + steps) % count) for source in range(count)]
    return lax.ppermute(value, axis, pairs)


def passed_along_2(block, axis, distance):
    devices = range(lax.axis_size(axis))
    route = [(i - distance, i) for i in devices if i - distance in devices]
    return lax.ppermute(block, axis, route)


def layer_norm(values, gain_vec, shift_vec):
    average = jnp.mean(values, axis=-1, keepdims=True)
    centred = values - average
    variance = jnp.mean(centred * centred, axis=-1, keepdims=True)
    return centred * lax.rsqrt(variance + EPSILON) * gain_vec + shift_vec


def mid_norm(up_proj, gain_vec, shift_vec):
    return layer_norm(jax.nn.gelu(up_proj, approximate=False), gain_vec, shift_vec)


def split_heads(values):
    return values.reshape(values.shape[0], values.shape[1], HEADS, HEAD_DIM)


def key_mask(query_pos, key_start, key_count, lengths):
    key_pos = key_start + jnp.arange(key_count, dtype=jnp.int32)
    causal = key_pos[None, :] <= query_pos[:, None]
    inside = key_pos[None, :] < lengths[:, None]
    return causal[None, :, :] & inside[:, None, :]


def fold_keys(running, pieces, key_start, heads_q, query_pos, lengths):
    row_max, row_total, weighted = running
    key_piece, value_piece = pieces
    key_count = key_piece.shape[1]
    score_scale = 1.0 / math.sqrt(HEAD_DIM)
    scores = (
        jnp.einsum(
            "sqhd,skhd->shqk", heads_q, split_heads(key_piece), preferred_element_type=jnp.float32
        )
        * score_scale
    )
    allowed = key_mask(query_pos, key_start, key_count, lengths)[:, None]
    scores = jnp.where(allowed, scores, NEGATIVE)
    fresh_max = jnp.maximum(row_max, jnp.max(scores, axis=-1))
    exponent_vals = jnp.exp(scores - fresh_max[..., None])
    row_total = jnp.sum(exponent_vals, axis=-1)
    update = jnp.einsum(
        "shqk,skhd->sqhd",
        exponent_vals.astype(jnp.bfloat16),
        split_heads(value_piece),
        preferred_element_type=jnp.float32,
    )
    weighted = update
    return (fresh_max, row_total, weighted)


def grad_keys(
    heads_q, heads_do, log_total, dterm, key_piece, value_piece, key_start, query_pos, lengths
):
    seq_count, key_count = (key_piece.shape[0], key_piece.shape[1])
    heads_k = split_heads(key_piece)
    heads_v = split_heads(value_piece)
    score_scale = 1.0 / math.sqrt(HEAD_DIM)
    scores = (
        jnp.einsum("sqhd,skhd->shqk", heads_q, heads_k, preferred_element_type=jnp.float32)
        * score_scale
    )
    allowed = key_mask(query_pos, key_start, key_count, lengths)[:, None]
    probability = jnp.where(allowed, jnp.exp(scores - log_total[..., None]), 0.0)
    dprob = jnp.einsum("sqhd,skhd->shqk", heads_do, heads_v, preferred_element_type=jnp.float32)
    dscores = (probability * (dprob - dterm[..., None])).astype(jnp.bfloat16)
    dq_part = (
        jnp.einsum("shqk,skhd->sqhd", dscores, heads_k, preferred_element_type=jnp.float32)
        * score_scale
    )
    dk_part = (
        jnp.einsum("shqk,sqhd->skhd", dscores, heads_q, preferred_element_type=jnp.float32)
        * score_scale
    )
    dv_part = jnp.einsum(
        "shqk,sqhd->skhd",
        probability.astype(jnp.bfloat16),
        heads_do,
        preferred_element_type=jnp.float32,
    )
    return (
        dq_part,
        dk_part.reshape(seq_count, key_count, -1),
        dv_part.reshape(seq_count, key_count, -1),
    )


def shards(
    hidden,
    teacher,
    lengths,
    w_qkv,
    w_out,
    w_up,
    w_down,
    norm_gain,
    norm_shift,
    proj_bias,
    mid_gain,
    mid_shift,
    up_bias,
):
    (
        full_qkv,
        full_out,
        full_up,
        full_down,
        gain_full,
        shift_full,
        bias_full,
        mid_gain_full,
        mid_shift_full,
        up_bias_full,
    ) = (
        lax.all_gather(w_qkv, "dp", axis=0, tiled=True),
        lax.all_gather(w_out, "dp", axis=0, tiled=True),
        lax.all_gather(w_up, "dp", axis=0, tiled=True),
        lax.all_gather(w_down, "dp", axis=0, tiled=True),
        lax.all_gather(norm_gain, "dp", axis=0, tiled=True),
        lax.all_gather(norm_shift, "dp", axis=0, tiled=True),
        lax.all_gather(proj_bias, "dp", axis=0, tiled=True),
        lax.all_gather(mid_gain, "dp", axis=0, tiled=True),
        lax.all_gather(mid_shift, "dp", axis=0, tiled=True),
        lax.all_gather(up_bias, "dp", axis=0, tiled=True),
    )
    gain_f = gain_full.astype(jnp.float32)
    shift_f = shift_full.astype(jnp.float32)
    bias_f = bias_full.astype(jnp.float32)
    mid_gain_f = mid_gain_full.astype(jnp.float32)
    mid_shift_f = mid_shift_full.astype(jnp.float32)
    up_bias_f = up_bias_full.astype(jnp.float32)
    seq_count, local_rows, model_width = hidden.shape
    token_rows = seq_count * local_rows
    seq_shape = (seq_count, local_rows, model_width)
    ctx_place = lax.axis_index("ctx")
    ctx_parts = lax.axis_size("ctx")
    query_pos = ctx_place * local_rows + jnp.arange(local_rows, dtype=jnp.int32)
    last_query = ctx_place * local_rows + local_rows - 1
    valid_mask = (query_pos[None, :] < lengths[:, None]).astype(jnp.float32)
    valid_rows = valid_mask.reshape(token_rows, 1)
    hidden_rows = hidden.reshape(token_rows, model_width).astype(jnp.float32)
    normed, pull_in = jax.vjp(layer_norm, hidden_rows, gain_f[:, 0], shift_f[:, 0])
    normed_low = normed.astype(jnp.bfloat16)
    projected = jnp.dot(normed_low, full_qkv, preferred_element_type=jnp.float32)
    query_low = (projected[:, :model_width] + bias_f[:, 0]).astype(jnp.bfloat16).reshape(seq_shape)
    key_low = projected[:, model_width : 2 * model_width].astype(jnp.bfloat16).reshape(seq_shape)
    value_low = (
        (projected[:, 2 * model_width :] + bias_f[:, 1]).astype(jnp.bfloat16).reshape(seq_shape)
    )
    heads_q = split_heads(query_low)
    start_state = (
        jnp.full((seq_count, HEADS, local_rows), NEGATIVE, jnp.float32),
        jnp.zeros((seq_count, HEADS, local_rows), jnp.float32),
        jnp.zeros((seq_count, local_rows, HEADS, HEAD_DIM), jnp.float32),
    )
    pieces = (
        lax.all_gather(key_low, "ctx", axis=1, tiled=True),
        lax.all_gather(value_low, "ctx", axis=1, tiled=True),
    )
    key_start = jnp.int32(0)
    row_max, row_total, weighted = lax.cond(
        key_start <= last_query,
        lambda: fold_keys(start_state, pieces, key_start, heads_q, query_pos, lengths),
        lambda: start_state,
    )
    attended = weighted / jnp.transpose(row_total, (0, 2, 1))[..., None]
    log_total = row_max + jnp.log(row_total)
    attended_rows = attended.reshape(token_rows, model_width)
    mixed, pull_mix = jax.vjp(layer_norm, attended_rows, gain_f[:, 1], shift_f[:, 1])
    mixed_low = mixed.astype(jnp.bfloat16)
    residual = (
        hidden_rows
        + jnp.dot(mixed_low, full_out, preferred_element_type=jnp.float32)
        + bias_f[:, 2]
    )
    ffn_in, pull_ffn = jax.vjp(layer_norm, residual, gain_f[:, 2], shift_f[:, 2])
    ffn_low = ffn_in.astype(jnp.bfloat16)
    up_proj = jnp.dot(ffn_low, full_up, preferred_element_type=jnp.float32) + up_bias_f
    activated, pull_mid = jax.vjp(mid_norm, up_proj, mid_gain_f, mid_shift_f)
    act_low = activated.astype(jnp.bfloat16)
    result = (
        residual + jnp.dot(act_low, full_down, preferred_element_type=jnp.float32) + bias_f[:, 3]
    )
    layer_output = (result * valid_rows).astype(jnp.bfloat16).reshape(hidden.shape)
    error_rows = (
        result - teacher.reshape(token_rows, model_width).astype(jnp.float32)
    ) * valid_rows
    loss_total, valid_total = lax.psum(
        (0.5 * jnp.sum(error_rows * error_rows), jnp.sum(valid_mask)), ("dp", "ctx")
    )
    loss = loss_total / (valid_total * model_width)
    down_low = error_rows.astype(jnp.bfloat16)
    bias_down_grad = jnp.sum(down_low.astype(jnp.float32), axis=0)
    down_grad = jnp.einsum("rf,rd->fd", act_low, down_low, preferred_element_type=jnp.float32)
    d_act = jnp.einsum("rd,fd->rf", down_low, full_down, preferred_element_type=jnp.float32)
    d_up, mid_gain_grad, mid_shift_grad = pull_mid(d_act)
    up_low = d_up.astype(jnp.bfloat16)
    up_bias_grad = jnp.sum(up_low.astype(jnp.float32), axis=0)
    up_grad = jnp.einsum("rd,rf->df", ffn_low, up_low, preferred_element_type=jnp.float32)
    d_ffn = jnp.einsum("rf,df->rd", up_low, full_up, preferred_element_type=jnp.float32)
    d_res_norm, gain_two, shift_two = pull_ffn(d_ffn)
    d_residual = error_rows + d_res_norm
    branch_low = d_residual.astype(jnp.bfloat16)
    bias_out_grad = jnp.sum(branch_low.astype(jnp.float32), axis=0)
    out_grad = jnp.einsum("rd,re->de", mixed_low, branch_low, preferred_element_type=jnp.float32)
    d_mixed = jnp.einsum("re,de->rd", branch_low, full_out, preferred_element_type=jnp.float32)
    d_att, gain_one, shift_one = pull_mix(d_mixed)
    heads_do = split_heads(d_att.astype(jnp.bfloat16).reshape(seq_shape))
    dterm = jnp.einsum("sqhd,sqhd->shq", heads_do.astype(jnp.float32), attended)

    def grad_step(key_piece, value_piece, key_start):
        return grad_keys(
            heads_q,
            heads_do,
            log_total,
            dterm,
            key_piece,
            value_piece,
            key_start,
            query_pos,
            lengths,
        )

    dq_zero = jnp.zeros((seq_count, local_rows, HEADS, HEAD_DIM), jnp.float32)
    own_zero = jnp.zeros(seq_shape, jnp.float32)

    def pass_step(step_index, running):
        key_cur, value_cur, dk_run, dv_run, dq_sum = running
        owner = (ctx_place - step_index) % ctx_parts
        dq_part, dk_part, dv_part = lax.cond(
            owner <= ctx_place,
            lambda: grad_step(key_cur, value_cur, owner * local_rows),
            lambda: (dq_zero, own_zero, own_zero),
        )
        dk_run, dv_run = (
            passed_along((dk_run + dk_part).astype(jnp.bfloat16), "ctx", 1).astype(jnp.float32),
            passed_along((dv_run + dv_part).astype(jnp.bfloat16), "ctx", 1).astype(jnp.float32),
        )
        key_cur, value_cur = passed_along_2((key_cur, value_cur), "ctx", 1)
        return (key_cur, value_cur, dk_run, dv_run, dq_sum + dq_part)

    key_end, value_end, dk_own, dv_own, dq_sum = lax.fori_loop(
        0, ctx_parts, pass_step, (key_low, value_low, own_zero, own_zero, dq_zero)
    )
    dq_low = dq_sum.reshape(token_rows, model_width).astype(jnp.bfloat16)
    dk_low = dk_own.reshape(token_rows, model_width).astype(jnp.bfloat16)
    dv_low = dv_own.reshape(token_rows, model_width).astype(jnp.bfloat16)
    dqkv_low = jnp.concatenate([dq_low, dk_low, dv_low], axis=1)
    bias_q_grad = jnp.sum(dq_low.astype(jnp.float32), axis=0)
    bias_v_grad = jnp.sum(dv_low.astype(jnp.float32), axis=0)
    qkv_grad = jnp.einsum("rd,re->de", normed_low, dqkv_low, preferred_element_type=jnp.float32)
    d_normed = jnp.einsum("re,de->rd", dqkv_low, full_qkv, preferred_element_type=jnp.float32)
    d_in_norm, gain_zero, shift_zero = pull_in(d_normed)
    hidden_grad = (d_residual + d_in_norm).reshape(hidden.shape)
    gain_grad = jnp.stack([gain_zero, gain_one, gain_two], axis=1)
    shift_grad = jnp.stack([shift_zero, shift_one, shift_two], axis=1)
    bias_grad = jnp.stack([bias_q_grad, bias_v_grad, bias_out_grad, bias_down_grad], axis=1)
    shares = (
        lax.psum_scatter(
            qkv_grad.astype(jnp.bfloat16), "dp", scatter_dimension=0, tiled=True
        ).astype(jnp.float32),
        lax.psum_scatter(
            out_grad.astype(jnp.bfloat16), "dp", scatter_dimension=0, tiled=True
        ).astype(jnp.float32),
        lax.psum_scatter(
            up_grad.astype(jnp.bfloat16), "dp", scatter_dimension=0, tiled=True
        ).astype(jnp.float32),
        lax.psum_scatter(
            down_grad.astype(jnp.bfloat16), "dp", scatter_dimension=0, tiled=True
        ).astype(jnp.float32),
        lax.psum_scatter(
            gain_grad.astype(jnp.bfloat16), "dp", scatter_dimension=0, tiled=True
        ).astype(jnp.float32),
        lax.psum_scatter(
            shift_grad.astype(jnp.bfloat16), "dp", scatter_dimension=0, tiled=True
        ).astype(jnp.float32),
        lax.psum_scatter(
            bias_grad.astype(jnp.bfloat16), "dp", scatter_dimension=0, tiled=True
        ).astype(jnp.float32),
        lax.psum_scatter(
            mid_gain_grad.astype(jnp.bfloat16), "dp", scatter_dimension=0, tiled=True
        ).astype(jnp.float32),
        lax.psum_scatter(
            mid_shift_grad.astype(jnp.bfloat16), "dp", scatter_dimension=0, tiled=True
        ).astype(jnp.float32),
        lax.psum_scatter(
            up_bias_grad.astype(jnp.bfloat16), "dp", scatter_dimension=0, tiled=True
        ).astype(jnp.float32),
    )
    summed = (
        lax.psum(shares[0].astype(jnp.bfloat16), "ctx").astype(jnp.float32),
        lax.psum(shares[1].astype(jnp.bfloat16), "ctx").astype(jnp.float32),
        lax.psum(shares[2].astype(jnp.bfloat16), "ctx").astype(jnp.float32),
        lax.psum(shares[3].astype(jnp.bfloat16), "ctx").astype(jnp.float32),
        lax.psum(shares[4].astype(jnp.bfloat16), "ctx").astype(jnp.float32),
        lax.psum(shares[5].astype(jnp.bfloat16), "ctx").astype(jnp.float32),
        lax.psum(shares[6].astype(jnp.bfloat16), "ctx").astype(jnp.float32),
        lax.psum(shares[7].astype(jnp.bfloat16), "ctx").astype(jnp.float32),
        lax.psum(shares[8].astype(jnp.bfloat16), "ctx").astype(jnp.float32),
        lax.psum(shares[9].astype(jnp.bfloat16), "ctx").astype(jnp.float32),
    )
    return (
        layer_output,
        loss,
        hidden_grad,
        summed[0],
        summed[1],
        summed[2],
        summed[3],
        summed[4],
        summed[5],
        summed[6],
        summed[7],
        summed[8],
        summed[9],
    )


def solution(mesh):
    placed = (
        P("dp", "ctx", None),
        P("dp", "ctx", None),
        P("dp"),
        P("dp", None),
        P("dp", None),
        P("dp", None),
        P("dp", None),
        P("dp", None),
        P("dp", None),
        P("dp", None),
        P("dp"),
        P("dp"),
        P("dp"),
    )
    return jax.shard_map(
        shards,
        mesh=mesh,
        in_specs=placed,
        out_specs=(
            P("dp", "ctx", None),
            P(),
            P("dp", "ctx", None),
            P("dp", None),
            P("dp", None),
            P("dp", None),
            P("dp", None),
            P("dp", None),
            P("dp", None),
            P("dp", None),
            P("dp"),
            P("dp"),
            P("dp"),
        ),
        check_vma=False,
    )
```

profile of v0, /device:TPU:9, one launch (start us, length us, event | category | flops | bytes accessed | tf_op | source)
XLA Modules:
  0.0 1041.0 jit_solution(1009641000833723574)
XLA Ops:
  8.0 14.5 %all-gather.3 = bf16[8,96,3]{1,2,0:T(4,128)(2,1)S(1)} all-gather(bf16[1,96,3]{1,2,0:T(4,128)(2,1)} %bitcast.185), channel_id=1, replica_groups=mesh['dp'=8,'ctx'=4] {'dp'}, dimensions={0}, use_global_device_ids=true | all-gather | bytes 5184 | tf_op jit(solution)/shard_map/all_gather | solution.py:144
  22.6 13.9 %all-gather.2 = bf16[8,96,3]{1,2,0:T(4,128)(2,1)S(1)} all-gather(bf16[1,96,3]{1,2,0:T(4,128)(2,1)} %bitcast.186), channel_id=1, replica_groups=mesh['dp'=8,'ctx'=4] {'dp'}, dimensions={0}, use_global_device_ids=true | all-gather | bytes 5184 | tf_op jit(solution)/shard_map/all_gather | solution.py:143
  39.1 36.0 %all-gather.15.cloned.1.call-done = bf16[768,2304]{1,0:T(8,128)(2,1)} async-done(((bf16[96,2304]{1,0:T(8,128)(2,1)}), bf16[768,2304]{1,0:T(8,128)(2,1)}) %all-gather.15.cloned.1.call-update) | async-done | bytes 3538960 | tf_op jit(solution)/shard_map/all_gather | solution.py:139
  75.1 3.3 fusion.73
  79.4 13.8 %all-gather.4 = bf16[8,96,4]{1,2,0:T(4,128)(2,1)S(1)} all-gather(bf16[1,96,4]{1,2,0:T(4,128)(2,1)S(1)} %bitcast.187), channel_id=1, replica_groups=mesh['dp'=8,'ctx'=4] {'dp'}, dimensions={0}, use_global_device_ids=true | all-gather | bytes 6912 | tf_op jit(solution)/shard_map/all_gather | solution.py:145
  96.7 22.1 %all-gather.5 = bf16[8,1,384]{2,1,0:T(2,128)(2,1)S(1)} all-gather(bf16[1,1,384]{2,1,0:T(2,128)(2,1)S(1)} %reshape.470), channel_id=1, replica_groups=mesh['dp'=8,'ctx'=4] {'dp'}, dimensions={0}, use_global_device_ids=true | all-gather | bytes 6912 | tf_op jit(solution)/shard_map/all_gather | solution.py:148
  118.8 21.2 %all-gather.7 = bf16[8,1,384]{2,1,0:T(2,128)(2,1)S(1)} all-gather(bf16[1,1,384]{2,1,0:T(2,128)(2,1)S(1)} %reshape.474), channel_id=1, replica_groups=mesh['dp'=8,'ctx'=4] {'dp'}, dimensions={0}, use_global_device_ids=true | all-gather | bytes 6912 | tf_op jit(solution)/shard_map/all_gather | solution.py:147
  140.1 22.1 %all-gather.6 = bf16[8,1,384]{2,1,0:T(2,128)(2,1)S(1)} all-gather(bf16[1,1,384]{2,1,0:T(2,128)(2,1)S(1)} %reshape.472), channel_id=1, replica_groups=mesh['dp'=8,'ctx'=4] {'dp'}, dimensions={0}, use_global_device_ids=true | all-gather | bytes 6912 | tf_op jit(solution)/shard_map/all_gather | solution.py:146
  165.1 21.0 %conditional.2 = (f32[1,12,256]{2,1,0:T(8,128)}, f32[1,12,256]{2,1,0:T(8,128)}, f32[1,256,12,64]{1,3,2,0:T(8,128)S(1)}, f32[1,12,256]{2,1,0:T(8,128)}) conditional(s32[]{:T(128)} %convert_element_type.247, () %tuple.48, (s32[256]{0:T(256)S(1)}, s32[1]{0:T(128)}, bf16[1,256,12,64]{1,3,2,0:T(8,128)(2,1)}, bf16[1,1024,768]{2,1,0:T(8,128)(2,1)}, ...), branch_computations={%region_2.0_spmd, %region_3.6_spmd} | conditional | flops 840431616 | bytes 106151000 | solution.py:185
  167.9 3.3 fusion.2
  171.8 4.1 fusion.4
  177.9 6.8 fusion.8
  190.6 52.3 %all-gather.19.cloned.1.call-done = bf16[768,3072]{1,0:T(8,128)(2,1)} async-done(((bf16[96,3072]{1,0:T(8,128)(2,1)}), bf16[768,3072]{1,0:T(8,128)(2,1)}) %all-gather.19.cloned.1.call-update) | async-done | bytes 4718608 | tf_op jit(solution)/shard_map/all_gather | solution.py:141
  242.9 12.0 %fusion.85 = (f32[256]{0:T(256)S(1)}, f32[256,3072]{1,0:T(8,128)S(1)}, f32[256,3072]{1,0:T(8,128)}, f32[256,3072]{1,0:T(8,128)}) fusion(f32[3072]{0:T(1024)S(1)} %bitcast.184, bf16[768,3072]{1,0:T(8,128)(2,1)} %all-gather.19.cloned.1.call-done, f32[256,768]{1,0:T(8,128)} %copy-done.6, f32[768]{0:T(1024)S(1)} %get-tuple-element.521, ...), kind=kOutput, calls=%fused_computation.178 | convolution fusion | flops 1260846848 | bytes 14963712 | tf_op jit(solution)/shard_map/dot_general | solution.py:202
  255.4 67.6 %all-gather.21.cloned.1.call-done = bf16[3072,768]{1,0:T(8,128)(2,1)} async-done(((bf16[384,768]{1,0:T(8,128)(2,1)}), bf16[3072,768]{1,0:T(8,128)(2,1)}) %all-gather.21.cloned.1.call-update) | async-done | bytes 4718608 | tf_op jit(solution)/shard_map/all_gather | solution.py:142
  323.0 5.8 convert_reduce_fusion.2
  328.8 2.3 fusion.76
  334.0 3.2 fusion.78
  343.5 2.8 multiply_reduce_fusion.4
  351.1 149.8 %while.24 = (s32[]{:T(128)}, bf16[1,256,768]{1,2,0:T(8,128)(2,1)}, bf16[1,256,768]{1,2,0:T(8,128)(2,1)}, f32[1,256,768]{1,2,0:T(8,128)}, f32[1,256,768]{1,2,0:T(...) while((s32[]{:T(128)}, bf16[1,256,768]{1,2,0:T(8,128)(2,1)}, ...), condition=%wide.region_25.26_spmd.clone, body=%wide.region_22.25_spmd.clone.sunk | while | flops 513672192 | bytes 48655496 | solution.py:266
  354.7 14.6 %conditional.5 = (f32[1,256,12,64]{1,3,2,0:T(8,128)}, f32[1,256,768]{1,2,0:T(8,128)}, f32[1,256,768]{1,2,0:T(8,128)}) conditional(s32[]{:T(128)} %convert_element_type.407, () %tuple.115, (s32[]{:T(128)}, s32[]{:T(128)}, s32[1]{0:T(128)}, bf16[1,256,12,64]{1,3,2,0:T(8,128)(2,1)}, bf16[1,256,768]{1,2,0:T(8,128)(2,1)S(1)}, ...), branch_computations={%region_23.23_spmd, %region_24.24_spmd} | conditional | flops 511706112 | bytes 32138860 | solution.py:254
  354.7 3.3 fusion.28
  359.3 3.5 multiply_convert_fusion
  364.3 2.3 convolution_multiply_fusion
  366.6 2.7 fusion.18
  371.2 2.8 collective-permute-start.2
  376.1 2.6 collective-permute-start
  387.4 4.3 collective-permute-done.1
  395.0 14.6 %conditional.5 = (f32[1,256,12,64]{1,3,2,0:T(8,128)}, f32[1,256,768]{1,2,0:T(8,128)}, f32[1,256,768]{1,2,0:T(8,128)}) conditional(s32[]{:T(128)} %convert_element_type.407, () %tuple.115, (s32[]{:T(128)}, s32[]{:T(128)}, s32[1]{0:T(128)}, bf16[1,256,12,64]{1,3,2,0:T(8,128)(2,1)}, bf16[1,256,768]{1,2,0:T(8,128)(2,1)S(1)}, ...), branch_computations={%region_23.23_spmd, %region_24.24_spmd} | conditional | flops 511706112 | bytes 32138860 | solution.py:254
  395.0 3.3 fusion.28
  399.7 3.5 multiply_convert_fusion
  404.7 2.3 convolution_multiply_fusion
  407.0 2.7 fusion.18
  409.6 2.2 fusion.110
  411.9 2.6 collective-permute-start.2
  414.4 2.2 fusion.111
  420.5 2.4 select_add_fusion.4
  427.8 4.3 collective-permute-done.1
  435.4 2.8 conditional.5
  438.3 2.2 fusion.110
  440.5 14.2 %collective-permute-start.2 = (bf16[1,256,768]{1,2,0:T(8,128)(2,1)}, bf16[1,256,768]{1,2,0:T(8,128)(2,1)}, u32[]{:S(2)}, u32[]{:S(2)}) collective-permute-start(bf16[1,256,768]{1,2,0:T(8,128)(2,1)} %fusion.110), channel_id=1, source_target_pairs={{0,1},{1,2},{2,3},{3,0},{4,5},{5,6},{6,7},{7,4},{8,9},{9,10},{10,1... | collective-permute-start | bytes 1179656 | tf_op jit(solution)/shard_map/while/body/eval_jaxpr/ppermute | solution.py:19
  454.7 2.2 fusion.111
  460.8 2.4 select_add_fusion.4
  468.1 4.3 collective-permute-done.1
  475.7 2.8 conditional.5
  478.5 2.2 fusion.110
  480.7 2.5 collective-permute-start.2
  483.2 2.2 fusion.111
  489.3 2.4 select_add_fusion.4
  496.6 4.3 collective-permute-done.1
  506.3 3.1 convolution_convert_fusion.2
  509.5 5.4 convolution_convert_fusion.1
  515.5 5.1 convolution_convert_fusion
  521.9 3.9 fusion.77
  543.8 44.7 %reduce-scatter.14.cloned.1.call-done = bf16[96,2304]{1,0:T(8,128)(2,1)} async-done(((bf16[768,2304]{1,0:T(8,128)(2,1)}), bf16[96,2304]{1,0:T(8,128)(2,1)}) %reduce-scatter.14.cloned.1.call-update) | async-done | bytes 442384 | tf_op jit(solution)/shard_map/reduce_scatter | solution.py:283
  588.5 98.9 %reduce-scatter.18.cloned.1.call-done = bf16[96,3072]{1,0:T(8,128)(2,1)} async-done(((bf16[768,3072]{1,0:T(8,128)(2,1)}), bf16[96,3072]{1,0:T(8,128)(2,1)}) %reduce-scatter.18.cloned.1.call-update) | async-done | bytes 589840 | tf_op jit(solution)/shard_map/reduce_scatter | solution.py:289
  687.4 98.5 %reduce-scatter.20.cloned.1.call-done = bf16[384,768]{1,0:T(8,128)(2,1)} async-done(((bf16[3072,768]{1,0:T(8,128)(2,1)}), bf16[384,768]{1,0:T(8,128)(2,1)}) %reduce-scatter.20.cloned.1.call-update) | async-done | bytes 589840 | tf_op jit(solution)/shard_map/reduce_scatter | solution.py:292
  788.5 2.6 add_bitcast_fusion
  792.3 39.0 %all-reduce.3 = (f32[]{:T(128)}, f32[]{:T(128)}) all-reduce(f32[]{:T(128)S(6)} %mul.346, f32[]{:T(128)} %fusion.71), channel_id=1, replica_groups=mesh['dp'=8,'ctx'=4] {'dp','ctx'}, use_global_device_ids=true, to_apply=%region_13.14 | all-reduce | flops 2 | bytes 16 | tf_op jit(solution)/shard_map/psum | solution.py:212
  831.3 27.0 %all-reduce.4 = (bf16[3072]{0:T(1024)(128)(2,1)S(1)}, bf16[3072]{0:T(1024)(128)(2,1)S(1)}, bf16[3072]{0:T(1024)(128)(2,1)S(1)}) all-reduce(bf16[3072]{0:T(1024)(128)(2,1)} %get-tuple-element.504, bf16[3072]{0:T(1024)(128)(2,1)} %get-tuple-element.506, bf16[3072]{0:T(1024)(128)(2,1)S(1)} %copy-done.41), channel_id=11, replica_groups=mesh['dp'=8,'ctx'=4] {'dp'}, use_global_device_ids=true, to_apply=%region_53.54.clone | all-reduce | flops 9216 | bytes 36864
  862.3 50.1 %reduce-scatter.24.cloned.1.call-done = bf16[96,3]{1,0:T(8,128)(2,1)} async-done(((bf16[768,3]{1,0:T(8,128)(2,1)}), bf16[96,3]{1,0:T(8,128)(2,1)}) %reduce-scatter.24.cloned.1.call-update) | async-done | bytes 592
  913.2 62.5 %reduce-scatter.26.cloned.1.call-done = bf16[96,4]{1,0:T(8,128)(2,1)} async-done(((bf16[768,4]{1,0:T(8,128)(2,1)}), bf16[96,4]{1,0:T(8,128)(2,1)}) %reduce-scatter.26.cloned.1.call-update) | async-done | bytes 784
  976.5 7.9 all-reduce.5
  987.9 38.0 %all-reduce.9.cloned.1.call-done = (bf16[96,2304]{1,0:T(8,128)(2,1)}, bf16[96,768]{1,0:T(8,128)(2,1)}, bf16[96,3072]{1,0:T(8,128)(2,1)}, bf16[384,768]{1,0:T(8,128)(2,1)}) async-done(((bf16[96,2304]{1,0:T(8,128)(2,1)}, bf16[96,768]{1,0:T(8,128)(2,1)}, bf16[96,3072]{1,0:T(8,128)(2,1)}, bf16[384,768]{1,0:T(8,128)(2,1)}), (bf16[96,2304]{1,0:T(8,128)(2,1)}, bf16[96,768]{1,0:T(8,128)(2,1)}, ...) | async-done | bytes 1769488 | tf_op jit(solution)/shard_map/psum | solution.py:315
  (353 shorter events, 141.3 us)
Async XLA Ops:
  7.2 67.9 %all-gather.15.cloned.1.call-start = ((), (), s32[]{:S(2)}) async-start(), calls=%async_computation.7 | async-start | bytes 3981312 | tf_op jit(solution)/shard_map/all_gather | solution.py:139
  7.9 157.1 %all-gather.23.cloned.1.call-start = ((), (), s32[]{:S(2)}) async-start(), calls=%async_computation.15 | async-start | bytes 1966080 | tf_op jit(solution)/shard_map/all_gather | solution.py:181
  36.6 41.8 %copy-start.36 = (f32[768]{0:T(1024)}, f32[768]{0:T(1024)S(1)}, u32[]{:S(2)}) copy-start(f32[768]{0:T(1024)S(1)} %get-tuple-element.604) | copy-start | bytes 9220
  36.6 41.8 %copy-start.64 = (f32[768]{0:T(1024)}, f32[768]{0:T(1024)S(1)}, u32[]{:S(2)}) copy-start(f32[768]{0:T(1024)S(1)} %get-tuple-element.523) | copy-start | bytes 9220
  36.7 150.8 %copy-start.33 = (f32[768]{0:T(1024)}, f32[768]{0:T(1024)S(1)}, u32[]{:S(2)}) copy-start(f32[768]{0:T(1024)S(1)} %get-tuple-element.605) | copy-start | bytes 9220
  36.7 150.8 %copy-start.48 = (f32[768]{0:T(1024)}, f32[768]{0:T(1024)S(1)}, u32[]{:S(2)}) copy-start(f32[768]{0:T(1024)S(1)} %get-tuple-element.522) | copy-start | bytes 9220
  36.7 206.2 %copy-start.32 = (f32[768]{0:T(1024)}, f32[768]{0:T(1024)S(1)}, u32[]{:S(2)}) copy-start(f32[768]{0:T(1024)S(1)} %get-tuple-element.521) | copy-start | bytes 9220
  37.8 40.6 %copy-start.42 = (f32[256]{0:T(256)}, f32[256]{0:T(256)S(1)}, u32[]{:S(2)}) copy-start(f32[256]{0:T(256)S(1)} %broadcast_multiply_fusion.3) | copy-start | bytes 3076
  39.1 39.4 %copy-start.60 = (f32[256]{0:T(256)}, f32[256]{0:T(256)S(1)}, u32[]{:S(2)}) copy-start(f32[256]{0:T(256)S(1)} %fusion.53) | copy-start | bytes 3076
  39.1 39.4 %copy-start.53 = (f32[256]{0:T(256)}, f32[256]{0:T(256)S(1)}, u32[]{:S(2)}) copy-start(f32[256]{0:T(256)S(1)} %fusion.62) | copy-start | bytes 3076
  78.5 18.2 %copy-start.70 = (bf16[384]{0:T(512)(128)(2,1)S(1)}, bf16[384]{0:T(512)(128)(2,1)}, u32[]{:S(2)}) copy-start(bf16[384]{0:T(512)(128)(2,1)} %param.31) | copy-start | bytes 2308
  78.5 40.3 %copy-start.71 = (bf16[384]{0:T(512)(128)(2,1)S(1)}, bf16[384]{0:T(512)(128)(2,1)}, u32[]{:S(2)}) copy-start(bf16[384]{0:T(512)(128)(2,1)} %param.30) | copy-start | bytes 2308
  78.5 61.6 %copy-start.72 = (bf16[384]{0:T(512)(128)(2,1)S(1)}, bf16[384]{0:T(512)(128)(2,1)}, u32[]{:S(2)}) copy-start(bf16[384]{0:T(512)(128)(2,1)} %param.29) | copy-start | bytes 2308
  79.3 85.7 %all-gather.25.cloned.1.call-start = ((), (), s32[]{:S(2)}) async-start(), calls=%async_computation.16 | async-start | bytes 1966080 | tf_op jit(solution)/shard_map/all_gather | solution.py:182
  94.2 69.9 %copy-start.17 = (bf16[256,768]{1,0:T(8,128)(2,1)S(1)}, bf16[256,768]{1,0:T(8,128)(2,1)}, u32[]{:S(2)}) copy-start(bf16[256,768]{1,0:T(8,128)(2,1)} %get-tuple-element.592) | copy-start | bytes 1179652
  94.2 93.2 %all-gather.17.cloned.1.call-start = ((), (), s32[]{:S(2)}) async-start(), calls=%async_computation.8 | async-start | bytes 1327104 | tf_op jit(solution)/shard_map/all_gather | solution.py:140
  94.8 148.1 %all-gather.19.cloned.1.call-start = ((), (), s32[]{:S(2)}) async-start(), calls=%async_computation.9 | async-start | bytes 5308416 | tf_op jit(solution)/shard_map/all_gather | solution.py:141
  95.4 227.6 %all-gather.21.cloned.1.call-start = ((), (), s32[]{:S(2)}) async-start(), calls=%async_computation.10 | async-start | bytes 5308416 | tf_op jit(solution)/shard_map/all_gather | solution.py:142
  96.0 447.8 %reduce-scatter.16.cloned.1.call-start = ((), (), s32[]{:S(2)}) async-start(), calls=%async_computation.12 | async-start | bytes 1327104 | tf_op jit(solution)/shard_map/reduce_scatter | solution.py:286
  140.1 182.9 %copy-start.29 = (f32[8,1,384]{2,1,0:T(1,128)}, f32[8,1,384]{2,1,0:T(1,128)S(1)}, u32[]{:S(2)}) copy-start(f32[8,1,384]{2,1,0:T(1,128)S(1)} %convert_element_type.300) | copy-start | bytes 36868
  162.2 160.8 %copy-start.66 = (f32[256]{0:T(256)}, f32[256]{0:T(256)S(1)}, u32[]{:S(2)}) copy-start(f32[256]{0:T(256)S(1)} %compare_convert_fusion) | copy-start | bytes 3076
  187.2 55.7 %copy-start.10 = (f32[256,768]{1,0:T(8,128)}, f32[256,768]{1,0:T(8,128)S(1)}, u32[]{:S(2)}) copy-start(f32[256,768]{1,0:T(8,128)S(1)} %copy.62) | copy-start | bytes 2359300
  187.3 67.7 %copy-start.45 = (f32[256]{0:T(256)}, f32[256]{0:T(256)S(1)}, u32[]{:S(2)}) copy-start(f32[256]{0:T(256)S(1)} %broadcast_multiply_fusion.2) | copy-start | bytes 3076
  189.5 151.1 %copy-start.40 = (f32[256]{0:T(256)}, f32[256]{0:T(256)S(1)}, u32[]{:S(2)}) copy-start(f32[256]{0:T(256)S(1)} %broadcast_multiply_fusion.1) | copy-start | bytes 3076
  190.6 150.0 %copy-start.51 = (f32[256]{0:T(256)}, f32[256]{0:T(256)S(1)}, u32[]{:S(2)}) copy-start(f32[256]{0:T(256)S(1)} %fusion.64) | copy-start | bytes 3076
  254.9 78.0 %copy-start.30 = (f32[256]{0:T(256)}, f32[256]{0:T(256)S(1)}, u32[]{:S(2)}) copy-start(f32[256]{0:T(256)S(1)} %broadcast_multiply_fusion) | copy-start | bytes 3076
  255.4 77.5 %copy-start.39 = (f32[256]{0:T(256)}, f32[256]{0:T(256)S(1)}, u32[]{:S(2)}) copy-start(f32[256]{0:T(256)S(1)} %fusion.65) | copy-start | bytes 3076
  323.0 5.8 copy-start.16
  328.8 12.1 %copy-start.4 = (f32[256,768]{1,0:T(8,128)}, f32[256,768]{1,0:T(8,128)S(1)}, u32[]{:S(2)}) copy-start(f32[256,768]{1,0:T(8,128)S(1)} %get-tuple-element.576) | copy-start | bytes 2359300
  331.1 7.2 slice-start
  349.7 238.8 %reduce-scatter.14.cloned.1.call-start = ((), (), s32[]{:S(2)}) async-start(), calls=%async_computation.11 | async-start | bytes 3981312 | tf_op jit(solution)/shard_map/reduce_scatter | solution.py:283
  371.2 11.4 %collective-permute-start.2 = (bf16[1,256,768]{1,2,0:T(8,128)(2,1)}, bf16[1,256,768]{1,2,0:T(8,128)(2,1)}, u32[]{:S(2)}, u32[]{:S(2)}) collective-permute-start(bf16[1,256,768]{1,2,0:T(8,128)(2,1)} %fusion.110), channel_id=1, source_target_pairs={{0,1},{1,2},{2,3},{3,0},{4,5},{5,6},{6,7},{7,4},{8,9},{9,10},{10,1... | collective-permute-start | bytes 1179656 | tf_op jit(solution)/shard_map/while/body/eval_jaxpr/ppermute | solution.py:19
  376.1 8.6 collective-permute-start.3
  376.1 11.4 %collective-permute-start = (bf16[1,256,768]{1,2,0:T(8,128)(2,1)S(1)}, bf16[1,256,768]{1,2,0:T(8,128)(2,1)}, u32[]{:S(2)}, u32[]{:S(2)}) collective-permute-start(bf16[1,256,768]{1,2,0:T(8,128)(2,1)S(1)} %copy.106), channel_id=1, source_target_pairs={{0,1},{1,2},{2,3},{4,5},{5,6},{6,7},{8,9},{9,10},{10,11},{12,13},{... | collective-permute-start | bytes 1179656 | tf_op jit(solution)/shard_map/while/body/eval_jaxpr/ppermute | solution.py:25
  378.6 13.1 %collective-permute-start.1 = (bf16[1,256,768]{1,2,0:T(8,128)(2,1)}, bf16[1,256,768]{1,2,0:T(8,128)(2,1)}, u32[]{:S(2)}, u32[]{:S(2)}) collective-permute-start(bf16[1,256,768]{1,2,0:T(8,128)(2,1)} %copy.107), channel_id=1, source_target_pairs={{0,1},{1,2},{2,3},{4,5},{5,6},{6,7},{8,9},{9,10},{10,11},{12,13},{... | collective-permute-start | bytes 1179656 | tf_op jit(solution)/shard_map/while/body/eval_jaxpr/ppermute | solution.py:25
  411.9 11.0 %collective-permute-start.2 = (bf16[1,256,768]{1,2,0:T(8,128)(2,1)}, bf16[1,256,768]{1,2,0:T(8,128)(2,1)}, u32[]{:S(2)}, u32[]{:S(2)}) collective-permute-start(bf16[1,256,768]{1,2,0:T(8,128)(2,1)} %fusion.110), channel_id=1, source_target_pairs={{0,1},{1,2},{2,3},{3,0},{4,5},{5,6},{6,7},{7,4},{8,9},{9,10},{10,1... | collective-permute-start | bytes 1179656 | tf_op jit(solution)/shard_map/while/body/eval_jaxpr/ppermute | solution.py:19
  416.7 8.2 collective-permute-start.3
  416.7 11.1 %collective-permute-start = (bf16[1,256,768]{1,2,0:T(8,128)(2,1)S(1)}, bf16[1,256,768]{1,2,0:T(8,128)(2,1)}, u32[]{:S(2)}, u32[]{:S(2)}) collective-permute-start(bf16[1,256,768]{1,2,0:T(8,128)(2,1)S(1)} %copy.106), channel_id=1, source_target_pairs={{0,1},{1,2},{2,3},{4,5},{5,6},{6,7},{8,9},{9,10},{10,11},{12,13},{... | collective-permute-start | bytes 1179656 | tf_op jit(solution)/shard_map/while/body/eval_jaxpr/ppermute | solution.py:25
  418.6 13.5 %collective-permute-start.1 = (bf16[1,256,768]{1,2,0:T(8,128)(2,1)}, bf16[1,256,768]{1,2,0:T(8,128)(2,1)}, u32[]{:S(2)}, u32[]{:S(2)}) collective-permute-start(bf16[1,256,768]{1,2,0:T(8,128)(2,1)} %copy.107), channel_id=1, source_target_pairs={{0,1},{1,2},{2,3},{4,5},{5,6},{6,7},{8,9},{9,10},{10,11},{12,13},{... | collective-permute-start | bytes 1179656 | tf_op jit(solution)/shard_map/while/body/eval_jaxpr/ppermute | solution.py:25
  440.5 22.7 %collective-permute-start.2 = (bf16[1,256,768]{1,2,0:T(8,128)(2,1)}, bf16[1,256,768]{1,2,0:T(8,128)(2,1)}, u32[]{:S(2)}, u32[]{:S(2)}) collective-permute-start(bf16[1,256,768]{1,2,0:T(8,128)(2,1)} %fusion.110), channel_id=1, source_target_pairs={{0,1},{1,2},{2,3},{3,0},{4,5},{5,6},{6,7},{7,4},{8,9},{9,10},{10,1... | collective-permute-start | bytes 1179656 | tf_op jit(solution)/shard_map/while/body/eval_jaxpr/ppermute | solution.py:19
  456.9 8.2 collective-permute-start.3
  456.9 11.1 %collective-permute-start = (bf16[1,256,768]{1,2,0:T(8,128)(2,1)S(1)}, bf16[1,256,768]{1,2,0:T(8,128)(2,1)}, u32[]{:S(2)}, u32[]{:S(2)}) collective-permute-start(bf16[1,256,768]{1,2,0:T(8,128)(2,1)S(1)} %copy.106), channel_id=1, source_target_pairs={{0,1},{1,2},{2,3},{4,5},{5,6},{6,7},{8,9},{9,10},{10,11},{12,13},{... | collective-permute-start | bytes 1179656 | tf_op jit(solution)/shard_map/while/body/eval_jaxpr/ppermute | solution.py:25
  458.9 13.5 %collective-permute-start.1 = (bf16[1,256,768]{1,2,0:T(8,128)(2,1)}, bf16[1,256,768]{1,2,0:T(8,128)(2,1)}, u32[]{:S(2)}, u32[]{:S(2)}) collective-permute-start(bf16[1,256,768]{1,2,0:T(8,128)(2,1)} %copy.107), channel_id=1, source_target_pairs={{0,1},{1,2},{2,3},{4,5},{5,6},{6,7},{8,9},{9,10},{10,11},{12,13},{... | collective-permute-start | bytes 1179656 | tf_op jit(solution)/shard_map/while/body/eval_jaxpr/ppermute | solution.py:25
  480.7 10.9 %collective-permute-start.2 = (bf16[1,256,768]{1,2,0:T(8,128)(2,1)}, bf16[1,256,768]{1,2,0:T(8,128)(2,1)}, u32[]{:S(2)}, u32[]{:S(2)}) collective-permute-start(bf16[1,256,768]{1,2,0:T(8,128)(2,1)} %fusion.110), channel_id=1, source_target_pairs={{0,1},{1,2},{2,3},{3,0},{4,5},{5,6},{6,7},{7,4},{8,9},{9,10},{10,1... | collective-permute-start | bytes 1179656 | tf_op jit(solution)/shard_map/while/body/eval_jaxpr/ppermute | solution.py:19
  485.5 8.2 collective-permute-start.3
  485.5 11.1 %collective-permute-start = (bf16[1,256,768]{1,2,0:T(8,128)(2,1)S(1)}, bf16[1,256,768]{1,2,0:T(8,128)(2,1)}, u32[]{:S(2)}, u32[]{:S(2)}) collective-permute-start(bf16[1,256,768]{1,2,0:T(8,128)(2,1)S(1)} %copy.106), channel_id=1, source_target_pairs={{0,1},{1,2},{2,3},{4,5},{5,6},{6,7},{8,9},{9,10},{10,11},{12,13},{... | collective-permute-start | bytes 1179656 | tf_op jit(solution)/shard_map/while/body/eval_jaxpr/ppermute | solution.py:25
  487.4 13.5 %collective-permute-start.1 = (bf16[1,256,768]{1,2,0:T(8,128)(2,1)}, bf16[1,256,768]{1,2,0:T(8,128)(2,1)}, u32[]{:S(2)}, u32[]{:S(2)}) collective-permute-start(bf16[1,256,768]{1,2,0:T(8,128)(2,1)} %copy.107), channel_id=1, source_target_pairs={{0,1},{1,2},{2,3},{4,5},{5,6},{6,7},{8,9},{9,10},{10,11},{12,13},{... | collective-permute-start | bytes 1179656 | tf_op jit(solution)/shard_map/while/body/eval_jaxpr/ppermute | solution.py:25
  500.9 5.4 copy-start.15
  500.9 5.4 copy-start.37
  500.9 5.4 copy-start.43
  500.9 5.4 copy-start.54
  500.9 5.4 copy-start.65
  509.4 178.0 %reduce-scatter.18.cloned.1.call-start = ((), (), s32[]{:S(2)}) async-start(), calls=%async_computation.13 | async-start | bytes 5308416 | tf_op jit(solution)/shard_map/reduce_scatter | solution.py:289
  514.9 271.0 %reduce-scatter.20.cloned.1.call-start = ((), (), s32[]{:S(2)}) async-start(), calls=%async_computation.14 | async-start | bytes 5308416 | tf_op jit(solution)/shard_map/reduce_scatter | solution.py:292
  520.7 340.8 %reduce-scatter.22.cloned.1.call-start = ((), (), s32[]{:S(2)}) async-start(), calls=%async_computation.17 | async-start | bytes 221184
  521.9 9.6 copy-start.2
  525.8 262.7 %copy-start.5 = (f32[256,768]{1,0:T(8,128)S(1)}, f32[256,768]{1,0:T(8,128)}, u32[]{:S(2)}) copy-start(f32[256,768]{1,0:T(8,128)} %copy-done.4) | copy-start | bytes 2359300
  525.8 262.7 %copy-start.9 = (f32[256,768]{1,0:T(8,128)S(1)}, f32[256,768]{1,0:T(8,128)}, u32[]{:S(2)}) copy-start(f32[256,768]{1,0:T(8,128)} %copy-done.8) | copy-start | bytes 2359300
  532.3 299.0 %copy-start.41 = (bf16[3072]{0:T(1024)(128)(2,1)S(1)}, bf16[3072]{0:T(1024)(128)(2,1)}, u32[]{:S(2)}) copy-start(bf16[3072]{0:T(1024)(128)(2,1)} %get-tuple-element.569) | copy-start | bytes 18436
  532.3 327.6 %copy-start.21 = (f32[256,768]{1,0:T(8,128)S(1)}, f32[256,768]{1,0:T(8,128)}, u32[]{:S(2)}) copy-start(f32[256,768]{1,0:T(8,128)} %get-tuple-element.599) | copy-start | bytes 2359300
  532.3 380.1 %reduce-scatter.24.cloned.1.call-start = ((), (), s32[]{:S(2)}) async-start(), calls=%async_computation.18 | async-start | bytes 221184
  540.5 435.3 %reduce-scatter.26.cloned.1.call-start = ((), (), s32[]{:S(2)}) async-start(), calls=%async_computation.19 | async-start | bytes 221184
  543.4 482.5 %all-reduce.9.cloned.1.call-start = ((), (), s32[]{:S(2)}) async-start(), calls=%async_computation.20 | async-start | bytes 3538944 | tf_op jit(solution)/shard_map/psum | solution.py:315
  1025.9 5.9 copy-start.22
  (43 other events, 99.0 us)
Sparse Core Ops, SparseCore 0:
  10.2 64.8 all-gather.14
  79.5 20.0 all-gather.22
  101.7 19.6 all-gather.24
  123.5 39.2 all-gather.16
  164.8 78.0 all-gather.18
  244.9 78.0 all-gather.20
  349.8 62.0 reduce-scatter.15
  509.6 78.8 reduce-scatter.13
  592.2 95.1 reduce-scatter.17
  690.9 94.9 reduce-scatter.19
  789.7 58.7 reduce-scatter.21
  852.2 60.0 reduce-scatter.23
  915.6 60.0 reduce-scatter.25
  978.2 47.6 all-reduce.8
where the time goes:
time: 1050 us; the launch traced here: 1040 us
  waiting for transfers between devices  572 us (54%)
  blocking collectives  182 us (17%)
  other arithmetic  90.3 us (9%)
  matrix products  85.9 us (8%)
  local copies, waits for them, and re-layouts  51.8 us (5%)
  starting transfers between devices  39 us (4%)
  between operations  19.7 us (2%)
    unnamed x17, waiting for transfers between devices  115 us
    reduce_scatter x1, waiting for transfers between devices, shards(): lax.psum_scatter(up_grad.astype(jnp.bfloat16), 'dp', scatter_dimension=0,...  98.9 us
    reduce_scatter x1, waiting for transfers between devices, shards(): lax.psum_scatter(down_grad.astype(jnp.bfloat16), 'dp', scatter_dimension=...  98.5 us
    all_gather x1, waiting for transfers between devices, shards(): lax.all_gather(w_down, 'dp', axis=0, tiled=True)  67.6 us
    all_gather x1, waiting for transfers between devices, shards(): lax.all_gather(w_up, 'dp', axis=0, tiled=True)  52.3 us
    reduce_scatter x1, waiting for transfers between devices, shards(): lax.psum_scatter(qkv_grad.astype(jnp.bfloat16), 'dp', scatter_dimension=0...  44.7 us
    psum x1, blocking collectives, shards(): lax.psum((0.5 * jnp.sum(error_rows * error_rows), jnp.sum(valid_mask)), (...  39 us
    psum x1, waiting for transfers between devices, shards(): lax.psum(shares[0].astype(jnp.bfloat16), 'ctx').astype(jnp.float32)  38 us
  transfers between devices with their start and end apart: 30, of which 17 were waited for; matrix products, arithmetic and copies ran while one was open for 18% of the time, Pallas kernels for 0%

commit v1 on v0

--- a/solution.py
+++ b/solution.py
@@ -3,6 +3,8 @@
 import jax
 import jax.numpy as jnp
 from jax import lax
+from jax.experimental import pallas as pl
+from jax.experimental.pallas import tpu as pltpu
 from jax.sharding import PartitionSpec as P
 
 HEADS = 12
@@ -340,7 +342,501 @@
     )
 
 
+AXES = ("dp", "ctx")
+
+
+def swap(value, mask):
+    count = lax.axis_size("dp") * lax.axis_size("ctx")
+    return lax.ppermute(value, AXES, [(i, i ^ mask) for i in range(count)])
+
+
+def near_of(piece):
+    return jnp.stack([piece] + [swap(piece, 8 * step) for step in (1, 2, 3)])
+
+
+def wide(value):
+    return value.astype(jnp.float32)
+
+
+def narrow(value):
+    return value.astype(jnp.bfloat16)
+
+
+def shared_dp(keep, send):
+    kept = wide(keep) + wide(swap(send, 4))
+    sent = narrow(kept)
+    return kept[0] + sum(wide(swap(sent[step], 8 * step)) for step in (1, 2, 3))
+
+
+def by_ctx(tiles, ctx_at):
+    stack = jnp.stack(tiles)
+    return [lax.dynamic_index_in_dim(stack, ctx_at ^ j, 0, keepdims=False) for j in range(4)]
+
+
+VMEM_BYTES = 56 * 1024 * 1024
+
+
+def whole(shape):
+    return pl.BlockSpec(tuple(shape), lambda i: (0,) * len(shape), pipeline_mode=pl.Buffered(1))
+
+
+def call(body, ins, outs, scratch=(), flops=0, moved=0):
+    pairs = [v if isinstance(v, tuple) else (v, whole(v.shape)) for v in ins[1:]]
+    return pl.pallas_call(
+        body,
+        grid=(1,),
+        in_specs=[pl.BlockSpec(memory_space=pltpu.SMEM)] + [spec for _, spec in pairs],
+        out_specs=[whole(shape) for shape, _ in outs],
+        out_shape=[jax.ShapeDtypeStruct(shape, dtype) for shape, dtype in outs],
+        scratch_shapes=[pltpu.VMEM(shape, dtype) for shape, dtype in scratch],
+        compiler_params=pltpu.CompilerParams(vmem_limit_bytes=VMEM_BYTES),
+        cost_estimate=pl.CostEstimate(flops=flops, bytes_accessed=moved, transcendentals=0),
+    )(ins[0], *[v for v, _ in pairs])
+
+
+BF, F32 = jnp.bfloat16, jnp.float32
+
+
+def contract(a, b, da, db):
+    return lax.dot_general(a, b, (((da,), (db,)), ((), ())), preferred_element_type=F32)
+
+
+def block_of(sc, xr, zr):
+    return 2 * ((sc[0] >> 1) ^ zr) + ((sc[0] & 1) ^ xr)
+
+
+def slot_of(sc, block):
+    return ((block & 1) ^ (sc[0] & 1)) * 4 + ((block >> 1) ^ (sc[0] >> 1))
+
+
+def lay(sc, scr, near, far, rows, stride, offset=0):
+    for xr, ref in ((0, near), (1, far)):
+        for zr in range(4):
+            at = pl.multiple_of(stride * block_of(sc, xr, zr) + offset, 16)
+            scr[pl.ds(at, rows), :] = ref[zr]
+
+
+def moments(value):
+    average = jnp.mean(value, axis=-1, keepdims=True)
+    centred = value - average
+    scale = lax.rsqrt(jnp.mean(centred * centred, axis=-1, keepdims=True) + EPSILON)
+    return centred * scale, scale
+
+
+def norm_back(grad, hat, scale):
+    return scale * (grad - jnp.mean(grad, axis=-1, keepdims=True) - hat * jnp.mean(grad * hat, axis=-1, keepdims=True))
+
+
+def mine(ctx_at, row):
+    out = row[:, :192]
+    for j in range(1, 4):
+        out = jnp.where(ctx_at == j, row[:, 192 * j:192 * j + 192], out)
+    return out
+
+
+def pack_body(sc, w, gain, shift, bias, out, scr):
+    scr[...] = jnp.zeros((16, 128), F32)
+    scr[0:3, :96] = gain[...].astype(F32)
+    scr[3:6, :96] = shift[...].astype(F32)
+    scr[6:10, :96] = bias[...].astype(F32)
+    small = scr[...].T[:96].astype(BF)
+    for j in range(4):
+        @pl.when(sc[1] == j)
+        def _():
+            cols = [w[:, 768 * part + 192 * j:768 * part + 192 * j + 192] for part in range(3)]
+            out[...] = jnp.concatenate(cols + [small, jnp.zeros((96, 48), BF)], axis=1)
+
+
+def attend_body(sc, h0, h1, h2, h3, wa, wb, a0, a1, a2, a3, q_o, k_o, v_o, lse_o, ot_o, n_o, vec_o, w_scr):
+    ctx_at, length = sc[1], sc[2]
+    lay(sc, w_scr, wa, wb, 96, 96)
+    vec = w_scr[:, 512:640].astype(F32).T[64:80]
+    vec_o[...] = vec
+    bias_q, bias_v = mine(ctx_at, vec[6:7]), mine(ctx_at, vec[7:8])
+    for r, ref in enumerate((h0, h1, h2, h3)):
+        rows = pl.ds(pl.multiple_of((ctx_at ^ r) * 256, 256), 256)
+        hat, _ = moments(ref[...].astype(F32))
+        normed = (hat * vec[0:1] + vec[3:4]).astype(BF)
+        n_o[rows, :] = normed
+        p = jnp.dot(normed, w_scr[...], preferred_element_type=F32)
+        for h in range(3):
+            q_o[h, rows, :] = ((p[:, 64 * h:64 * h + 64] + bias_q[:, 64 * h:64 * h + 64]) * 0.125).astype(BF)
+            k_o[h, rows, :] = p[:, 192 + 64 * h:256 + 64 * h].astype(BF)
+            v_o[h, rows, :] = (p[:, 384 + 64 * h:448 + 64 * h] + bias_v[:, 64 * h:64 * h + 64]).astype(BF)
+
+    def head(h, carry):
+        for i in range(4):
+            n = 256 * (i + 1)
+            scores = contract(k_o[h, :n, :], q_o[h, 256 * i:256 * i + 256, :], 1, 1)
+            limit = jnp.minimum(256 * i + lax.broadcasted_iota(jnp.int32, (1, 256), 1), length - 1)
+            scores = jnp.where(lax.broadcasted_iota(jnp.int32, (n, 256), 0) <= limit, scores, NEGATIVE)
+            top = jnp.max(scores, axis=0, keepdims=True)
+            grown = jnp.exp(scores - top)
+            total = jnp.sum(grown, axis=0, keepdims=True)
+            out = contract(v_o[h, :n, :], grown.astype(BF), 0, 0) / total
+            ot_o[i, pl.ds(pl.multiple_of(64 * h, 64), 64), :] = out
+            lse_o[h, i:i + 1, :] = top + jnp.log(total)
+        return carry
+
+    lax.fori_loop(0, 3, head, 0)
+    for r, ref in enumerate((a0, a1, a2, a3)):
+        ref[...] = ot_o[ctx_at ^ r].T.astype(BF)
+
+
+def attend(sc, hids, wa, wb):
+    rows = (256, 192)
+    return call(
+        attend_body, [sc, *hids, wa, wb],
+        [(rows, BF)] * 4 + [((3, 1024, 64), BF)] * 3
+        + [((3, 8, 256), F32), ((4, 192, 256), F32), ((1024, 768), BF), ((16, 768), F32)],
+        [((768, 640), BF)], flops=2 * 10 ** 9, moved=8 * 10 ** 6)
+
+
+def attend_back_body(sc, d0, d1, d2, d3, q_i, k_i, v_i, lse_i, ot_i, n_i, h0, h1, h2, h3, wa, wb, vec_i, side_e, side_d, mids,
+                     n0, n1, n2, n3, keep, send, w_scr, do_scr, dq_s, dk_s, dv_s, dk_acc, dv_acc, all_scr, g_scr):
+    ctx_at, length = sc[1], sc[2]
+    lay(sc, w_scr, wa, wb, 96, 96)
+    for r, ref in enumerate((d0, d1, d2, d3)):
+        rows = pl.ds(pl.multiple_of((ctx_at ^ r) * 256, 256), 256)
+        value = ref[...]
+        for h in range(3):
+            do_scr[h, rows, :] = value[:, 64 * h:64 * h + 64]
+
+    def head(h, carry):
+        for i in (3, 2, 1, 0):
+            n = 256 * (i + 1)
+            mine_rows = slice(256 * i, 256 * i + 256)
+            q, do, k = q_i[h, mine_rows, :], do_scr[h, mine_rows, :], k_i[h, :n, :]
+            out = ot_i[i, pl.ds(pl.multiple_of(64 * h, 64), 64), :]
+            dterm = jnp.sum(do.astype(F32).T * out, axis=0, keepdims=True)
+            limit = jnp.minimum(256 * i + lax.broadcasted_iota(jnp.int32, (1, 256), 1), length - 1)
+            prob = jnp.exp(contract(k, q, 1, 1) - lse_i[h, i:i + 1, :])
+            prob = jnp.where(lax.broadcasted_iota(jnp.int32, (n, 256), 0) <= limit, prob, 0.0)
+            dscore = (prob * (contract(v_i[h, :n, :], do, 1, 1) - dterm)).astype(BF)
+            dv = jnp.dot(prob.astype(BF), do, preferred_element_type=F32)
+            dk = jnp.dot(dscore, q, preferred_element_type=F32)
+            if i == 3:
+                dv_acc[...] = dv
+                dk_acc[...] = dk
+            else:
+                dv_acc[:n, :] += dv
+                dk_acc[:n, :] += dk
+            dq_s[h, mine_rows, :] = (contract(k, dscore, 0, 0) * 0.125).T.astype(BF)
+        dk_s[h] = dk_acc[...].astype(BF)
+        dv_s[h] = dv_acc[...].astype(BF)
+        return carry
+
+    lax.fori_loop(0, 3, head, 0)
+    for i in range(4):
+        rows = slice(256 * i, 256 * i + 256)
+        all_scr[rows, :] = jnp.concatenate([s[h, rows, :] for s in (dq_s, dk_s, dv_s) for h in range(3)], axis=1)
+    sums = jnp.sum(all_scr[...].astype(F32), axis=0, keepdims=True)
+    bias_q = jnp.concatenate([jnp.where(ctx_at == j, sums[:, :192], 0.0) for j in range(4)], axis=1)
+    bias_v = jnp.concatenate([jnp.where(ctx_at == j, sums[:, 384:], 0.0) for j in range(4)], axis=1)
+    gain_sum, shift_sum = jnp.zeros((1, 768), F32), jnp.zeros((1, 768), F32)
+    for r, (ref, out) in enumerate(((h0, n0), (h1, n1), (h2, n2), (h3, n3))):
+        rows = pl.ds(pl.multiple_of((ctx_at ^ r) * 256, 256), 256)
+        grad = contract(all_scr[rows, :], w_scr[:, :576], 1, 1)
+        hat, _ = moments(ref[...].astype(F32))
+        gain_sum += jnp.sum(grad * hat, axis=0, keepdims=True)
+        shift_sum += jnp.sum(grad, axis=0, keepdims=True)
+        out[...] = grad.astype(BF)
+    rows16 = jnp.concatenate(
+        [gain_sum, side_e[0:2], shift_sum, side_e[2:4], bias_q, bias_v, side_e[4:5], side_d[0:2], jnp.zeros((5, 768), F32)], axis=0)
+    w_grad = contract(n_i[...], all_scr[...], 0, 0)
+    for b in range(8):
+        at = slot_of(sc, b)
+        extra = jnp.concatenate([mids[:, 384 * b:384 * b + 384], rows16[:, 96 * b:96 * b + 96], jnp.zeros((16, 96), F32)], axis=1)
+        g_scr[at, :96, :] = w_grad[96 * b:96 * b + 96].astype(BF)
+        g_scr[at, 96:112, :] = extra.astype(BF)
+    keep[...] = g_scr[:4]
+    send[...] = g_scr[4:]
+
+
+def attend_back(sc, douts, saved, hids, wa, wb, side_e, side_d, mids):
+    q, k, v, lse, ot, normed, vec = saved
+    return call(
+        attend_back_body, [sc, *douts, q, k, v, lse, ot, normed, *hids, wa, wb, vec, side_e, side_d, mids],
+        [((256, 768), BF)] * 4 + [((4, 112, 576), BF)] * 2,
+        [((768, 640), BF), ((3, 1024, 64), BF), ((3, 1024, 64), BF), ((3, 1024, 64), BF), ((3, 1024, 64), BF),
+         ((1024, 64), F32), ((1024, 64), F32), ((1024, 576), BF), ((8, 112, 576), BF)],
+        flops=4 * 10 ** 9, moved=12 * 10 ** 6)
+
+
+def part(rows, at):
+    return pl.BlockSpec((4, rows, 768), lambda i: (0, at, 0), pipeline_mode=pl.Buffered(1))
+
+
+def lay_out(sc, scr, own_near, own_far, other_near, other_far):
+    core = sc[1] & 1
+    lay(sc, scr, own_near, own_far, 48, 96, 48 * core)
+    lay(sc, scr, other_near, other_far, 48, 96, 48 * (1 - core))
+
+
+def lay_down(sc, scr, own_near, own_far, other_near, other_far):
+    for c, refs in ((0, (own_near, own_far)), (1, (other_near, other_far))):
+        for y in (0, 1):
+            offset = 96 * (sc[1] ^ (2 * y + c))
+            for xr in (0, 1):
+                for zr in range(4):
+                    at = pl.multiple_of(384 * block_of(sc, xr, zr) + offset, 32)
+                    scr[pl.ds(at, 96), :] = refs[xr][zr, y]
+
+
+def join_heads(sc, scr, pieces):
+    for r, ref in enumerate(pieces):
+        scr[r] = ref[...]
+    return jnp.concatenate([scr[sc[1] ^ j] for j in range(4)], axis=1).astype(F32)
+
+
+def mid_body(sc, g0, g1, g2, g3, own, vec, on, of, tn, tf, mixed_o, resid_o, ffn_o, w_scr, a_scr):
+    lay_out(sc, w_scr, on, of, tn, tf)
+    hat, _ = moments(join_heads(sc, a_scr, (g0, g1, g2, g3)))
+    mixed = (hat * vec[1:2] + vec[4:5]).astype(BF)
+    mixed_o[...] = mixed
+    resid = own[...].astype(F32) + jnp.dot(mixed, w_scr[...], preferred_element_type=F32) + vec[8:9]
+    resid_o[...] = resid
+    hat, _ = moments(resid)
+    ffn_o[...] = (hat * vec[2:3] + vec[5:6]).astype(BF)
+
+
+def up_body(sc, ffn, w0n, w0f, w1n, w1f, w2n, w2f, w3n, w3f, mn, mf, act_o, hat_o, slope_o, scale_o, nat_o,
+            w_scr, g_scr, m_scr):
+    for xr, ref in ((0, mn), (1, mf)):
+        for zr in range(4):
+            m_scr[block_of(sc, xr, zr)] = ref[zr].astype(F32)
+    flat = [m_scr[b] for b in range(8)]
+    for j in range(4):
+        two = flat[2 * j:2 * j + 2]
+        nat_o[j, 0:1, :] = jnp.concatenate([m[0:1, :384] for m in two], axis=1)
+        nat_o[j, 1:2, :] = jnp.concatenate([m[0:1, 384:] for m in two], axis=1)
+        nat_o[j, 2:3, :] = jnp.concatenate([m[1:2, :384] for m in two], axis=1)
+        nat_o[j, 3:8, :] = jnp.zeros((5, 768), F32)
+    value = ffn[...]
+    total = jnp.zeros((256, 1), F32)
+    for t, (near, far) in enumerate(((w0n, w0f), (w1n, w1f), (w2n, w2f), (w3n, w3f))):
+        j = sc[1] ^ t
+        lay(sc, w_scr.at[t % 2], near, far, 96, 96)
+        up = jnp.dot(value, w_scr[t % 2], preferred_element_type=F32) + nat_o[j, 2:3, :]
+        chance = 0.5 * (1.0 + lax.erf(up * math.sqrt(0.5)))
+        slope_o[j] = (chance + up * jnp.exp(-0.5 * up * up) * (1.0 / math.sqrt(2.0 * math.pi))).astype(BF)
+        gelu = up * chance
+        g_scr[j] = gelu
+        total += jnp.sum(gelu, axis=-1, keepdims=True)
+    average = total * (1.0 / 3072)
+    square = jnp.zeros((256, 1), F32)
+    for j in range(4):
+        centred = g_scr[j] - average
+        square += jnp.sum(centred * centred, axis=-1, keepdims=True)
+    scale = lax.rsqrt(square * (1.0 / 3072) + EPSILON)
+    scale_o[...] = scale
+    for j in range(4):
+        hat = (g_scr[j] - average) * scale
+        hat_o[j] = hat.astype(BF)
+        act_o[j] = (hat * nat_o[j, 0:1, :] + nat_o[j, 1:2, :]).astype(BF)
+
+
+def down_body(sc, act, resid, teacher, vec, on, of, tn, tf, out_o, err_o, low_o, side_o, w_scr):
+    lay_down(sc, w_scr, on, of, tn, tf)
+    result = resid[...] + vec[9:10]
+    for j in range(4):
+        result += jnp.dot(act[j], w_scr[768 * j:768 * j + 768, :], preferred_element_type=F32)
+    pos = sc[1] * 256 + lax.broadcasted_iota(jnp.int32, (256, 1), 0)
+    valid = jnp.where(pos < sc[2], 1.0, 0.0)
+    out_o[...] = (result * valid).astype(BF)
+    error = (result - teacher[...].astype(F32)) * valid
+    err_o[...] = error
+    low = error.astype(BF)
+    low_o[...] = low
+    side_o[0:1, :] = jnp.sum(low.astype(F32), axis=0, keepdims=True)
+    loss = 0.5 * jnp.sum(jnp.sum(error * error, axis=0, keepdims=True), axis=1, keepdims=True)
+    count = jnp.sum(valid, axis=0, keepdims=True)
+    high = loss.astype(BF).astype(F32)
+    lane = lax.broadcasted_iota(jnp.int32, (1, 768), 1) % 96
+    side_o[1:2, :] = jnp.where(lane == 0, high, jnp.where(lane == 1, loss - high, jnp.where(lane == 2, count, 0.0)))
+    side_o[2:8, :] = jnp.zeros((6, 768), F32)
+
+
+def down_grad_body(sc, act, low, keep, send, g_scr):
+    value = low[...]
+    for j in range(4):
+        grad = contract(act[j], value, 0, 0).astype(BF)
+        for half in (0, 1):
+            at = slot_of(sc, 2 * j + half)
+            for q in range(4):
+                g_scr[sc[1] ^ q, at] = grad[384 * half + 96 * q:384 * half + 96 * q + 96]
+    for y in (0, 1):
+        keep[y] = g_scr[2 * y]
+        send[y] = g_scr[2 * y + 1]
+
+
+def ffn_back_body(sc, low, err, resid, hat_i, slope, scale, nat, don, dof, dtn, dtf,
+                  w0n, w0f, w1n, w1f, w2n, w2f, w3n, w3f, on, of, tn, tf, vec, g0, g1, g2, g3,
+                  up_o, branch_o, dres_o, p0, p1, p2, p3, side_o, mids_o, wd_scr, w_scr, dh_scr, a_scr):
+    lay_down(sc, wd_scr, don, dof, dtn, dtf)
+    value = low[...]
+    first, second = jnp.zeros((256, 1), F32), jnp.zeros((256, 1), F32)
+    for j in range(4):
+        grad = contract(value, wd_scr[768 * j:768 * j + 768, :], 1, 1)
+        hat = hat_i[j].astype(F32)
+        cols = slice(768 * j, 768 * j + 768)
+        mids_o[0:1, cols] = jnp.sum(grad * hat, axis=0, keepdims=True)
+        mids_o[1:2, cols] = jnp.sum(grad, axis=0, keepdims=True)
+        grad = grad * nat[j, 0:1, :]
+        dh_scr[j] = grad
+        first += jnp.sum(grad, axis=-1, keepdims=True)
+        second += jnp.sum(grad * hat, axis=-1, keepdims=True)
+    first, second = first * (1.0 / 3072), second * (1.0 / 3072)
+    for j in range(4):
+        hat = hat_i[j].astype(F32)
+        grad = (scale[...] * (dh_scr[j] - first - hat * second) * slope[j].astype(F32)).astype(BF)
+        up_o[j] = grad
+        mids_o[2:3, 768 * j:768 * j + 768] = jnp.sum(grad.astype(F32), axis=0, keepdims=True)
+    mids_o[3:16, :] = jnp.zeros((13, 3072), F32)
+    grad = jnp.zeros((256, 768), F32)
+    for t, (near, far) in enumerate(((w0n, w0f), (w1n, w1f), (w2n, w2f), (w3n, w3f))):
+        lay(sc, w_scr.at[t % 2], near, far, 96, 96)
+        grad += contract(up_o[sc[1] ^ t], w_scr[t % 2], 1, 1)
+    hat, factor = moments(resid[...])
+    side_o[1:2, :] = jnp.sum(grad * hat, axis=0, keepdims=True)
+    side_o[3:4, :] = jnp.sum(grad, axis=0, keepdims=True)
+    dres = err[...] + norm_back(grad * vec[2:3], hat, factor)
+    dres_o[...] = dres
+    branch = dres.astype(BF)
+    branch_o[...] = branch
+    side_o[4:5, :] = jnp.sum(branch.astype(F32), axis=0, keepdims=True)
+    lay_out(sc, w_scr.at[0], on, of, tn, tf)
+    grad = contract(branch, w_scr[0], 1, 1)
+    hat, factor = moments(join_heads(sc, a_scr, (g0, g1, g2, g3)))
+    side_o[0:1, :] = jnp.sum(grad * hat, axis=0, keepdims=True)
+    side_o[2:3, :] = jnp.sum(grad, axis=0, keepdims=True)
+    side_o[5:8, :] = jnp.zeros((3, 768), F32)
+    grad = norm_back(grad * vec[1:2], hat, factor).astype(BF)
+    for j in range(4):
+        a_scr[j] = grad[:, 192 * j:192 * j + 192]
+    for r, ref in enumerate((p0, p1, p2, p3)):
+        ref[...] = a_scr[sc[1] ^ r]
+
+
+def up_grad_body(sc, ffn, up, mixed, branch, keep, send, out_keep, out_send, g_scr, o_scr):
+    value = ffn[...]
+    for j in range(4):
+        grad = contract(value, up[j], 0, 0).astype(BF)
+        for b in range(8):
+            g_scr[sc[1] ^ j, slot_of(sc, b)] = grad[96 * b:96 * b + 96]
+    for y in (0, 1):
+        keep[y] = g_scr[2 * y]
+        send[y] = g_scr[2 * y + 1]
+    grad = contract(mixed[...], branch[...], 0, 0).astype(BF)
+    for b in range(8):
+        for c in (0, 1):
+            o_scr[(sc[1] & 1) ^ c, slot_of(sc, b)] = grad[96 * b + 48 * c:96 * b + 48 * c + 48]
+    out_keep[...] = o_scr[0]
+    out_send[...] = o_scr[1]
+
+
+def both(value):
+    return tuple(swap(v, 1) for v in value)
+
+
+def fast(
+    hidden, teacher, lengths, w_qkv, w_out, w_up, w_down, norm_gain, norm_shift, proj_bias,
+    mid_gain, mid_shift, up_bias,
+):
+    dp_at, ctx_at = lax.axis_index("dp"), lax.axis_index("ctx")
+    core = ctx_at & 1
+    sc = jnp.stack([dp_at, ctx_at, lengths[0]]).astype(jnp.int32)
+    own = hidden[0]
+    tall = (256, 768)
+    h_y = swap(own, 2)
+    h_c = swap(own, 1)
+    piece = call(pack_body, [sc, w_qkv, norm_gain.T, norm_shift.T, proj_bias.T], [((96, 640), BF)], [((16, 128), F32)])[0]
+    q_near = near_of(piece)
+    q_far = swap(q_near, 4)
+    h_yc = swap(h_y, 1)
+    mid_rows = jnp.concatenate([mid_gain, mid_shift, up_bias, jnp.zeros((13 * 384,), BF)]).reshape(8, 768)
+    piece_a = jnp.concatenate([
+        lax.dynamic_slice(w_up, (0, 768 * ctx_at), (96, 768)),
+        lax.dynamic_slice(w_out, (48 * core, 0), (48, 768)), mid_rows])
+    a_near = near_of(piece_a)
+    a_far = swap(a_near, 4)
+    down4 = w_down.reshape(4, 96, 768)
+    piece_b = jnp.stack([lax.dynamic_index_in_dim(down4, ctx_at ^ t, 0, keepdims=False) for t in (0, 2)])
+    b_near = near_of(piece_b)
+    b_far = swap(b_near, 4)
+
+    hids = [own, h_c, h_y, h_yc]
+    *att, q, k, v, lse, ot, normed, vec = attend(sc, hids, q_near, q_far)
+    got = [att[0]] + [swap(att[r], r) for r in (1, 2, 3)]
+    a_own = (a_near, a_far)
+    a_other = both(a_own)
+    outs = [(t, part(48, 2)) for t in a_own + a_other]
+    mixed, resid, ffn = call(
+        mid_body, [sc, *got, own, vec, *outs], [(tall, BF), (tall, F32), (tall, BF)],
+        [((768, 768), BF), ((4, 256, 192), BF)], flops=3 * 10 ** 8, moved=3 * 10 ** 6)
+    y_own = tuple(swap(t[:, :96], 2) for t in a_own)
+    y_other = both(y_own)
+    ups = [(t, part(96, 0)) for t in a_own + a_other] + [*y_own, *y_other]
+    four = (4, 256, 768)
+    act, hat, slope, scale, nat = call(
+        up_body, [sc, ffn, *ups] + [(t, part(8, 18)) for t in a_own],
+        [(four, BF), (four, BF), (four, BF), ((256, 1), F32), ((4, 8, 768), F32)],
+        [((2, 768, 768), BF), (four, F32), ((8, 8, 768), F32)], flops=12 * 10 ** 8, moved=10 ** 7)
+    downs = (b_near, b_far) + both((b_near, b_far))
+    out, err, low, side_d = call(
+        down_body, [sc, act, resid, teacher[0], vec, *downs],
+        [(tall, BF), (tall, F32), (tall, BF), ((8, 768), F32)], [((3072, 768), BF)], flops=12 * 10 ** 8, moved=8 * 10 ** 6)
+    halves_of = ((2, 8, 96, 768), BF)
+    down_keep, down_send = call(
+        down_grad_body, [sc, act, low], [halves_of] * 2, [((4, 8, 96, 768), BF)], flops=12 * 10 ** 8, moved=7 * 10 ** 6)
+    *pieces, side_e, mids = call(
+        ffn_back_body, [sc, low, err, resid, hat, slope, scale, nat, *downs, *ups, *outs, vec, *got],
+        [(four, BF), (tall, BF), (tall, F32)] + [((256, 192), BF)] * 4 + [((8, 768), F32), ((16, 3072), F32)],
+        [((3072, 768), BF), ((2, 768, 768), BF), (four, F32), ((4, 256, 192), BF)], flops=27 * 10 ** 8, moved=2 * 10 ** 7)
+    up_low, branch, d_res, *d_att = pieces
+    up_keep, up_send, out_keep, out_send = call(
+        up_grad_body, [sc, ffn, up_low, mixed, branch], [halves_of] * 2 + [((8, 48, 768), BF)] * 2,
+        [((4, 8, 96, 768), BF), ((2, 8, 48, 768), BF)], flops=15 * 10 ** 8, moved=8 * 10 ** 6)
+    d_got = [d_att[0]] + [swap(d_att[r], r) for r in (1, 2, 3)]
+    *dn, q_keep, q_send = attend_back(sc, d_got, (q, k, v, lse, ot, normed, vec), hids, q_near, q_far, side_e, side_d, mids)
+    dn_0 = wide(dn[0]) + wide(swap(dn[1], 1))
+    dn_2 = wide(dn[2]) + wide(swap(dn[3], 1))
+    d_own = dn_0 + wide(swap(narrow(dn_2), 2))
+    _, pull_own = jax.vjp(lambda t: layer_norm(t, vec[0], vec[3]), wide(own))
+    hidden_grad = (d_res + pull_own(d_own)[0])[None]
+    q_share = narrow(shared_dp(q_keep, q_send))
+
+    def ctx_sum(keep, send):
+        pair = wide(keep) + wide(swap(send, 1))
+        total = pair[0] + wide(swap(narrow(pair[1]), 2))
+        return narrow(total[:4]), narrow(total[4:])
+
+    down_share = narrow(shared_dp(*ctx_sum(down_keep, down_send)))
+    up_share = narrow(shared_dp(*ctx_sum(up_keep, up_send)))
+    out_pair = wide(out_keep) + wide(swap(out_send, 1))
+    out_share = narrow(shared_dp(narrow(out_pair[:4]), narrow(out_pair[4:])))
+    out_share = narrow(wide(out_share) + wide(swap(out_share, 2)))
+
+    def ctx_all(share):
+        far = swap(share, 2)
+        return by_ctx([share, swap(share, 1), far, swap(far, 1)], ctx_at)
+
+    q_all = ctx_all(q_share)
+    grad_qkv = wide(jnp.concatenate([q_all[j][:96, 192 * p:192 * p + 192] for p in range(3) for j in range(4)], axis=1))
+    rest = sum(wide(t[96:]) for t in q_all)
+    mid_gain_out, mid_shift_out, up_bias_out = (rest[i, :384] for i in range(3))
+    vec_out = rest[:10, 384:480]
+    loss = (rest[10, 384] + rest[10, 385]) / (rest[10, 386] * hidden.shape[2])
+    grad_up = wide(jnp.concatenate(ctx_all(up_share), axis=1))
+    grad_down = wide(jnp.concatenate(ctx_all(down_share), axis=0))
+    out_far = swap(out_share, 1)
+    grad_out = wide(jnp.where(core == 0, jnp.concatenate([out_share, out_far]), jnp.concatenate([out_far, out_share])))
+    return (out[None], loss, hidden_grad, grad_qkv, grad_out, grad_up, grad_down,
+            vec_out[:3].T, vec_out[3:6].T, vec_out[6:].T, mid_gain_out, mid_shift_out, up_bias_out)
+
+
 def solution(mesh):
+    step = fast if (mesh.shape["dp"], mesh.shape["ctx"]) == (8, 4) else shards
     placed = (
         P("dp", "ctx", None),
         P("dp", "ctx", None),
@@ -357,7 +853,7 @@
         P("dp"),
     )
     return jax.shard_map(
-        shards,
+        step,
         mesh=mesh,
         in_specs=placed,
         out_specs=(

time: 1050 us -> 338 us (0.32)
  waiting for transfers between devices: 572 us -> 152 us
  blocking collectives: 182 us -> 0 us
  Pallas kernels: 0 us -> 87.4 us
  matrix products: 85.9 us -> 0 us
  other arithmetic: 90.3 us -> 10.8 us
  local copies, waits for them, and re-layouts: 51.8 us -> 10.4 us
  starting transfers between devices: 39 us -> 73.2 us
  between operations: 19.7 us -> 5.22 us
    reduce_scatter x4 -> x0, waiting for transfers between devices: 242 us -> none  [the longest x1 98.9 us: shards(): lax.psum_scatter(up_grad.astype(jnp.bfloat16), 'dp', scatter_dimension=0,...]
    all_gather x6 -> x0, waiting for transfers between devices: 156 us -> none  [the longest x1 67.6 us: shards(): lax.all_gather(w_down, 'dp', axis=0, tiled=True)]
    ppermute x16 -> x64, waiting for transfers between devices: 21.2 us -> 152 us  [swap(): return lax.ppermute(value, AXES, [(i, i ^ mask) for i in range(count)])]
    unnamed x17 -> x0, waiting for transfers between devices: 115 us -> none
    all_gather x6 -> x0, blocking collectives: 108 us -> none  [the longest x1 22.1 us: shards(): lax.all_gather(up_bias, 'dp', axis=0, tiled=True)]
    pallas_call x0 -> x9, Pallas kernels: none -> 87.4 us  [call(): pl.pallas_call(body, grid=(1,), in_specs=[pl.BlockSpec(memory_space=pltpu...]
    dot_general x24 -> x0, matrix products: 85.9 us -> none  [the longest x1 12 us: shards(): jnp.dot(ffn_low, full_up, preferred_element_type=jnp.float32) + up_bias_f]
    psum x2 -> x0, blocking collectives: 46.9 us -> none  [the longest x1 39 us: shards(): lax.psum((0.5 * jnp.sum(error_rows * error_rows), jnp.sum(valid_mask)), (...]
  transfers between devices with their start and end apart: 30 -> 64, of which waited for: 17 -> 25; matrix products, arithmetic and copies ran while one was open for 18% -> 4% of each run, Pallas kernels for 0% -> 16%
where the time goes in v1:
time: 338 us; the launch traced here: 339 us
  waiting for transfers between devices  152 us (45%)
  Pallas kernels  87.4 us (26%)
  starting transfers between devices  73.2 us (22%)
  other arithmetic  10.8 us (3%)
  local copies, waits for them, and re-layouts  10.4 us (3%)
  between operations  5.22 us (2%)
    ppermute x64, waiting for transfers between devices, swap(): return lax.ppermute(value, AXES, [(i, i ^ mask) for i in range(count)])  152 us
    pallas_call x9, Pallas kernels, call(): pl.pallas_call(body, grid=(1,), in_specs=[pl.BlockSpec(memory_space=pltpu...  87.4 us
    ppermute x64, starting transfers between devices, swap(): return lax.ppermute(value, AXES, [(i, i ^ mask) for i in range(count)])  73.2 us
  transfers between devices with their start and end apart: 64, of which 25 were waited for; matrix products, arithmetic and copies ran while one was open for 4% of the time, Pallas kernels for 16%

profile of v1, /device:TPU:9, one launch (start us, length us, event | category | flops | bytes accessed | tf_op | source)
XLA Modules:
  0.0 339.0 jit_solution(13868015925463559615)
XLA Ops:
  2.6 2.5 collective-permute-start.11
  5.3 1.2 collective-permute-start.20
  6.5 2.2 collective-permute-start.21
  8.6 2.5 collective-permute-done.10
  11.2 2.0 collective-permute-start.22
  13.9 1.3 collective-permute-done.11
  15.2 9.9 %collective-permute-done.12 = bf16[152,768]{1,0:T(8,128)(2,1)S(1)} collective-permute-done((bf16[152,768]{1,0:T(8,128)(2,1)S(1)}, bf16[152,768]{1,0:T(8,128)(2,1)S(1)}, u32[]{:S(2)}, u32[]{:S(2)}) %collective-permute-start.12) | collective-permute-done | bytes 233504 | tf_op jit(solution)/shard_map/ppermute | solution.py:350
  25.3 1.3 collective-permute-start.13
  27.1 1.9 shard_map.228
  29.0 14.2 %collective-permute-done.21 = bf16[2,96,768]{2,1,0:T(8,128)(2,1)S(1)} collective-permute-done((bf16[2,96,768]{2,1,0:T(8,128)(2,1)S(1)}, bf16[2,96,768]{2,1,0:T(8,128)(2,1)S(1)}, u32[]{:S(2)}, u32[]{:S(2)}) %collective-permute-start.21) | collective-permute-done | bytes 294944 | tf_op jit(solution)/shard_map/ppermute | solution.py:350
  43.2 7.2 %collective-permute-done.22 = bf16[2,96,768]{2,1,0:T(8,128)(2,1)S(1)} collective-permute-done((bf16[2,96,768]{2,1,0:T(8,128)(2,1)S(1)}, bf16[2,96,768]{2,1,0:T(8,128)(2,1)S(1)}, u32[]{:S(2)}, u32[]{:S(2)}) %collective-permute-start.22) | collective-permute-done | bytes 294944 | tf_op jit(solution)/shard_map/ppermute | solution.py:350
  50.6 1.3 collective-permute-start.23
  51.9 1.3 collective-permute-start.1
  53.2 2.4 collective-permute-start
  55.6 1.0 collective-permute-done.4
  56.6 1.3 collective-permute-start.5
  57.9 3.1 collective-permute-done.5
  61.9 1.3 collective-permute-start.16
  63.2 4.2 %collective-permute-start.2 = (bf16[256,768]{1,0:T(8,128)(2,1)S(1)}, bf16[256,768]{1,0:T(8,128)(2,1)}, u32[]{:S(2)}, u32[]{:S(2)}) collective-permute-start(bf16[256,768]{1,0:T(8,128)(2,1)S(1)} %collective-permute-done.1.h2), channel_id=1, source_target_pairs={{0,1},{1,0},{2,3},{3,2},{4,5},{5,4},{6,7},{7,6},{8,9},{9,8},{10,11... | collective-permute-start | bytes 1179656 | tf_op jit(solution)/shard_map/ppermute | solution.py:350
  67.5 1.0 slice.233
  68.5 18.5 %collective-permute-done.6.wb = bf16[4,96,640]{2,1,0:T(8,128)(2,1)S(1)} collective-permute-done((bf16[4,96,640]{2,1,0:T(8,128)(2,1)S(1)}, bf16[4,96,640]{2,1,0:T(8,128)(2,1)S(1)}, u32[]{:S(2)}, u32[]{:S(2)}) %collective-permute-start.6) | collective-permute-done | bytes 491552 | tf_op jit(solution)/shard_map/ppermute | solution.py:350
  87.0 1.2 collective-permute-start.17
  88.3 13.1 %shard_map.229 = (bf16[256,192]{1,0:T(8,128)(2,1)}, bf16[256,192]{1,0:T(8,128)(2,1)}, bf16[256,192]{1,0:T(8,128)(2,1)}, bf16[256,192]{1,0:T(8,128)(2,1)}, bf16[3...) custom-call(s32[3]{0:T(128)} %pad_add_fusion.sc, ...), custom_call_target="tpu_custom_call" | custom-call | flops 2000000000 | bytes 8000000 | tf_op jit(solution)/shard_map/pallas_call | solution.py:385
  101.4 3.0 collective-permute-start.7
  106.1 3.6 %collective-permute-done.8.g2 = bf16[256,192]{1,0:T(8,128)(2,1)S(1)} collective-permute-done((bf16[256,192]{1,0:T(8,128)(2,1)}, bf16[256,192]{1,0:T(8,128)(2,1)S(1)}, u32[]{:S(2)}, u32[]{:S(2)}) %collective-permute-start.8) | collective-permute-done | bytes 98336 | tf_op jit(solution)/shard_map/ppermute | solution.py:350
  109.6 1.3 collective-permute-start.9
  110.9 5.0 %collective-permute-done.9.g3 = bf16[256,192]{1,0:T(8,128)(2,1)} collective-permute-done((bf16[256,192]{1,0:T(8,128)(2,1)}, bf16[256,192]{1,0:T(8,128)(2,1)}, u32[]{:S(2)}, u32[]{:S(2)}) %collective-permute-start.9) | collective-permute-done | bytes 98336 | tf_op jit(solution)/shard_map/ppermute | solution.py:350
  117.1 1.5 collective-permute-done.15.tf.w1f
  119.5 3.7 %shard_map.230 = (bf16[256,768]{1,0:T(8,128)(2,1)}, f32[256,768]{1,0:T(8,128)}, bf16[256,768]{1,0:T(8,128)(2,1)}) custom-call(s32[3]{0:T(128)} %pad_add_fusion.sc, bf16[256,192]{1,0:T(8,128)(2,1)} %get-tuple-element.57.g0, bf16[256,192]{1,0:T(8,128)(2,1)} %copy-done.20, bf16[256,192]{1,0:T(8,128)(2,1)} %copy-done.21, ...), custom_call_target="tpu_custom_call" | custom-call | flops 300000000 | bytes 3000000 | tf_op jit(solution)/shard_map/pallas_call | solution.py:385
  124.0 8.3 %shard_map.231 = (bf16[4,256,768]{2,1,0:T(8,128)(2,1)}, bf16[4,256,768]{2,1,0:T(8,128)(2,1)}, bf16[4,256,768]{2,1,0:T(8,128)(2,1)}, f32[256,1]{1,0:T(8,128)}, f32[4,8,768]{2,1,0:T(8,128)}) custom-call(s32[3]{0:T(128)} %pad_add_fusion.sc, bf16[256,768]{1,0:T(8,128)(2,1)} %get-tuple-element.62.ffn, bf16[4,152,768]{2,1,0:T(8,128)(2,1)} %copy-done.2, ...), custom_call_target="tpu_custom_call" | custom-call | flops 1200000000 | bytes 10000000 | tf_op jit(solution)/shard_map/pallas_call | solution.py:385
  132.3 1.0 copy-done.11
  133.4 6.2 %shard_map.232 = (bf16[256,768]{1,0:T(8,128)(2,1)}, f32[256,768]{1,0:T(8,128)}, bf16[256,768]{1,0:T(8,128)(2,1)}, f32[8,768]{1,0:T(8,128)}) custom-call(s32[3]{0:T(128)} %pad_add_fusion.sc, bf16[4,256,768]{2,1,0:T(8,128)(2,1)} %get-tuple-element.63.act, f32[256,768]{1,0:T(8,128)} %get-tuple-element.64.resid, bf16[256,768]{1,0:T(8,128)(2,1)} %bitcast.148, ...), custom_call_target="tpu_custom_call" | custom-call | flops 1200000000 | bytes 8000000 | tf_op jit(solution)/shard_map/pallas_call | solution.py:385
  139.5 27.6 %shard_map.233 = (bf16[4,256,768]{2,1,0:T(8,128)(2,1)}, bf16[256,768]{1,0:T(8,128)(2,1)}, f32[256,768]{1,0:T(8,128)}, bf16[256,192]{1,0:T(8,128)(2,1)}, bf16[256...) custom-call(s32[3]{0:T(128)} %pad_add_fusion.sc, ...), custom_call_target="tpu_custom_call" | custom-call | flops 2700000000 | bytes 20000000 | tf_op jit(solution)/shard_map/pallas_call | solution.py:385
  168.1 1.3 collective-permute-start.28
  169.4 6.0 %shard_map.235 = (bf16[2,8,96,768]{3,2,1,0:T(8,128)(2,1)}, bf16[2,8,96,768]{3,2,1,0:T(8,128)(2,1)}, bf16[8,48,768]{2,1,0:T(8,128)(2,1)}, bf16[8,48,768]{2,1,0:T(8,128)(2,1)}) custom-call(s32[3]{0:T(128)} %pad_add_fusion.sc, bf16[256,768]{1,0:T(8,128)(2,1)} %get-tuple-element.62.ffn, bf16[4,256,768]{2,1,0:T(8,128)(2,1)} %get-tuple-element.92.up, ...), custom_call_target="tpu_custom_call" | custom-call | flops 1500000000 | bytes 8000000 | tf_op jit(solution)/shard_map/pallas_call | solution.py:385
  176.5 15.4 %shard_map.234 = (bf16[256,768]{1,0:T(8,128)(2,1)}, bf16[256,768]{1,0:T(8,128)(2,1)}, bf16[256,768]{1,0:T(8,128)(2,1)}, bf16[256,768]{1,0:T(8,128)(2,1)}, bf16[4...) custom-call(s32[3]{0:T(128)} %pad_add_fusion.sc, bf16[256,192]{1,0:T(8,128)(2,1)} %get-tuple-element.72.d0, ...), custom_call_target="tpu_custom_call" | custom-call | flops 4000000000 | bytes 12000000 | tf_op jit(solution)/shard_map/pallas_call | solution.py:385
  191.9 1.3 collective-permute-start.29
  194.5 5.2 %shard_map.236 = (bf16[2,8,96,768]{3,2,1,0:T(8,128)(2,1)}, bf16[2,8,96,768]{3,2,1,0:T(8,128)(2,1)}) custom-call(s32[3]{0:T(128)} %pad_add_fusion.sc, bf16[4,256,768]{2,1,0:T(8,128)(2,1)} %get-tuple-element.63.act, bf16[256,768]{1,0:T(8,128)(2,1)} %get-tuple-element.66.low), custom_call_target="tpu_custom_call" | custom-call | flops 1200000000 | bytes 7000000 | tf_op jit(solution)/shard_map/pallas_call | solution.py:385
  200.3 6.3 %collective-permute-done.29 = bf16[4,112,576]{2,1,0:T(8,128)(2,1)S(1)} collective-permute-done((bf16[4,112,576]{2,1,0:T(8,128)(2,1)}, bf16[4,112,576]{2,1,0:T(8,128)(2,1)S(1)}, u32[]{:S(2)}, u32[]{:S(2)}) %collective-permute-start.29) | collective-permute-done | bytes 516128 | tf_op jit(solution)/shard_map/ppermute | solution.py:350
  206.9 3.4 %collective-permute-start.31 = (bf16[112,576]{1,0:T(8,128)(2,1)S(1)}, bf16[112,576]{1,0:T(8,128)(2,1)S(1)}, u32[]{:S(2)}, u32[]{:S(2)}) collective-permute-start(bf16[112,576]{1,0:T(8,128)(2,1)S(1)} %get-tuple-element.138), channel_id=1, source_target_pairs={{0,16},{1,17},{2,18},{3,19},{4,20},{5,21},{6,22},{7,23},{8,24},{9,... | collective-permute-start | bytes 387080 | tf_op jit(solution)/shard_map/ppermute | solution.py:350
  211.1 3.9 %collective-permute-start.55 = (bf16[2,8,96,768]{3,2,1,0:T(8,128)(2,1)S(1)}, bf16[2,8,96,768]{3,2,1,0:T(8,128)(2,1)S(1)}, u32[]{:S(2)}, u32[]{:S(2)}) collective-permute-start(bf16[2,8,96,768]{3,2,1,0:T(8,128)(2,1)S(1)} %copy-done.27), channel_id=1, source_target_pairs={{0,1},{1,0},{2,3},{3,2},{4,5},{5,4},{6,7},{7,6},{8,9},{9,8},{10,11... | collective-permute-start | bytes 7077896 | tf_op jit(solution)/shard_map/ppermute | solution.py:350
  215.3 6.2 %collective-permute-start.36 = (bf16[256,768]{1,0:T(8,128)(2,1)S(1)}, bf16[256,768]{1,0:T(8,128)(2,1)S(1)}, u32[]{:S(2)}, u32[]{:S(2)}) collective-permute-start(bf16[256,768]{1,0:T(8,128)(2,1)S(1)} %copy-done.31), channel_id=1, source_target_pairs={{0,1},{1,0},{2,3},{3,2},{4,5},{5,4},{6,7},{7,6},{8,9},{9,8},{10,11... | collective-permute-start | bytes 1179656 | tf_op jit(solution)/shard_map/ppermute | solution.py:350
  222.4 1.0 collective-permute-start.34
  223.6 2.0 collective-permute-start.41
  225.6 4.6 %collective-permute-done.38 = bf16[256,768]{1,0:T(8,128)(2,1)S(1)} collective-permute-done((bf16[256,768]{1,0:T(8,128)(2,1)S(1)}, bf16[256,768]{1,0:T(8,128)(2,1)S(1)}, u32[]{:S(2)}, u32[]{:S(2)}) %collective-permute-start.38) | collective-permute-done | bytes 393248 | tf_op jit(solution)/shard_map/ppermute | solution.py:350
  230.2 5.1 %collective-permute-start.42 = (bf16[48,768]{1,0:T(8,128)(2,1)S(1)}, bf16[48,768]{1,0:T(8,128)(2,1)S(1)}, u32[]{:S(2)}, u32[]{:S(2)}) collective-permute-start(bf16[48,768]{1,0:T(8,128)(2,1)S(1)} %get-tuple-element.141), channel_id=1, source_target_pairs={{0,16},{1,17},{2,18},{3,19},{4,20},{5,21},{6,22},{7,23},{8,24},{9,... | collective-permute-start | bytes 221192 | tf_op jit(solution)/shard_map/ppermute | solution.py:350
  236.9 1.0 add_bitcast_fusion
  237.9 2.0 collective-permute-start.33
  240.3 1.6 collective-permute-done.43
  243.3 1.0 collective-permute-start.47
  245.5 1.0 collective-permute-start.56
  247.4 23.5 %collective-permute-done.47 = bf16[8,96,768]{2,1,0:T(8,128)(2,1)S(1)} collective-permute-done((bf16[8,96,768]{2,1,0:T(8,128)(2,1)S(1)}, bf16[8,96,768]{2,1,0:T(8,128)(2,1)S(1)}, u32[]{:S(2)}, u32[]{:S(2)}) %collective-permute-start.47) | collective-permute-done | bytes 1179680 | tf_op jit(solution)/shard_map/ppermute | solution.py:350
  271.3 1.3 collective-permute-start.48
  273.1 23.1 %collective-permute-done.56 = bf16[8,96,768]{2,1,0:T(8,128)(2,1)S(1)} collective-permute-done((bf16[8,96,768]{2,1,0:T(8,128)(2,1)S(1)}, bf16[8,96,768]{2,1,0:T(8,128)(2,1)S(1)}, u32[]{:S(2)}, u32[]{:S(2)}) %collective-permute-start.56) | collective-permute-done | bytes 1179680 | tf_op jit(solution)/shard_map/ppermute | solution.py:350
  296.7 1.3 collective-permute-start.57
  298.9 1.2 collective-permute-start.50
  300.1 1.4 collective-permute-start.51
  301.5 8.5 %collective-permute-done.57 = bf16[4,96,768]{2,1,0:T(8,128)(2,1)S(1)} collective-permute-done((bf16[4,96,768]{2,1,0:T(8,128)(2,1)S(1)}, bf16[4,96,768]{2,1,0:T(8,128)(2,1)S(1)}, u32[]{:S(2)}, u32[]{:S(2)}) %collective-permute-start.57) | collective-permute-done | bytes 589856 | tf_op jit(solution)/shard_map/ppermute | solution.py:350
  310.8 2.1 collective-permute-start.60
  312.9 3.5 %collective-permute-done.51 = bf16[96,768]{1,0:T(8,128)(2,1)S(1)} collective-permute-done((bf16[96,768]{1,0:T(8,128)(2,1)S(1)}, bf16[96,768]{1,0:T(8,128)(2,1)S(1)}, u32[]{:S(2)}, u32[]{:S(2)}) %collective-permute-start.51) | collective-permute-done | bytes 147488 | tf_op jit(solution)/shard_map/ppermute | solution.py:350
  316.9 10.3 %collective-permute-done.60 = bf16[96,768]{1,0:T(8,128)(2,1)S(1)} collective-permute-done((bf16[96,768]{1,0:T(8,128)(2,1)S(1)}, bf16[96,768]{1,0:T(8,128)(2,1)S(1)}, u32[]{:S(2)}, u32[]{:S(2)}) %collective-permute-start.60) | collective-permute-done | bytes 147488 | tf_op jit(solution)/shard_map/ppermute | solution.py:350
  327.7 1.7 collective-permute-start.45
  335.5 1.1 maximum_convert_fusion.1
  336.6 1.1 maximum_convert_fusion
  (206 shorter events, 28.4 us)
Async XLA Ops:
  2.5 8.7 %collective-permute-start.10 = (bf16[152,768]{1,0:T(8,128)(2,1)S(1)}, bf16[152,768]{1,0:T(8,128)(2,1)S(1)}, u32[]{:S(2)}, u32[]{:S(2)}) collective-permute-start(bf16[152,768]{1,0:T(8,128)(2,1)S(1)} %get-tuple-element.145), channel_id=1, source_target_pairs={{0,8},{1,9},{2,10},{3,11},{4,12},{5,13},{6,14},{7,15},{8,0},{9,1},... | collective-permute-start | bytes 700424 | tf_op jit(solution)/shard_map/ppermute | solution.py:350
  2.6 12.6 %collective-permute-start.11 = (bf16[152,768]{1,0:T(8,128)(2,1)S(1)}, bf16[152,768]{1,0:T(8,128)(2,1)S(1)}, u32[]{:S(2)}, u32[]{:S(2)}) collective-permute-start(bf16[152,768]{1,0:T(8,128)(2,1)S(1)} %get-tuple-element.145), channel_id=1, source_target_pairs={{0,16},{1,17},{2,18},{3,19},{4,20},{5,21},{6,22},{7,23},{8,24},{9,... | collective-permute-start | bytes 700424 | tf_op jit(solution)/shard_map/ppermute | solution.py:350
  5.0 20.1 %collective-permute-start.12 = (bf16[152,768]{1,0:T(8,128)(2,1)S(1)}, bf16[152,768]{1,0:T(8,128)(2,1)S(1)}, u32[]{:S(2)}, u32[]{:S(2)}) collective-permute-start(bf16[152,768]{1,0:T(8,128)(2,1)S(1)} %get-tuple-element.145), channel_id=1, source_target_pairs={{0,24},{1,25},{2,26},{3,27},{4,28},{5,29},{6,30},{7,31},{8,16},{9,... | collective-permute-start | bytes 700424 | tf_op jit(solution)/shard_map/ppermute | solution.py:350
  5.3 23.7 %collective-permute-start.20 = (bf16[2,96,768]{2,1,0:T(8,128)(2,1)S(1)}, bf16[2,96,768]{2,1,0:T(8,128)(2,1)S(1)}, u32[]{:S(2)}, u32[]{:S(2)}) collective-permute-start(bf16[2,96,768]{2,1,0:T(8,128)(2,1)S(1)} %get-tuple-element.143), channel_id=1, source_target_pairs={{0,8},{1,9},{2,10},{3,11},{4,12},{5,13},{6,14},{7,15},{8,0},{9,1},... | collective-permute-start | bytes 884744 | tf_op jit(solution)/shard_map/ppermute | solution.py:350
  6.5 36.7 %collective-permute-start.21 = (bf16[2,96,768]{2,1,0:T(8,128)(2,1)S(1)}, bf16[2,96,768]{2,1,0:T(8,128)(2,1)S(1)}, u32[]{:S(2)}, u32[]{:S(2)}) collective-permute-start(bf16[2,96,768]{2,1,0:T(8,128)(2,1)S(1)} %get-tuple-element.143), channel_id=1, source_target_pairs={{0,16},{1,17},{2,18},{3,19},{4,20},{5,21},{6,22},{7,23},{8,24},{9,... | collective-permute-start | bytes 884744 | tf_op jit(solution)/shard_map/ppermute | solution.py:350
  11.2 39.2 %collective-permute-start.22 = (bf16[2,96,768]{2,1,0:T(8,128)(2,1)S(1)}, bf16[2,96,768]{2,1,0:T(8,128)(2,1)S(1)}, u32[]{:S(2)}, u32[]{:S(2)}) collective-permute-start(bf16[2,96,768]{2,1,0:T(8,128)(2,1)S(1)} %get-tuple-element.143), channel_id=1, source_target_pairs={{0,24},{1,25},{2,26},{3,27},{4,28},{5,29},{6,30},{7,31},{8,16},{9,... | collective-permute-start | bytes 884744 | tf_op jit(solution)/shard_map/ppermute | solution.py:350
  25.3 42.2 %collective-permute-start.13 = (bf16[4,152,768]{2,1,0:T(8,128)(2,1)S(1)}, bf16[4,152,768]{2,1,0:T(8,128)(2,1)S(1)}, u32[]{:S(2)}, u32[]{:S(2)}) collective-permute-start(bf16[4,152,768]{2,1,0:T(8,128)(2,1)S(1)} %pad_maximum_fusion.1.on.w0n.mn), channel_id=1, source_target_pairs={{0,4},{1,5},{2,6},{3,7},{4,0},{5,1},{6,2},{7,3},{8,12},{9,13},{10,... | collective-permute-start | bytes 2801672 | tf_op jit(solution)/shard_map/ppermute | solution.py:350
  29.0 24.1 %collective-permute-start.3 = (bf16[96,640]{1,0:T(8,128)(2,1)}, bf16[96,640]{1,0:T(8,128)(2,1)S(1)}, u32[]{:S(2)}, u32[]{:S(2)}) collective-permute-start(bf16[96,640]{1,0:T(8,128)(2,1)} %shard_map.228), channel_id=1, source_target_pairs={{0,8},{1,9},{2,10},{3,11},{4,12},{5,13},{6,14},{7,15},{8,0},{9,1},... | collective-permute-start | bytes 368648 | tf_op jit(solution)/shard_map/ppermute | solution.py:350
  50.6 55.4 %collective-permute-start.23 = (bf16[4,2,96,768]{3,2,1,0:T(8,128)(2,1)S(1)}, bf16[4,2,96,768]{3,2,1,0:T(8,128)(2,1)S(1)}, u32[]{:S(2)}, u32[]{:S(2)}) collective-permute-start(bf16[4,2,96,768]{3,2,1,0:T(8,128)(2,1)S(1)} %pad_maximum_fusion.on.don), channel_id=1, source_target_pairs={{0,4},{1,5},{2,6},{3,7},{4,0},{5,1},{6,2},{7,3},{8,12},{9,13},{10,... | collective-permute-start | bytes 3538952 | tf_op jit(solution)/shard_map/ppermute | solution.py:350
  51.9 4.7 %collective-permute-start.4 = (bf16[96,640]{1,0:T(8,128)(2,1)S(1)}, bf16[96,640]{1,0:T(8,128)(2,1)S(1)}, u32[]{:S(2)}, u32[]{:S(2)}) collective-permute-start(bf16[96,640]{1,0:T(8,128)(2,1)S(1)} %copy-done.23), channel_id=1, source_target_pairs={{0,16},{1,17},{2,18},{3,19},{4,20},{5,21},{6,22},{7,23},{8,24},{9,... | collective-permute-start | bytes 368648 | tf_op jit(solution)/shard_map/ppermute | solution.py:350
  51.9 10.0 %collective-permute-start.1 = (bf16[256,768]{1,0:T(8,128)(2,1)S(1)}, bf16[256,768]{1,0:T(8,128)(2,1)S(1)}, u32[]{:S(2)}, u32[]{:S(2)}) collective-permute-start(bf16[256,768]{1,0:T(8,128)(2,1)S(1)} %bitcast.142), channel_id=1, source_target_pairs={{0,2},{1,3},{2,0},{3,1},{4,6},{5,7},{6,4},{7,5},{8,10},{9,11},{10,... | collective-permute-start | bytes 1179656 | tf_op jit(solution)/shard_map/ppermute | solution.py:350
  53.2 10.0 %collective-permute-start = (bf16[256,768]{1,0:T(8,128)(2,1)S(1)}, bf16[256,768]{1,0:T(8,128)(2,1)S(1)}, u32[]{:S(2)}, u32[]{:S(2)}) collective-permute-start(bf16[256,768]{1,0:T(8,128)(2,1)S(1)} %bitcast.143), channel_id=1, source_target_pairs={{0,1},{1,0},{2,3},{3,2},{4,5},{5,4},{6,7},{7,6},{8,9},{9,8},{10,11... | collective-permute-start | bytes 1179656 | tf_op jit(solution)/shard_map/ppermute | solution.py:350
  56.6 4.4 %collective-permute-start.5 = (bf16[96,640]{1,0:T(8,128)(2,1)S(1)}, bf16[96,640]{1,0:T(8,128)(2,1)S(1)}, u32[]{:S(2)}, u32[]{:S(2)}) collective-permute-start(bf16[96,640]{1,0:T(8,128)(2,1)S(1)} %copy-done.23), channel_id=1, source_target_pairs={{0,24},{1,25},{2,26},{3,27},{4,28},{5,29},{6,30},{7,31},{8,16},{9,... | collective-permute-start | bytes 368648 | tf_op jit(solution)/shard_map/ppermute | solution.py:350
  61.1 26.0 %collective-permute-start.6 = (bf16[4,96,640]{2,1,0:T(8,128)(2,1)S(1)}, bf16[4,96,640]{2,1,0:T(8,128)(2,1)S(1)}, u32[]{:S(2)}, u32[]{:S(2)}) collective-permute-start(bf16[4,96,640]{2,1,0:T(8,128)(2,1)S(1)} %pad_maximum_fusion.5.wa), channel_id=1, source_target_pairs={{0,4},{1,5},{2,6},{3,7},{4,0},{5,1},{6,2},{7,3},{8,12},{9,13},{10,... | collective-permute-start | bytes 1474568 | tf_op jit(solution)/shard_map/ppermute | solution.py:350
  61.9 42.5 %collective-permute-start.16 = (bf16[4,96,768]{2,1,0:T(8,128)(2,1)S(1)}, bf16[4,96,768]{2,1,0:T(8,128)(2,1)S(1)}, u32[]{:S(2)}, u32[]{:S(2)}) collective-permute-start(bf16[4,96,768]{2,1,0:T(8,128)(2,1)S(1)} %slice.232), channel_id=1, source_target_pairs={{0,2},{1,3},{2,0},{3,1},{4,6},{5,7},{6,4},{7,5},{8,10},{9,11},{10,... | collective-permute-start | bytes 1769480 | tf_op jit(solution)/shard_map/ppermute | solution.py:350
  63.2 25.0 %collective-permute-start.2 = (bf16[256,768]{1,0:T(8,128)(2,1)S(1)}, bf16[256,768]{1,0:T(8,128)(2,1)}, u32[]{:S(2)}, u32[]{:S(2)}) collective-permute-start(bf16[256,768]{1,0:T(8,128)(2,1)S(1)} %collective-permute-done.1.h2), channel_id=1, source_target_pairs={{0,1},{1,0},{2,3},{3,2},{4,5},{5,4},{6,7},{7,6},{8,9},{9,8},{10,11... | collective-permute-start | bytes 1179656 | tf_op jit(solution)/shard_map/ppermute | solution.py:350
  67.4 49.0 %collective-permute-start.14 = (bf16[4,152,768]{2,1,0:T(8,128)(2,1)S(1)}, bf16[4,152,768]{2,1,0:T(8,128)(2,1)S(1)}, u32[]{:S(2)}, u32[]{:S(2)}) collective-permute-start(bf16[4,152,768]{2,1,0:T(8,128)(2,1)S(1)} %pad_maximum_fusion.1.on.w0n.mn), channel_id=1, source_target_pairs={{0,1},{1,0},{2,3},{3,2},{4,5},{5,4},{6,7},{7,6},{8,9},{9,8},{10,11... | collective-permute-start | bytes 2801672 | tf_op jit(solution)/shard_map/ppermute | solution.py:350
  87.0 29.5 %collective-permute-start.17 = (bf16[4,96,768]{2,1,0:T(8,128)(2,1)}, bf16[4,96,768]{2,1,0:T(8,128)(2,1)}, u32[]{:S(2)}, u32[]{:S(2)}) collective-permute-start(bf16[4,96,768]{2,1,0:T(8,128)(2,1)} %slice.233), channel_id=1, source_target_pairs={{0,2},{1,3},{2,0},{3,1},{4,6},{5,7},{6,4},{7,5},{8,10},{9,11},{10,... | collective-permute-start | bytes 1769480 | tf_op jit(solution)/shard_map/ppermute | solution.py:350
  101.4 4.2 %collective-permute-start.7 = (bf16[256,192]{1,0:T(8,128)(2,1)}, bf16[256,192]{1,0:T(8,128)(2,1)S(1)}, u32[]{:S(2)}, u32[]{:S(2)}) collective-permute-start(bf16[256,192]{1,0:T(8,128)(2,1)} %get-tuple-element.58), channel_id=1, source_target_pairs={{0,1},{1,0},{2,3},{3,2},{4,5},{5,4},{6,7},{7,6},{8,9},{9,8},{10,11... | collective-permute-start | bytes 294920 | tf_op jit(solution)/shard_map/ppermute | solution.py:350
  104.4 5.3 %collective-permute-start.8 = (bf16[256,192]{1,0:T(8,128)(2,1)}, bf16[256,192]{1,0:T(8,128)(2,1)S(1)}, u32[]{:S(2)}, u32[]{:S(2)}) collective-permute-start(bf16[256,192]{1,0:T(8,128)(2,1)} %get-tuple-element.59), channel_id=1, source_target_pairs={{0,2},{1,3},{2,0},{3,1},{4,6},{5,7},{6,4},{7,5},{8,10},{9,11},{10,... | collective-permute-start | bytes 294920 | tf_op jit(solution)/shard_map/ppermute | solution.py:350
  105.6 26.7 %collective-permute-start.24 = (bf16[4,2,96,768]{3,2,1,0:T(8,128)(2,1)S(1)}, bf16[4,2,96,768]{3,2,1,0:T(8,128)(2,1)S(1)}, u32[]{:S(2)}, u32[]{:S(2)}) collective-permute-start(bf16[4,2,96,768]{3,2,1,0:T(8,128)(2,1)S(1)} %pad_maximum_fusion.on.don), channel_id=1, source_target_pairs={{0,1},{1,0},{2,3},{3,2},{4,5},{5,4},{6,7},{7,6},{8,9},{9,8},{10,11... | collective-permute-start | bytes 3538952 | tf_op jit(solution)/shard_map/ppermute | solution.py:350
  105.9 26.4 %collective-permute-start.25 = (bf16[4,2,96,768]{3,2,1,0:T(8,128)(2,1)S(1)}, bf16[4,2,96,768]{3,2,1,0:T(8,128)(2,1)}, u32[]{:S(2)}, u32[]{:S(2)}) collective-permute-start(bf16[4,2,96,768]{3,2,1,0:T(8,128)(2,1)S(1)} %collective-permute-done.23.of.dof), channel_id=1, source_target_pairs={{0,1},{1,0},{2,3},{3,2},{4,5},{5,4},{6,7},{7,6},{8,9},{9,8},{10,11... | collective-permute-start | bytes 3538952 | tf_op jit(solution)/shard_map/ppermute | solution.py:350
  109.6 6.2 %collective-permute-start.9 = (bf16[256,192]{1,0:T(8,128)(2,1)}, bf16[256,192]{1,0:T(8,128)(2,1)}, u32[]{:S(2)}, u32[]{:S(2)}) collective-permute-start(bf16[256,192]{1,0:T(8,128)(2,1)} %get-tuple-element.60), channel_id=1, source_target_pairs={{0,3},{1,2},{2,1},{3,0},{4,7},{5,6},{6,5},{7,4},{8,11},{9,10},{10,... | collective-permute-start | bytes 294920 | tf_op jit(solution)/shard_map/ppermute | solution.py:350
  115.9 2.7 collective-permute-start.15
  116.5 6.7 %collective-permute-start.18 = (bf16[4,96,768]{2,1,0:T(8,128)(2,1)S(1)}, bf16[4,96,768]{2,1,0:T(8,128)(2,1)S(1)}, u32[]{:S(2)}, u32[]{:S(2)}) collective-permute-start(bf16[4,96,768]{2,1,0:T(8,128)(2,1)S(1)} %collective-permute-done.16.w2n), channel_id=1, source_target_pairs={{0,1},{1,0},{2,3},{3,2},{4,5},{5,4},{6,7},{7,6},{8,9},{9,8},{10,11... | collective-permute-start | bytes 1769480 | tf_op jit(solution)/shard_map/ppermute | solution.py:350
  116.5 6.6 %collective-permute-start.19 = (bf16[4,96,768]{2,1,0:T(8,128)(2,1)}, bf16[4,96,768]{2,1,0:T(8,128)(2,1)}, u32[]{:S(2)}, u32[]{:S(2)}) collective-permute-start(bf16[4,96,768]{2,1,0:T(8,128)(2,1)} %collective-permute-done.17.w2f), channel_id=1, source_target_pairs={{0,1},{1,0},{2,3},{3,2},{4,5},{5,4},{6,7},{7,6},{8,9},{9,8},{10,11... | collective-permute-start | bytes 1769480 | tf_op jit(solution)/shard_map/ppermute | solution.py:350
  167.2 8.3 %collective-permute-start.26 = (bf16[256,192]{1,0:T(8,128)(2,1)}, bf16[256,192]{1,0:T(8,128)(2,1)S(1)}, u32[]{:S(2)}, u32[]{:S(2)}) collective-permute-start(bf16[256,192]{1,0:T(8,128)(2,1)} %get-tuple-element.73), channel_id=1, source_target_pairs={{0,1},{1,0},{2,3},{3,2},{4,5},{5,4},{6,7},{7,6},{8,9},{9,8},{10,11... | collective-permute-start | bytes 294920 | tf_op jit(solution)/shard_map/ppermute | solution.py:350
  167.6 7.9 %collective-permute-start.27 = (bf16[256,192]{1,0:T(8,128)(2,1)}, bf16[256,192]{1,0:T(8,128)(2,1)S(1)}, u32[]{:S(2)}, u32[]{:S(2)}) collective-permute-start(bf16[256,192]{1,0:T(8,128)(2,1)} %get-tuple-element.74), channel_id=1, source_target_pairs={{0,2},{1,3},{2,0},{3,1},{4,6},{5,7},{6,4},{7,5},{8,10},{9,11},{10,... | collective-permute-start | bytes 294920 | tf_op jit(solution)/shard_map/ppermute | solution.py:350
  168.1 7.7 %collective-permute-start.28 = (bf16[256,192]{1,0:T(8,128)(2,1)}, bf16[256,192]{1,0:T(8,128)(2,1)S(1)}, u32[]{:S(2)}, u32[]{:S(2)}) collective-permute-start(bf16[256,192]{1,0:T(8,128)(2,1)} %get-tuple-element.75), channel_id=1, source_target_pairs={{0,3},{1,2},{2,1},{3,0},{4,7},{5,6},{6,5},{7,4},{8,11},{9,10},{10,... | collective-permute-start | bytes 294920 | tf_op jit(solution)/shard_map/ppermute | solution.py:350
  175.4 24.4 %collective-permute-start.39 = (bf16[8,48,768]{2,1,0:T(8,128)(2,1)}, bf16[8,48,768]{2,1,0:T(8,128)(2,1)S(1)}, u32[]{:S(2)}, u32[]{:S(2)}) collective-permute-start(bf16[8,48,768]{2,1,0:T(8,128)(2,1)} %get-tuple-element.96), channel_id=1, source_target_pairs={{0,1},{1,0},{2,3},{3,2},{4,5},{5,4},{6,7},{7,6},{8,9},{9,8},{10,11... | collective-permute-start | bytes 1769480 | tf_op jit(solution)/shard_map/ppermute | solution.py:350
  191.9 14.7 %collective-permute-start.29 = (bf16[4,112,576]{2,1,0:T(8,128)(2,1)}, bf16[4,112,576]{2,1,0:T(8,128)(2,1)S(1)}, u32[]{:S(2)}, u32[]{:S(2)}) collective-permute-start(bf16[4,112,576]{2,1,0:T(8,128)(2,1)} %get-tuple-element.86), channel_id=1, source_target_pairs={{0,4},{1,5},{2,6},{3,7},{4,0},{5,1},{6,2},{7,3},{8,12},{9,13},{10,... | collective-permute-start | bytes 1548296 | tf_op jit(solution)/shard_map/ppermute | solution.py:350
  193.9 48.6 %collective-permute-start.46 = (bf16[2,8,96,768]{3,2,1,0:T(8,128)(2,1)S(1)}, bf16[2,8,96,768]{3,2,1,0:T(8,128)(2,1)S(1)}, u32[]{:S(2)}, u32[]{:S(2)}) collective-permute-start(bf16[2,8,96,768]{3,2,1,0:T(8,128)(2,1)S(1)} %copy-done.26), channel_id=1, source_target_pairs={{0,1},{1,0},{2,3},{3,2},{4,5},{5,4},{6,7},{7,6},{8,9},{9,8},{10,11... | collective-permute-start | bytes 7077896 | tf_op jit(solution)/shard_map/ppermute | solution.py:350
  199.7 10.6 %collective-permute-start.37 = (bf16[256,768]{1,0:T(8,128)(2,1)}, bf16[256,768]{1,0:T(8,128)(2,1)S(1)}, u32[]{:S(2)}, u32[]{:S(2)}) collective-permute-start(bf16[256,768]{1,0:T(8,128)(2,1)} %get-tuple-element.91), channel_id=1, source_target_pairs={{0,1},{1,0},{2,3},{3,2},{4,5},{5,4},{6,7},{7,6},{8,9},{9,8},{10,11... | collective-permute-start | bytes 1179656 | tf_op jit(solution)/shard_map/ppermute | solution.py:350
  200.0 22.4 %collective-permute-start.40 = (bf16[4,48,768]{2,1,0:T(8,128)(2,1)S(1)}, bf16[4,48,768]{2,1,0:T(8,128)(2,1)S(1)}, u32[]{:S(2)}, u32[]{:S(2)}) collective-permute-start(bf16[4,48,768]{2,1,0:T(8,128)(2,1)S(1)} %slice.254), channel_id=1, source_target_pairs={{0,4},{1,5},{2,6},{3,7},{4,0},{5,1},{6,2},{7,3},{8,12},{9,13},{10,... | collective-permute-start | bytes 884744 | tf_op jit(solution)/shard_map/ppermute | solution.py:350
  206.8 4.3 %collective-permute-start.30 = (bf16[112,576]{1,0:T(8,128)(2,1)S(1)}, bf16[112,576]{1,0:T(8,128)(2,1)S(1)}, u32[]{:S(2)}, u32[]{:S(2)}) collective-permute-start(bf16[112,576]{1,0:T(8,128)(2,1)S(1)} %get-tuple-element.136), channel_id=1, source_target_pairs={{0,8},{1,9},{2,10},{3,11},{4,12},{5,13},{6,14},{7,15},{8,0},{9,1},... | collective-permute-start | bytes 387080 | tf_op jit(solution)/shard_map/ppermute | solution.py:350
  206.9 8.4 %collective-permute-start.31 = (bf16[112,576]{1,0:T(8,128)(2,1)S(1)}, bf16[112,576]{1,0:T(8,128)(2,1)S(1)}, u32[]{:S(2)}, u32[]{:S(2)}) collective-permute-start(bf16[112,576]{1,0:T(8,128)(2,1)S(1)} %get-tuple-element.138), channel_id=1, source_target_pairs={{0,16},{1,17},{2,18},{3,19},{4,20},{5,21},{6,22},{7,23},{8,24},{9,... | collective-permute-start | bytes 387080 | tf_op jit(solution)/shard_map/ppermute | solution.py:350
  210.3 11.6 %collective-permute-start.32 = (bf16[112,576]{1,0:T(8,128)(2,1)S(1)}, bf16[112,576]{1,0:T(8,128)(2,1)S(1)}, u32[]{:S(2)}, u32[]{:S(2)}) collective-permute-start(bf16[112,576]{1,0:T(8,128)(2,1)S(1)} %get-tuple-element.137), channel_id=1, source_target_pairs={{0,24},{1,25},{2,26},{3,27},{4,28},{5,29},{6,30},{7,31},{8,16},{9,... | collective-permute-start | bytes 387080 | tf_op jit(solution)/shard_map/ppermute | solution.py:350
  211.1 33.2 %collective-permute-start.55 = (bf16[2,8,96,768]{3,2,1,0:T(8,128)(2,1)S(1)}, bf16[2,8,96,768]{3,2,1,0:T(8,128)(2,1)S(1)}, u32[]{:S(2)}, u32[]{:S(2)}) collective-permute-start(bf16[2,8,96,768]{3,2,1,0:T(8,128)(2,1)S(1)} %copy-done.27), channel_id=1, source_target_pairs={{0,1},{1,0},{2,3},{3,2},{4,5},{5,4},{6,7},{7,6},{8,9},{9,8},{10,11... | collective-permute-start | bytes 7077896 | tf_op jit(solution)/shard_map/ppermute | solution.py:350
  215.3 8.3 %collective-permute-start.36 = (bf16[256,768]{1,0:T(8,128)(2,1)S(1)}, bf16[256,768]{1,0:T(8,128)(2,1)S(1)}, u32[]{:S(2)}, u32[]{:S(2)}) collective-permute-start(bf16[256,768]{1,0:T(8,128)(2,1)S(1)} %copy-done.31), channel_id=1, source_target_pairs={{0,1},{1,0},{2,3},{3,2},{4,5},{5,4},{6,7},{7,6},{8,9},{9,8},{10,11... | collective-permute-start | bytes 1179656 | tf_op jit(solution)/shard_map/ppermute | solution.py:350
  221.8 8.3 %collective-permute-start.38 = (bf16[256,768]{1,0:T(8,128)(2,1)S(1)}, bf16[256,768]{1,0:T(8,128)(2,1)S(1)}, u32[]{:S(2)}, u32[]{:S(2)}) collective-permute-start(bf16[256,768]{1,0:T(8,128)(2,1)S(1)} %add_convert_fusion.1), channel_id=1, source_target_pairs={{0,2},{1,3},{2,0},{3,1},{4,6},{5,7},{6,4},{7,5},{8,10},{9,11},{10,... | collective-permute-start | bytes 1179656 | tf_op jit(solution)/shard_map/ppermute | solution.py:350
  222.4 13.8 %collective-permute-start.34 = (bf16[112,576]{1,0:T(8,128)(2,1)S(1)}, bf16[112,576]{1,0:T(8,128)(2,1)S(1)}, u32[]{:S(2)}, u32[]{:S(2)}) collective-permute-start(bf16[112,576]{1,0:T(8,128)(2,1)S(1)} %fusion.16), channel_id=1, source_target_pairs={{0,2},{1,3},{2,0},{3,1},{4,6},{5,7},{6,4},{7,5},{8,10},{9,11},{10,... | collective-permute-start | bytes 387080 | tf_op jit(solution)/shard_map/ppermute | solution.py:350
  223.6 14.3 %collective-permute-start.41 = (bf16[48,768]{1,0:T(8,128)(2,1)S(1)}, bf16[48,768]{1,0:T(8,128)(2,1)S(1)}, u32[]{:S(2)}, u32[]{:S(2)}) collective-permute-start(bf16[48,768]{1,0:T(8,128)(2,1)S(1)} %get-tuple-element.139), channel_id=1, source_target_pairs={{0,8},{1,9},{2,10},{3,11},{4,12},{5,13},{6,14},{7,15},{8,0},{9,1},... | collective-permute-start | bytes 221192 | tf_op jit(solution)/shard_map/ppermute | solution.py:350
  230.2 9.7 %collective-permute-start.42 = (bf16[48,768]{1,0:T(8,128)(2,1)S(1)}, bf16[48,768]{1,0:T(8,128)(2,1)S(1)}, u32[]{:S(2)}, u32[]{:S(2)}) collective-permute-start(bf16[48,768]{1,0:T(8,128)(2,1)S(1)} %get-tuple-element.141), channel_id=1, source_target_pairs={{0,16},{1,17},{2,18},{3,19},{4,20},{5,21},{6,22},{7,23},{8,24},{9,... | collective-permute-start | bytes 221192 | tf_op jit(solution)/shard_map/ppermute | solution.py:350
  236.2 5.6 %collective-permute-start.43 = (bf16[48,768]{1,0:T(8,128)(2,1)S(1)}, bf16[48,768]{1,0:T(8,128)(2,1)S(1)}, u32[]{:S(2)}, u32[]{:S(2)}) collective-permute-start(bf16[48,768]{1,0:T(8,128)(2,1)S(1)} %get-tuple-element.140), channel_id=1, source_target_pairs={{0,24},{1,25},{2,26},{3,27},{4,28},{5,29},{6,30},{7,31},{8,16},{9,... | collective-permute-start | bytes 221192 | tf_op jit(solution)/shard_map/ppermute | solution.py:350
  237.9 4.5 %collective-permute-start.33 = (bf16[112,576]{1,0:T(8,128)(2,1)S(1)}, bf16[112,576]{1,0:T(8,128)(2,1)S(1)}, u32[]{:S(2)}, u32[]{:S(2)}) collective-permute-start(bf16[112,576]{1,0:T(8,128)(2,1)S(1)} %fusion.16), channel_id=1, source_target_pairs={{0,1},{1,0},{2,3},{3,2},{4,5},{5,4},{6,7},{7,6},{8,9},{9,8},{10,11... | collective-permute-start | bytes 387080 | tf_op jit(solution)/shard_map/ppermute | solution.py:350
  239.9 2.6 collective-permute-start.35
  241.9 85.8 %collective-permute-start.44 = (bf16[48,768]{1,0:T(8,128)(2,1)S(1)}, bf16[48,768]{1,0:T(8,128)(2,1)S(1)}, u32[]{:S(2)}, u32[]{:S(2)}) collective-permute-start(bf16[48,768]{1,0:T(8,128)(2,1)S(1)} %fusion.18), channel_id=1, source_target_pairs={{0,2},{1,3},{2,0},{3,1},{4,6},{5,7},{6,4},{7,5},{8,10},{9,11},{10,... | collective-permute-start | bytes 221192 | tf_op jit(solution)/shard_map/ppermute | solution.py:350
  243.3 27.7 %collective-permute-start.47 = (bf16[8,96,768]{2,1,0:T(8,128)(2,1)S(1)}, bf16[8,96,768]{2,1,0:T(8,128)(2,1)S(1)}, u32[]{:S(2)}, u32[]{:S(2)}) collective-permute-start(bf16[8,96,768]{2,1,0:T(8,128)(2,1)S(1)} %fusion.4), channel_id=1, source_target_pairs={{0,2},{1,3},{2,0},{3,1},{4,6},{5,7},{6,4},{7,5},{8,10},{9,11},{10,... | collective-permute-start | bytes 3538952 | tf_op jit(solution)/shard_map/ppermute | solution.py:350
  245.5 50.7 %collective-permute-start.56 = (bf16[8,96,768]{2,1,0:T(8,128)(2,1)S(1)}, bf16[8,96,768]{2,1,0:T(8,128)(2,1)S(1)}, u32[]{:S(2)}, u32[]{:S(2)}) collective-permute-start(bf16[8,96,768]{2,1,0:T(8,128)(2,1)S(1)} %fusion.5), channel_id=1, source_target_pairs={{0,2},{1,3},{2,0},{3,1},{4,6},{5,7},{6,4},{7,5},{8,10},{9,11},{10,... | collective-permute-start | bytes 3538952 | tf_op jit(solution)/shard_map/ppermute | solution.py:350
  271.3 27.3 %collective-permute-start.48 = (bf16[4,96,768]{2,1,0:T(8,128)(2,1)S(1)}, bf16[4,96,768]{2,1,0:T(8,128)(2,1)S(1)}, u32[]{:S(2)}, u32[]{:S(2)}) collective-permute-start(bf16[4,96,768]{2,1,0:T(8,128)(2,1)S(1)} %slice.262), channel_id=1, source_target_pairs={{0,4},{1,5},{2,6},{3,7},{4,0},{5,1},{6,2},{7,3},{8,12},{9,13},{10,... | collective-permute-start | bytes 1769480 | tf_op jit(solution)/shard_map/ppermute | solution.py:350
  296.7 13.3 %collective-permute-start.57 = (bf16[4,96,768]{2,1,0:T(8,128)(2,1)S(1)}, bf16[4,96,768]{2,1,0:T(8,128)(2,1)S(1)}, u32[]{:S(2)}, u32[]{:S(2)}) collective-permute-start(bf16[4,96,768]{2,1,0:T(8,128)(2,1)S(1)} %slice.270), channel_id=1, source_target_pairs={{0,4},{1,5},{2,6},{3,7},{4,0},{5,1},{6,2},{7,3},{8,12},{9,13},{10,... | collective-permute-start | bytes 1769480 | tf_op jit(solution)/shard_map/ppermute | solution.py:350
  298.8 11.5 %collective-permute-start.49 = (bf16[96,768]{1,0:T(8,128)(2,1)S(1)}, bf16[96,768]{1,0:T(8,128)(2,1)S(1)}, u32[]{:S(2)}, u32[]{:S(2)}) collective-permute-start(bf16[96,768]{1,0:T(8,128)(2,1)S(1)} %get-tuple-element.127), channel_id=1, source_target_pairs={{0,8},{1,9},{2,10},{3,11},{4,12},{5,13},{6,14},{7,15},{8,0},{9,1},... | collective-permute-start | bytes 442376 | tf_op jit(solution)/shard_map/ppermute | solution.py:350
  298.9 12.0 %collective-permute-start.50 = (bf16[96,768]{1,0:T(8,128)(2,1)S(1)}, bf16[96,768]{1,0:T(8,128)(2,1)S(1)}, u32[]{:S(2)}, u32[]{:S(2)}) collective-permute-start(bf16[96,768]{1,0:T(8,128)(2,1)S(1)} %get-tuple-element.129), channel_id=1, source_target_pairs={{0,16},{1,17},{2,18},{3,19},{4,20},{5,21},{6,22},{7,23},{8,24},{9,... | collective-permute-start | bytes 442376 | tf_op jit(solution)/shard_map/ppermute | solution.py:350
  300.1 16.3 %collective-permute-start.51 = (bf16[96,768]{1,0:T(8,128)(2,1)S(1)}, bf16[96,768]{1,0:T(8,128)(2,1)S(1)}, u32[]{:S(2)}, u32[]{:S(2)}) collective-permute-start(bf16[96,768]{1,0:T(8,128)(2,1)S(1)} %get-tuple-element.128), channel_id=1, source_target_pairs={{0,24},{1,25},{2,26},{3,27},{4,28},{5,29},{6,30},{7,31},{8,16},{9,... | collective-permute-start | bytes 442376 | tf_op jit(solution)/shard_map/ppermute | solution.py:350
  310.2 6.7 %collective-permute-start.58 = (bf16[96,768]{1,0:T(8,128)(2,1)S(1)}, bf16[96,768]{1,0:T(8,128)(2,1)S(1)}, u32[]{:S(2)}, u32[]{:S(2)}) collective-permute-start(bf16[96,768]{1,0:T(8,128)(2,1)S(1)} %get-tuple-element.120), channel_id=1, source_target_pairs={{0,8},{1,9},{2,10},{3,11},{4,12},{5,13},{6,14},{7,15},{8,0},{9,1},... | collective-permute-start | bytes 442376 | tf_op jit(solution)/shard_map/ppermute | solution.py:350
  310.3 6.7 %collective-permute-start.59 = (bf16[96,768]{1,0:T(8,128)(2,1)S(1)}, bf16[96,768]{1,0:T(8,128)(2,1)S(1)}, u32[]{:S(2)}, u32[]{:S(2)}) collective-permute-start(bf16[96,768]{1,0:T(8,128)(2,1)S(1)} %get-tuple-element.122), channel_id=1, source_target_pairs={{0,16},{1,17},{2,18},{3,19},{4,20},{5,21},{6,22},{7,23},{8,24},{9,... | collective-permute-start | bytes 442376 | tf_op jit(solution)/shard_map/ppermute | solution.py:350
  310.8 16.4 %collective-permute-start.60 = (bf16[96,768]{1,0:T(8,128)(2,1)S(1)}, bf16[96,768]{1,0:T(8,128)(2,1)S(1)}, u32[]{:S(2)}, u32[]{:S(2)}) collective-permute-start(bf16[96,768]{1,0:T(8,128)(2,1)S(1)} %get-tuple-element.121), channel_id=1, source_target_pairs={{0,24},{1,25},{2,26},{3,27},{4,28},{5,29},{6,30},{7,31},{8,16},{9,... | collective-permute-start | bytes 442376 | tf_op jit(solution)/shard_map/ppermute | solution.py:350
  316.5 13.0 %collective-permute-start.53 = (bf16[96,768]{1,0:T(8,128)(2,1)S(1)}, bf16[96,768]{1,0:T(8,128)(2,1)S(1)}, u32[]{:S(2)}, u32[]{:S(2)}) collective-permute-start(bf16[96,768]{1,0:T(8,128)(2,1)S(1)} %fusion.14), channel_id=1, source_target_pairs={{0,2},{1,3},{2,0},{3,1},{4,6},{5,7},{6,4},{7,5},{8,10},{9,11},{10,... | collective-permute-start | bytes 442376 | tf_op jit(solution)/shard_map/ppermute | solution.py:350
  327.3 6.5 %collective-permute-start.62 = (bf16[96,768]{1,0:T(8,128)(2,1)S(1)}, bf16[96,768]{1,0:T(8,128)(2,1)S(1)}, u32[]{:S(2)}, u32[]{:S(2)}) collective-permute-start(bf16[96,768]{1,0:T(8,128)(2,1)S(1)} %fusion.12), channel_id=1, source_target_pairs={{0,2},{1,3},{2,0},{3,1},{4,6},{5,7},{6,4},{7,5},{8,10},{9,11},{10,... | collective-permute-start | bytes 442376 | tf_op jit(solution)/shard_map/ppermute | solution.py:350
  327.7 6.5 %collective-permute-start.45 = (bf16[48,768]{1,0:T(8,128)(2,1)S(1)}, bf16[48,768]{1,0:T(8,128)(2,1)S(1)}, u32[]{:S(2)}, u32[]{:S(2)}) collective-permute-start(bf16[48,768]{1,0:T(8,128)(2,1)S(1)} %add_convert_fusion.2), channel_id=1, source_target_pairs={{0,1},{1,0},{2,3},{3,2},{4,5},{5,4},{6,7},{7,6},{8,9},{9,8},{10,11... | collective-permute-start | bytes 221192 | tf_op jit(solution)/shard_map/ppermute | solution.py:350
  329.4 5.6 %collective-permute-start.52 = (bf16[96,768]{1,0:T(8,128)(2,1)S(1)}, bf16[96,768]{1,0:T(8,128)(2,1)S(1)}, u32[]{:S(2)}, u32[]{:S(2)}) collective-permute-start(bf16[96,768]{1,0:T(8,128)(2,1)S(1)} %fusion.14), channel_id=1, source_target_pairs={{0,1},{1,0},{2,3},{3,2},{4,5},{5,4},{6,7},{7,6},{8,9},{9,8},{10,11... | collective-permute-start | bytes 442376 | tf_op jit(solution)/shard_map/ppermute | solution.py:350
  329.4 5.5 %collective-permute-start.54 = (bf16[96,768]{1,0:T(8,128)(2,1)S(1)}, bf16[96,768]{1,0:T(8,128)(2,1)S(1)}, u32[]{:S(2)}, u32[]{:S(2)}) collective-permute-start(bf16[96,768]{1,0:T(8,128)(2,1)S(1)} %collective-permute-done.53), channel_id=1, source_target_pairs={{0,1},{1,0},{2,3},{3,2},{4,5},{5,4},{6,7},{7,6},{8,9},{9,8},{10,11... | collective-permute-start | bytes 442376 | tf_op jit(solution)/shard_map/ppermute | solution.py:350
  333.6 1.4 collective-permute-start.61
  333.8 1.5 collective-permute-start.63
  (35 other events, 384.8 us)

commit v2 on v1

--- a/solution.py
+++ b/solution.py
@@ -350,8 +350,8 @@
     return lax.ppermute(value, AXES, [(i, i ^ mask) for i in range(count)])
 
 
-def near_of(piece):
-    return jnp.stack([piece] + [swap(piece, 8 * step) for step in (1, 2, 3)])
+def along_z(piece):
+    return [swap(piece, 8 * step) for step in (1, 2, 3)]
 
 
 def wide(value):
@@ -360,12 +360,6 @@
 
 def narrow(value):
     return value.astype(jnp.bfloat16)
-
-
-def shared_dp(keep, send):
-    kept = wide(keep) + wide(swap(send, 4))
-    sent = narrow(kept)
-    return kept[0] + sum(wide(swap(sent[step], 8 * step)) for step in (1, 2, 3))
 
 
 def by_ctx(tiles, ctx_at):
@@ -380,18 +374,38 @@
     return pl.BlockSpec(tuple(shape), lambda i: (0,) * len(shape), pipeline_mode=pl.Buffered(1))
 
 
-def call(body, ins, outs, scratch=(), flops=0, moved=0):
+def padded(shape, dtype):
+    lead = math.prod(shape[:-2])
+    size = jnp.dtype(dtype).itemsize
+    rows = -(-shape[-2] // (32 // size)) * (32 // size) if len(shape) > 1 else 8
+    return lead * rows * (-(-shape[-1] // 128) * 128) * size
+
+
+def call(body, ins, outs, scratch=(), us=1, deps=(), room=6):
     pairs = [v if isinstance(v, tuple) else (v, whole(v.shape)) for v in ins[1:]]
+    held = sum(padded(spec.block_shape, v.dtype) for v, spec in pairs)
+    held += sum(padded(shape, dtype) for shape, dtype in (*outs, *scratch))
+    count = len(pairs)
+
+    def kernel(sc, *refs):
+        body(sc, *refs[:count], *refs[count + len(deps):])
+
     return pl.pallas_call(
-        body,
+        kernel,
         grid=(1,),
-        in_specs=[pl.BlockSpec(memory_space=pltpu.SMEM)] + [spec for _, spec in pairs],
+        in_specs=[pl.BlockSpec(memory_space=pltpu.SMEM)] + [spec for _, spec in pairs]
+        + [pl.BlockSpec(memory_space=pl.ANY)] * len(deps),
         out_specs=[whole(shape) for shape, _ in outs],
         out_shape=[jax.ShapeDtypeStruct(shape, dtype) for shape, dtype in outs],
         scratch_shapes=[pltpu.VMEM(shape, dtype) for shape, dtype in scratch],
-        compiler_params=pltpu.CompilerParams(vmem_limit_bytes=VMEM_BYTES),
-        cost_estimate=pl.CostEstimate(flops=flops, bytes_accessed=moved, transcendentals=0),
-    )(ins[0], *[v for v, _ in pairs])
+        compiler_params=pltpu.CompilerParams(vmem_limit_bytes=held + room * 1024 * 1024),
+        cost_estimate=pl.CostEstimate(flops=int(us * 2e7), bytes_accessed=0, transcendentals=0),
+        name=body.__name__,
+    )(ins[0], *[v for v, _ in pairs], *deps)
+
+
+def after(value, *deps):
+    return lax.optimization_barrier((value, *deps))[0]
 
 
 BF, F32 = jnp.bfloat16, jnp.float32
@@ -483,17 +497,17 @@
         ref[...] = ot_o[ctx_at ^ r].T.astype(BF)
 
 
-def attend(sc, hids, wa, wb):
+def attend(sc, hids, wa, wb, deps):
     rows = (256, 192)
     return call(
         attend_body, [sc, *hids, wa, wb],
         [(rows, BF)] * 4 + [((3, 1024, 64), BF)] * 3
         + [((3, 8, 256), F32), ((4, 192, 256), F32), ((1024, 768), BF), ((16, 768), F32)],
-        [((768, 640), BF)], flops=2 * 10 ** 9, moved=8 * 10 ** 6)
+        [((768, 640), BF)], us=13, deps=deps)
 
 
 def attend_back_body(sc, d0, d1, d2, d3, q_i, k_i, v_i, lse_i, ot_i, n_i, h0, h1, h2, h3, wa, wb, vec_i, side_e, side_d, mids,
-                     n0, n1, n2, n3, keep, send, w_scr, do_scr, dq_s, dk_s, dv_s, dk_acc, dv_acc, all_scr, g_scr):
+                     n0, n2, n13, keep, send, w_scr, do_scr, dq_s, dk_s, dv_s, dk_acc, dv_acc, all_scr, g_scr):
     ctx_at, length = sc[1], sc[2]
     lay(sc, w_scr, wa, wb, 96, 96)
     for r, ref in enumerate((d0, d1, d2, d3)):
@@ -534,7 +548,7 @@
     bias_q = jnp.concatenate([jnp.where(ctx_at == j, sums[:, :192], 0.0) for j in range(4)], axis=1)
     bias_v = jnp.concatenate([jnp.where(ctx_at == j, sums[:, 384:], 0.0) for j in range(4)], axis=1)
     gain_sum, shift_sum = jnp.zeros((1, 768), F32), jnp.zeros((1, 768), F32)
-    for r, (ref, out) in enumerate(((h0, n0), (h1, n1), (h2, n2), (h3, n3))):
+    for r, (ref, out) in enumerate(((h0, n0), (h1, n13.at[0]), (h2, n2), (h3, n13.at[1]))):
         rows = pl.ds(pl.multiple_of((ctx_at ^ r) * 256, 256), 256)
         grad = contract(all_scr[rows, :], w_scr[:, :576], 1, 1)
         hat, _ = moments(ref[...].astype(F32))
@@ -553,14 +567,14 @@
     send[...] = g_scr[4:]
 
 
-def attend_back(sc, douts, saved, hids, wa, wb, side_e, side_d, mids):
+def attend_back(sc, douts, saved, hids, wa, wb, side_e, side_d, mids, deps):
     q, k, v, lse, ot, normed, vec = saved
     return call(
         attend_back_body, [sc, *douts, q, k, v, lse, ot, normed, *hids, wa, wb, vec, side_e, side_d, mids],
-        [((256, 768), BF)] * 4 + [((4, 112, 576), BF)] * 2,
+        [((256, 768), BF)] * 2 + [((2, 256, 768), BF)] + [((4, 112, 576), BF)] * 2,
         [((768, 640), BF), ((3, 1024, 64), BF), ((3, 1024, 64), BF), ((3, 1024, 64), BF), ((3, 1024, 64), BF),
          ((1024, 64), F32), ((1024, 64), F32), ((1024, 576), BF), ((8, 112, 576), BF)],
-        flops=4 * 10 ** 9, moved=12 * 10 ** 6)
+        us=12, deps=deps)
 
 
 def part(rows, at):
@@ -573,14 +587,16 @@
     lay(sc, scr, other_near, other_far, 48, 96, 48 * (1 - core))
 
 
-def lay_down(sc, scr, own_near, own_far, other_near, other_far):
-    for c, refs in ((0, (own_near, own_far)), (1, (other_near, other_far))):
-        for y in (0, 1):
-            offset = 96 * (sc[1] ^ (2 * y + c))
-            for xr in (0, 1):
-                for zr in range(4):
-                    at = pl.multiple_of(384 * block_of(sc, xr, zr) + offset, 32)
-                    scr[pl.ds(at, 96), :] = refs[xr][zr, y]
+def lay_down(sc, scr, refs):
+    for c in (0, 1):
+        for xr in (0, 1):
+            for y in (0, 1):
+                lay_one(sc, scr, refs[4 * c + 2 * xr + y], xr, 96 * (sc[1] ^ (2 * y + c)))
+
+
+def lay_one(sc, scr, ref, xr, offset):
+    for zr in range(4):
+        scr[pl.ds(pl.multiple_of(384 * block_of(sc, xr, zr) + offset, 32), 96), :] = ref[zr]
 
 
 def join_heads(sc, scr, pieces):
@@ -616,8 +632,8 @@
     total = jnp.zeros((256, 1), F32)
     for t, (near, far) in enumerate(((w0n, w0f), (w1n, w1f), (w2n, w2f), (w3n, w3f))):
         j = sc[1] ^ t
-        lay(sc, w_scr.at[t % 2], near, far, 96, 96)
-        up = jnp.dot(value, w_scr[t % 2], preferred_element_type=F32) + nat_o[j, 2:3, :]
+        lay(sc, w_scr.at[t], near, far, 96, 96)
+        up = jnp.dot(value, w_scr[t], preferred_element_type=F32) + nat_o[j, 2:3, :]
         chance = 0.5 * (1.0 + lax.erf(up * math.sqrt(0.5)))
         slope_o[j] = (chance + up * jnp.exp(-0.5 * up * up) * (1.0 / math.sqrt(2.0 * math.pi))).astype(BF)
         gelu = up * chance
@@ -636,8 +652,8 @@
         act_o[j] = (hat * nat_o[j, 0:1, :] + nat_o[j, 1:2, :]).astype(BF)
 
 
-def down_body(sc, act, resid, teacher, vec, on, of, tn, tf, out_o, err_o, low_o, side_o, w_scr):
-    lay_down(sc, w_scr, on, of, tn, tf)
+def down_body(sc, act, resid, teacher, vec, e0, e1, e2, e3, e4, e5, e6, e7, out_o, err_o, low_o, side_o, w_scr):
+    lay_down(sc, w_scr, (e0, e1, e2, e3, e4, e5, e6, e7))
     result = resid[...] + vec[9:10]
     for j in range(4):
         result += jnp.dot(act[j], w_scr[768 * j:768 * j + 768, :], preferred_element_type=F32)
@@ -670,10 +686,8 @@
         send[y] = g_scr[2 * y + 1]
 
 
-def ffn_back_body(sc, low, err, resid, hat_i, slope, scale, nat, don, dof, dtn, dtf,
-                  w0n, w0f, w1n, w1f, w2n, w2f, w3n, w3f, on, of, tn, tf, vec, g0, g1, g2, g3,
-                  up_o, branch_o, dres_o, p0, p1, p2, p3, side_o, mids_o, wd_scr, w_scr, dh_scr, a_scr):
-    lay_down(sc, wd_scr, don, dof, dtn, dtf)
+def act_back_body(sc, low, hat_i, slope, scale, nat, e0, e1, e2, e3, e4, e5, e6, e7, up_o, mids_o, wd_scr, dh_scr):
+    lay_down(sc, wd_scr, (e0, e1, e2, e3, e4, e5, e6, e7))
     value = low[...]
     first, second = jnp.zeros((256, 1), F32), jnp.zeros((256, 1), F32)
     for j in range(4):
@@ -693,10 +707,14 @@
         up_o[j] = grad
         mids_o[2:3, 768 * j:768 * j + 768] = jnp.sum(grad.astype(F32), axis=0, keepdims=True)
     mids_o[3:16, :] = jnp.zeros((13, 3072), F32)
+
+
+def ffn_back_body(sc, up_i, err, resid, w0n, w0f, w1n, w1f, w2n, w2f, w3n, w3f, on, of, tn, tf, vec, g0, g1, g2, g3,
+                  branch_o, dres_o, p0, p1, p2, p3, side_o, w_scr, o_scr, a_scr, b_scr):
     grad = jnp.zeros((256, 768), F32)
     for t, (near, far) in enumerate(((w0n, w0f), (w1n, w1f), (w2n, w2f), (w3n, w3f))):
-        lay(sc, w_scr.at[t % 2], near, far, 96, 96)
-        grad += contract(up_o[sc[1] ^ t], w_scr[t % 2], 1, 1)
+        lay(sc, w_scr.at[t], near, far, 96, 96)
+        grad += contract(up_i[sc[1] ^ t], w_scr[t], 1, 1)
     hat, factor = moments(resid[...])
     side_o[1:2, :] = jnp.sum(grad * hat, axis=0, keepdims=True)
     side_o[3:4, :] = jnp.sum(grad, axis=0, keepdims=True)
@@ -705,20 +723,20 @@
     branch = dres.astype(BF)
     branch_o[...] = branch
     side_o[4:5, :] = jnp.sum(branch.astype(F32), axis=0, keepdims=True)
-    lay_out(sc, w_scr.at[0], on, of, tn, tf)
-    grad = contract(branch, w_scr[0], 1, 1)
+    lay_out(sc, o_scr, on, of, tn, tf)
+    grad = contract(branch, o_scr[...], 1, 1)
     hat, factor = moments(join_heads(sc, a_scr, (g0, g1, g2, g3)))
     side_o[0:1, :] = jnp.sum(grad * hat, axis=0, keepdims=True)
     side_o[2:3, :] = jnp.sum(grad, axis=0, keepdims=True)
     side_o[5:8, :] = jnp.zeros((3, 768), F32)
     grad = norm_back(grad * vec[1:2], hat, factor).astype(BF)
     for j in range(4):
-        a_scr[j] = grad[:, 192 * j:192 * j + 192]
+        b_scr[j] = grad[:, 192 * j:192 * j + 192]
     for r, ref in enumerate((p0, p1, p2, p3)):
-        ref[...] = a_scr[sc[1] ^ r]
-
-
-def up_grad_body(sc, ffn, up, mixed, branch, keep, send, out_keep, out_send, g_scr, o_scr):
+        ref[...] = b_scr[sc[1] ^ r]
+
+
+def up_grad_body(sc, ffn, up, keep, send, g_scr):
     value = ffn[...]
     for j in range(4):
         grad = contract(value, up[j], 0, 0).astype(BF)
@@ -727,6 +745,9 @@
     for y in (0, 1):
         keep[y] = g_scr[2 * y]
         send[y] = g_scr[2 * y + 1]
+
+
+def out_grad_body(sc, mixed, branch, out_keep, out_send, o_scr):
     grad = contract(mixed[...], branch[...], 0, 0).astype(BF)
     for b in range(8):
         for c in (0, 1):
@@ -735,8 +756,32 @@
     out_send[...] = o_scr[1]
 
 
-def both(value):
-    return tuple(swap(v, 1) for v in value)
+def added(a, b):
+    return a.astype(F32) + b.astype(F32)
+
+
+def pair_body(sc, keep, got, near0, near1, far0, far1):
+    for y, near, far in ((0, near0, far0), (1, near1, far1)):
+        near[...] = added(keep[y, :4], got[y, :4]).astype(BF)
+        far[...] = added(keep[y, 4:], got[y, 4:]).astype(BF)
+
+
+def slots_body(sc, near, got, own, s1, s2, s3):
+    own[...] = added(near[0], got[0])
+    for at, out in ((1, s1), (2, s2), (3, s3)):
+        out[...] = added(near[at], got[at]).astype(BF)
+
+
+def join_far_body(sc, mine, got, out_keep, out_got, far):
+    far[:, :96, :] = added(mine[...], got[...]).astype(BF)
+    far[:, 96:, :] = added(out_keep[...], out_got[...]).astype(BF)
+
+
+def join_near_body(sc, mine, y_got, out_keep, out_got, x_got, own, s1, s2, s3):
+    for at, out in ((0, own), (1, s1), (2, s2), (3, s3)):
+        kind = out.dtype
+        out[:96, :] = (added(mine[at], y_got[at]) + x_got[at, :96, :].astype(F32)).astype(kind)
+        out[96:, :] = (added(out_keep[at], out_got[at]) + x_got[at, 96:, :].astype(F32)).astype(kind)
 
 
 def fast(
@@ -748,89 +793,134 @@
     sc = jnp.stack([dp_at, ctx_at, lengths[0]]).astype(jnp.int32)
     own = hidden[0]
     tall = (256, 768)
-    h_y = swap(own, 2)
-    h_c = swap(own, 1)
+    barrier = lax.optimization_barrier
+    h_y, h_c = swap(own, 2), swap(own, 1)
     piece = call(pack_body, [sc, w_qkv, norm_gain.T, norm_shift.T, proj_bias.T], [((96, 640), BF)], [((16, 128), F32)])[0]
-    q_near = near_of(piece)
+    q_cols = along_z(piece)
+    mid_rows = jnp.concatenate([mid_gain, mid_shift, up_bias, jnp.zeros((13 * 384,), BF)]).reshape(8, 768)
+    piece_a = jnp.concatenate([
+        lax.dynamic_slice(w_up, (0, 768 * ctx_at), (96, 768)), lax.dynamic_slice(w_out, (48 * core, 0), (48, 768)), mid_rows])
+    down4 = w_down.reshape(4, 96, 768)
+    piece_b, piece_c = (lax.dynamic_index_in_dim(down4, ctx_at ^ t, 0, keepdims=False) for t in (0, 2))
+    q_cols, piece_a, h_y = barrier((q_cols, piece_a, h_y))
+    q_near = jnp.stack([piece] + q_cols)
     q_far = swap(q_near, 4)
     h_yc = swap(h_y, 1)
-    mid_rows = jnp.concatenate([mid_gain, mid_shift, up_bias, jnp.zeros((13 * 384,), BF)]).reshape(8, 768)
-    piece_a = jnp.concatenate([
-        lax.dynamic_slice(w_up, (0, 768 * ctx_at), (96, 768)),
-        lax.dynamic_slice(w_out, (48 * core, 0), (48, 768)), mid_rows])
-    a_near = near_of(piece_a)
+    a_cols = along_z(piece_a)
+    a_cols, q_far, piece_b, h_c, h_yc = barrier((a_cols, q_far, piece_b, h_c, h_yc))
+    a_near = jnp.stack([piece_a] + a_cols)
     a_far = swap(a_near, 4)
-    down4 = w_down.reshape(4, 96, 768)
-    piece_b = jnp.stack([lax.dynamic_index_in_dim(down4, ctx_at ^ t, 0, keepdims=False) for t in (0, 2)])
-    b_near = near_of(piece_b)
-    b_far = swap(b_near, 4)
-
+    y_near = swap(a_near[:, :96], 2)
+    a_near_o = swap(a_near, 1)
+    b_cols = along_z(piece_b)
     hids = [own, h_c, h_y, h_yc]
-    *att, q, k, v, lse, ot, normed, vec = attend(sc, hids, q_near, q_far)
+    *att, q, k, v, lse, ot, normed, vec = attend(sc, hids, q_near, q_far, (a_near,))
+    b_cols, piece_c, att = barrier((b_cols, piece_c, att))
+    c_cols = along_z(piece_c)
+    b_near = jnp.stack([piece_b] + b_cols)
+    a_far, y_near, b_near, att = barrier((a_far, y_near, b_near, att))
+    b_far, b_near_o = swap(b_near, 4), swap(b_near, 1)
     got = [att[0]] + [swap(att[r], r) for r in (1, 2, 3)]
-    a_own = (a_near, a_far)
-    a_other = both(a_own)
-    outs = [(t, part(48, 2)) for t in a_own + a_other]
+    y_far = swap(a_far[:, :96], 2)
+    a_far_o, y_near_o = swap(a_far, 1), swap(y_near, 1)
+    outs = [(t, part(48, 2)) for t in (a_near, a_far, a_near_o, a_far_o)]
     mixed, resid, ffn = call(
         mid_body, [sc, *got, own, vec, *outs], [(tall, BF), (tall, F32), (tall, BF)],
-        [((768, 768), BF), ((4, 256, 192), BF)], flops=3 * 10 ** 8, moved=3 * 10 ** 6)
-    y_own = tuple(swap(t[:, :96], 2) for t in a_own)
-    y_other = both(y_own)
-    ups = [(t, part(96, 0)) for t in a_own + a_other] + [*y_own, *y_other]
+        [((768, 768), BF), ((4, 256, 192), BF)], us=3)
+    c_cols, b_far, mixed = barrier((c_cols, b_far, mixed))
+    c_near = jnp.stack([piece_c] + c_cols)
+    c_far, c_near_o = swap(c_near, 4), swap(c_near, 1)
+    b_far_o, y_far_o = swap(b_far, 1), swap(y_far, 1)
+    ups = [(t, part(96, 0)) for t in (a_near, a_far, a_near_o, a_far_o)] + [y_near, y_far, y_near_o, y_far_o]
     four = (4, 256, 768)
     act, hat, slope, scale, nat = call(
-        up_body, [sc, ffn, *ups] + [(t, part(8, 18)) for t in a_own],
+        up_body, [sc, ffn, *ups] + [(t, part(8, 18)) for t in (a_near, a_far)],
         [(four, BF), (four, BF), (four, BF), ((256, 1), F32), ((4, 8, 768), F32)],
-        [((2, 768, 768), BF), (four, F32), ((8, 8, 768), F32)], flops=12 * 10 ** 8, moved=10 ** 7)
-    downs = (b_near, b_far) + both((b_near, b_far))
+        [((4, 768, 768), BF), (four, F32), ((8, 8, 768), F32)], us=5, deps=(c_near,))
+    c_far_o = swap(c_far, 1)
+    downs = [b_near, c_near, b_far, c_far, b_near_o, c_near_o, b_far_o, c_far_o]
     out, err, low, side_d = call(
         down_body, [sc, act, resid, teacher[0], vec, *downs],
-        [(tall, BF), (tall, F32), (tall, BF), ((8, 768), F32)], [((3072, 768), BF)], flops=12 * 10 ** 8, moved=8 * 10 ** 6)
+        [(tall, BF), (tall, F32), (tall, BF), ((8, 768), F32)], [((3072, 768), BF)], us=5)
     halves_of = ((2, 8, 96, 768), BF)
     down_keep, down_send = call(
-        down_grad_body, [sc, act, low], [halves_of] * 2, [((4, 8, 96, 768), BF)], flops=12 * 10 ** 8, moved=7 * 10 ** 6)
-    *pieces, side_e, mids = call(
-        ffn_back_body, [sc, low, err, resid, hat, slope, scale, nat, *downs, *ups, *outs, vec, *got],
-        [(four, BF), (tall, BF), (tall, F32)] + [((256, 192), BF)] * 4 + [((8, 768), F32), ((16, 3072), F32)],
-        [((3072, 768), BF), ((2, 768, 768), BF), (four, F32), ((4, 256, 192), BF)], flops=27 * 10 ** 8, moved=2 * 10 ** 7)
-    up_low, branch, d_res, *d_att = pieces
-    up_keep, up_send, out_keep, out_send = call(
-        up_grad_body, [sc, ffn, up_low, mixed, branch], [halves_of] * 2 + [((8, 48, 768), BF)] * 2,
-        [((4, 8, 96, 768), BF), ((2, 8, 48, 768), BF)], flops=15 * 10 ** 8, moved=8 * 10 ** 6)
+        down_grad_body, [sc, act, low], [halves_of] * 2, [((4, 8, 96, 768), BF)], us=3)
+    down_got = swap(down_send, 1)
+    up_low, mids = call(
+        act_back_body, [sc, low, hat, slope, scale, nat, *downs], [(four, BF), ((16, 3072), F32)],
+        [((3072, 768), BF), (four, F32)], us=5, deps=(down_keep,))
+    slots = ((4, 96, 768), BF)
+    d_near0, d_near1, d_far0, d_far1 = call(pair_body, [sc, down_keep, down_got], [slots] * 4, us=2, deps=(mids,))
+    d_got0 = swap(d_far0, 4)
+    up_keep, up_send = call(up_grad_body, [sc, ffn, up_low], [halves_of] * 2, [((4, 8, 96, 768), BF)], us=3, deps=(d_near0,))
+    up_got = swap(up_send, 1)
+    branch, d_res, *d_att, side_e = call(
+        ffn_back_body, [sc, up_low, err, resid, *ups, *outs, vec, *got],
+        [(tall, BF), (tall, F32)] + [((256, 192), BF)] * 4 + [((8, 768), F32)],
+        [((4, 768, 768), BF), ((768, 768), BF), ((4, 256, 192), BF), ((4, 256, 192), BF)], us=6, deps=(up_keep,))
+    u_near0, u_near1, u_far0, u_far1 = call(pair_body, [sc, up_keep, up_got], [slots] * 4, us=2, deps=(side_e,))
     d_got = [d_att[0]] + [swap(d_att[r], r) for r in (1, 2, 3)]
-    *dn, q_keep, q_send = attend_back(sc, d_got, (q, k, v, lse, ot, normed, vec), hids, q_near, q_far, side_e, side_d, mids)
-    dn_0 = wide(dn[0]) + wide(swap(dn[1], 1))
-    dn_2 = wide(dn[2]) + wide(swap(dn[3], 1))
-    d_own = dn_0 + wide(swap(narrow(dn_2), 2))
+    out_keep, out_send = call(
+        out_grad_body, [sc, mixed, branch], [((8, 48, 768), BF)] * 2, [((2, 8, 48, 768), BF)], us=1, deps=(u_near0,))
+    out_got = swap(out_send, 1)
+    own_part, sent = ((96, 768), F32), ((96, 768), BF)
+    d_own0, *d_z0 = call(slots_body, [sc, d_near0, d_got0], [own_part] + [sent] * 3, us=1, deps=(out_keep,))
+
+    def along_z_back(parts):
+        return [swap(parts[step - 1], 8 * step) for step in (1, 2, 3)]
+
+    d_z0, d_far1, u_far1, d_got, out_got = barrier((d_z0, d_far1, u_far1, d_got, out_got))
+    d_z0 = along_z_back(d_z0)
+    d_got1 = swap(d_far1, 4)
+    uy_far = swap(u_far1, 2)
+    dn_0, dn_2, dn_13, q_keep, q_send = attend_back(
+        sc, d_got, (q, k, v, lse, ot, normed, vec), hids, q_near, q_far, side_e, side_d, mids, (d_own0, out_got))
+    d_z0, d_got1, uy_far, u_near1, dn_0, dn_2, dn_13, q_keep, q_send = barrier(
+        (d_z0, d_got1, uy_far, u_near1, dn_0, dn_2, dn_13, q_keep, q_send))
+    near, far = (pl.BlockSpec((4, 48, 768), lambda i, at=at: (at, 0, 0), pipeline_mode=pl.Buffered(1)) for at in (0, 1))
+    u_x = call(join_far_body, [sc, u_far0, uy_far, (out_keep, far), (out_got, far)], [((4, 144, 768), BF)], us=1)[0]
+    ux_got = swap(u_x, 4)
+    uy_near = swap(u_near1, 2)
+    d_own1, *d_z1 = call(slots_body, [sc, d_near1, d_got1], [own_part] + [sent] * 3, us=1, deps=(u_x,))
+    d_z1 = along_z_back(d_z1)
+    ux_got, uy_near, d_z1, q_send, dn_13 = barrier((ux_got, uy_near, d_z1, q_send, dn_13))
+    q_got = swap(q_send, 4)
+    u_own, *u_z = call(
+        join_near_body, [sc, u_near0, uy_near, (out_keep, near), (out_got, near), ux_got],
+        [((144, 768), F32)] + [((144, 768), BF)] * 3, us=1)
+    u_z = along_z_back(u_z)
+    dn_got = swap(dn_13, 1)
+
+    def total(own_sum, parts):
+        return narrow(own_sum + sum(wide(t) for t in parts))
+
+    q_got, u_z, dn_got, d_z0, d_z1 = barrier((q_got, u_z, dn_got, d_z0, d_z1))
+    q_own, *q_z = call(slots_body, [sc, q_keep, q_got], [((112, 576), F32)] + [((112, 576), BF)] * 3, us=1)
+    q_z = along_z_back(q_z)
+    dn_2 = swap(narrow(wide(dn_2) + wide(dn_got[1])), 2)
+    sums = jnp.concatenate([total(u_own, u_z), total(d_own0, d_z0), total(d_own1, d_z1)])
+    sums_y = swap(sums, 2)
+    q_z, dn_2, sums_y = barrier((q_z, dn_2, sums_y))
+    q_sum = total(q_own, q_z)
+    q_two = jnp.stack([q_sum, swap(q_sum, 2)])
+    q_more = swap(q_two, 1)
+    q_all = by_ctx([q_two[0], q_more[0], q_two[1], q_more[1]], ctx_at)
+    d_own = wide(dn_0) + wide(dn_got[0]) + wide(dn_2)
     _, pull_own = jax.vjp(lambda t: layer_norm(t, vec[0], vec[3]), wide(own))
     hidden_grad = (d_res + pull_own(d_own)[0])[None]
-    q_share = narrow(shared_dp(q_keep, q_send))
-
-    def ctx_sum(keep, send):
-        pair = wide(keep) + wide(swap(send, 1))
-        total = pair[0] + wide(swap(narrow(pair[1]), 2))
-        return narrow(total[:4]), narrow(total[4:])
-
-    down_share = narrow(shared_dp(*ctx_sum(down_keep, down_send)))
-    up_share = narrow(shared_dp(*ctx_sum(up_keep, up_send)))
-    out_pair = wide(out_keep) + wide(swap(out_send, 1))
-    out_share = narrow(shared_dp(narrow(out_pair[:4]), narrow(out_pair[4:])))
-    out_share = narrow(wide(out_share) + wide(swap(out_share, 2)))
-
-    def ctx_all(share):
-        far = swap(share, 2)
-        return by_ctx([share, swap(share, 1), far, swap(far, 1)], ctx_at)
-
-    q_all = ctx_all(q_share)
+    five = jnp.concatenate([
+        sums[:96], sums_y[:96], narrow(wide(sums[96:144]) + wide(sums_y[96:144])),
+        narrow(wide(sums[144:240]) + wide(sums_y[240:])), narrow(wide(sums[240:]) + wide(sums_y[144:240]))])
+    more = swap(five, 1)
     grad_qkv = wide(jnp.concatenate([q_all[j][:96, 192 * p:192 * p + 192] for p in range(3) for j in range(4)], axis=1))
     rest = sum(wide(t[96:]) for t in q_all)
     mid_gain_out, mid_shift_out, up_bias_out = (rest[i, :384] for i in range(3))
     vec_out = rest[:10, 384:480]
     loss = (rest[10, 384] + rest[10, 385]) / (rest[10, 386] * hidden.shape[2])
-    grad_up = wide(jnp.concatenate(ctx_all(up_share), axis=1))
-    grad_down = wide(jnp.concatenate(ctx_all(down_share), axis=0))
-    out_far = swap(out_share, 1)
-    grad_out = wide(jnp.where(core == 0, jnp.concatenate([out_share, out_far]), jnp.concatenate([out_far, out_share])))
+    grad_up = wide(jnp.concatenate(by_ctx([five[:96], more[:96], five[96:192], more[96:192]], ctx_at), axis=1))
+    out_mine, out_far = five[192:240], more[192:240]
+    grad_out = wide(jnp.where(core == 0, jnp.concatenate([out_mine, out_far]), jnp.concatenate([out_far, out_mine])))
+    grad_down = wide(jnp.concatenate(by_ctx([five[240:336], more[240:336], five[336:], more[336:]], ctx_at), axis=0))
     return (out[None], loss, hidden_grad, grad_qkv, grad_out, grad_up, grad_down,
             vec_out[:3].T, vec_out[3:6].T, vec_out[6:].T, mid_gain_out, mid_shift_out, up_bias_out)
 

time: 338 us -> 260 us (0.77); the launches traced: 339 us -> 255 us
  waiting for transfers between devices: 152 us -> 108 us
  Pallas kernels: 87.4 us -> 51.2 us
  starting transfers between devices: 73.2 us -> 59.1 us
  other arithmetic: 10.8 us -> 18.6 us
    ppermute x64 -> x62, waiting for transfers between devices: 152 us -> 108 us  [swap(): return lax.ppermute(value, AXES, [(i, i ^ mask) for i in range(count)])]
    pallas_call x9 -> x18, Pallas kernels: 87.4 us -> 51.2 us  [call(): pl.pallas_call(kernel, grid=(1,), in_specs=[pl.BlockSpec(memory_space=plt...]
    ppermute x64 -> x62, starting transfers between devices: 73.2 us -> 59.1 us  [swap(): return lax.ppermute(value, AXES, [(i, i ^ mask) for i in range(count)])]
  transfers between devices with their start and end apart: 64 -> 62, of which waited for: 25 -> 28; matrix products, arithmetic and copies ran while one was open for 4% -> 5% of each run, Pallas kernels for 16% -> 16%
where the time goes in v2:
time: 260 us; the launch traced here: 255 us
  waiting for transfers between devices  108 us (42%)
  starting transfers between devices  59.1 us (23%)
  Pallas kernels  51.2 us (20%)
  other arithmetic  18.6 us (7%)
  local copies, waits for them, and re-layouts  12.4 us (5%)
  between operations  5.5 us (2%)
    ppermute x62, waiting for transfers between devices, swap(): return lax.ppermute(value, AXES, [(i, i ^ mask) for i in range(count)])  108 us
    ppermute x62, starting transfers between devices, swap(): return lax.ppermute(value, AXES, [(i, i ^ mask) for i in range(count)])  59.1 us
    pallas_call x18, Pallas kernels, call(): pl.pallas_call(kernel, grid=(1,), in_specs=[pl.BlockSpec(memory_space=plt...  51.2 us
  transfers between devices with their start and end apart: 62, of which 28 were waited for; matrix products, arithmetic and copies ran while one was open for 5% of the time, Pallas kernels for 16%

profile of v2, /device:TPU:9, one launch (start us, length us, event | category | flops | bytes accessed | tf_op | source)
XLA Modules:
  0.0 254.9 jit_solution(5342760756093784201)
XLA Ops:
  5.3 2.5 collective-permute-start.1
  8.0 1.2 collective-permute-start.3
  9.2 1.8 collective-permute-start.8
  13.2 5.2 %collective-permute-done.2 = bf16[96,640]{1,0:T(8,128)(2,1)S(1)} collective-permute-done((bf16[96,640]{1,0:T(8,128)(2,1)S(1)}, bf16[96,640]{1,0:T(8,128)(2,1)S(1)}, u32[]{:S(2)}, u32[]{:S(2)}) %collective-permute-start.2) | collective-permute-done | bytes 122912 | tf_op jit(solution)/shard_map/ppermute | solution.py:350
  18.5 1.3 collective-permute-start.7
  19.8 2.1 collective-permute-start.9
  22.5 2.1 collective-permute-start.5
  25.9 6.4 %collective-permute-done.4 = bf16[152,768]{1,0:T(8,128)(2,1)S(1)} collective-permute-done((bf16[152,768]{1,0:T(8,128)(2,1)S(1)}, bf16[152,768]{1,0:T(8,128)(2,1)S(1)}, u32[]{:S(2)}, u32[]{:S(2)}) %collective-permute-start.4) | collective-permute-done | bytes 233504 | tf_op jit(solution)/shard_map/ppermute | solution.py:350
  32.3 7.4 %collective-permute-done.5 = bf16[152,768]{1,0:T(8,128)(2,1)S(1)} collective-permute-done((bf16[152,768]{1,0:T(8,128)(2,1)S(1)}, bf16[152,768]{1,0:T(8,128)(2,1)S(1)}, u32[]{:S(2)}, u32[]{:S(2)}) %collective-permute-start.5) | collective-permute-done | bytes 233504 | tf_op jit(solution)/shard_map/ppermute | solution.py:350
  39.7 6.1 %collective-permute-done.6 = bf16[152,768]{1,0:T(8,128)(2,1)} collective-permute-done((bf16[152,768]{1,0:T(8,128)(2,1)S(1)}, bf16[152,768]{1,0:T(8,128)(2,1)}, u32[]{:S(2)}, u32[]{:S(2)}) %collective-permute-start.6) | collective-permute-done | bytes 233504 | tf_op jit(solution)/shard_map/ppermute | solution.py:350
  47.4 1.3 collective-permute-start.11
  48.6 2.3 collective-permute-start.13
  51.3 1.6 collective-permute-done.12
  52.9 3.8 %collective-permute-start.18 = (bf16[4,152,768]{2,1,0:T(8,128)(2,1)S(1)}, bf16[4,152,768]{2,1,0:T(8,128)(2,1)S(1)}, u32[]{:S(2)}, u32[]{:S(2)}) collective-permute-start(bf16[4,152,768]{2,1,0:T(8,128)(2,1)S(1)} %pad_maximum_fusion.refs_6_.refs_1_.refs_9_.refs_3_.refs_11_), channel_id=1, source_target_pairs={{0,1},{1,0},{2,3},{3,2},{4,5},{5,4},{6,7},{7,6},{8,9},{9,8},{10,11... | collective-permute-start | bytes 2801672 | tf_op jit(solution)/shard_map/ppermute | solution.py:350
  56.8 9.7 %attend_body.1 = (bf16[256,192]{1,0:T(8,128)(2,1)S(1)}, bf16[256,192]{1,0:T(8,128)(2,1)S(1)}, bf16[256,192]{1,0:T(8,128)(2,1)S(1)}, bf16[256,192]{1,0:T(8,128)(2...) custom-call(s32[3]{0:T(128)S(1)} %pad_add_fusion.sc, ...), custom_call_target="tpu_custom_call" | custom-call | flops 260000000 | tf_op jit(solution)/shard_map/attend_body/pallas_call | solution.py:393
  66.6 1.9 collective-permute-done.10.refs_7_.refs_2_.refs_10_.refs_4_.refs_12_
  68.5 1.7 collective-permute-start.19
  70.7 1.2 collective-permute-start.16
  72.6 3.0 %collective-permute-done.16.refs_2_.refs_18_ = bf16[256,192]{1,0:T(8,128)(2,1)S(1)} collective-permute-done((bf16[256,192]{1,0:T(8,128)(2,1)S(1)}, bf16[256,192]{1,0:T(8,128)(2,1)S(1)}, u32[]{:S(2)}, u32[]{:S(2)}) %collective-permute-start.16) | collective-permute-done | bytes 98336 | tf_op jit(solution)/shard_map/ppermute | solution.py:350
  75.6 3.5 %collective-permute-done.17.refs_3_.refs_19_ = bf16[256,192]{1,0:T(8,128)(2,1)S(1)} collective-permute-done((bf16[256,192]{1,0:T(8,128)(2,1)S(1)}, bf16[256,192]{1,0:T(8,128)(2,1)S(1)}, u32[]{:S(2)}, u32[]{:S(2)}) %collective-permute-start.17) | collective-permute-done | bytes 98336 | tf_op jit(solution)/shard_map/ppermute | solution.py:350
  79.0 1.2 collective-permute-start.25
  80.3 1.3 collective-permute-start.20
  81.5 1.7 mid_body.1
  83.7 5.5 %collective-permute-done.25 = bf16[96,768]{1,0:T(8,128)(2,1)S(1)} collective-permute-done((bf16[96,768]{1,0:T(8,128)(2,1)S(1)}, bf16[96,768]{1,0:T(8,128)(2,1)S(1)}, u32[]{:S(2)}, u32[]{:S(2)}) %collective-permute-start.25) | collective-permute-done | bytes 147488 | tf_op jit(solution)/shard_map/ppermute | solution.py:350
  89.2 1.3 collective-permute-start.27
  90.5 4.7 %collective-permute-done.20.refs_6_.refs_8_ = bf16[4,96,768]{2,1,0:T(8,128)(2,1)S(1)} collective-permute-done((bf16[4,96,768]{2,1,0:T(8,128)(2,1)S(1)}, bf16[4,96,768]{2,1,0:T(8,128)(2,1)S(1)}, u32[]{:S(2)}, u32[]{:S(2)}) %collective-permute-start.20) | collective-permute-done | bytes 589856 | tf_op jit(solution)/shard_map/ppermute | solution.py:350
  96.6 5.7 %collective-permute-done.27.refs_7_.refs_8_ = bf16[4,96,768]{2,1,0:T(8,128)(2,1)S(1)} collective-permute-done((bf16[4,96,768]{2,1,0:T(8,128)(2,1)S(1)}, bf16[4,96,768]{2,1,0:T(8,128)(2,1)S(1)}, u32[]{:S(2)}, u32[]{:S(2)}) %collective-permute-start.27) | collective-permute-done | bytes 589856 | tf_op jit(solution)/shard_map/ppermute | solution.py:350
  102.3 2.8 %collective-permute-start.31 = (bf16[4,96,768]{2,1,0:T(8,128)(2,1)S(1)}, bf16[4,96,768]{2,1,0:T(8,128)(2,1)S(1)}, u32[]{:S(2)}, u32[]{:S(2)}) collective-permute-start(bf16[4,96,768]{2,1,0:T(8,128)(2,1)S(1)} %collective-permute-done.27.refs_7_.refs_8_), channel_id=1, source_target_pairs={{0,1},{1,0},{2,3},{3,2},{4,5},{5,4},{6,7},{7,6},{8,9},{9,8},{10,11... | collective-permute-start | bytes 1769480 | tf_op jit(solution)/shard_map/ppermute | solution.py:350
  105.1 4.2 %up_body.1 = (bf16[4,256,768]{2,1,0:T(8,128)(2,1)S(1)}, bf16[4,256,768]{2,1,0:T(8,128)(2,1)S(1)}, bf16[4,256,768]{2,1,0:T(8,128)(2,1)S(1)}, f32[256,1]{1,0:T(8,128)S(1)}, f32[4,8,768]{2,1,0:T(8,128)S(1)}) custom-call(s32[3]{0:T(128)S(1)} %pad_add_fusion.sc, bf16[256,768]{1,0:T(8,128)(2,1)S(1)} %get-tuple-element.185.refs_0_, ...), custom_call_target="tpu_custom_call" | custom-call | flops 100000000 | tf_op jit(solution)/shard_map/up_body/pallas_call | solution.py:393
  109.3 3.2 %down_body.1 = (bf16[256,768]{1,0:T(8,128)(2,1)}, f32[256,768]{1,0:T(8,128)S(1)}, bf16[256,768]{1,0:T(8,128)(2,1)S(1)}, f32[8,768]{1,0:T(8,128)S(1)}) custom-call(s32[3]{0:T(128)S(1)} %pad_add_fusion.sc, bf16[4,256,768]{2,1,0:T(8,128)(2,1)S(1)} %get-tuple-element.193.refs_0_, f32[256,768]{1,0:T(8,128)S(1)} %get-tuple-element.194.refs_1_.refs_2_, ...), custom_call_target="tpu_custom_call" | custom-call | flops 100000000 | tf_op jit(solution)/shard_map/down_body/pallas_call | solution.py:393
  112.5 2.3 down_grad_body.1
  114.9 4.4 %act_back_body.1 = (bf16[4,256,768]{2,1,0:T(8,128)(2,1)S(1)}, f32[16,3072]{1,0:T(8,128)S(1)}) custom-call(s32[3]{0:T(128)S(1)} %pad_add_fusion.sc, bf16[256,768]{1,0:T(8,128)(2,1)S(1)} %get-tuple-element.197.refs_1_.refs_0_, bf16[4,256,768]{2,1,0:T(8,128)(2,1)S(1)} %get-tuple-element.200.refs_1_, bf16[4,256,768]{2,1,0:T(8,128)(2,1)S(1)} %get-tuple-element.201.refs_2_, ...), custom_call_target="tpu_custom_call" | custom-call | flops 100000000 | tf_op jit(solution)/shard_map/act_back_body/pallas_call | solution.py:393
  120.5 2.3 up_grad_body.1
  123.2 1.2 collective-permute-start.33
  124.4 3.9 %ffn_back_body.1 = (bf16[256,768]{1,0:T(8,128)(2,1)S(1)}, f32[256,768]{1,0:T(8,128)S(1)}, bf16[256,192]{1,0:T(8,128)(2,1)S(1)}, bf16[256,192]{1,0:T(8,128)(2,1)S...) custom-call(s32[3]{0:T(128)S(1)} %pad_add_fusion.sc, ...), custom_call_target="tpu_custom_call" | custom-call | flops 120000000 | tf_op jit(solution)/shard_map/ffn_back_body/pallas_call | solution.py:393
  131.2 1.2 collective-permute-start.36
  133.3 4.6 %collective-permute-done.33.refs_1_ = bf16[4,96,768]{2,1,0:T(8,128)(2,1)S(1)} collective-permute-done((bf16[4,96,768]{2,1,0:T(8,128)(2,1)S(1)}, bf16[4,96,768]{2,1,0:T(8,128)(2,1)S(1)}, u32[]{:S(2)}, u32[]{:S(2)}) %collective-permute-start.33) | collective-permute-done | bytes 589856 | tf_op jit(solution)/shard_map/ppermute | solution.py:350
  139.9 1.2 collective-permute-start.43
  141.2 2.0 collective-permute-start.40
  143.8 11.9 %attend_back_body.1 = (bf16[256,768]{1,0:T(8,128)(2,1)S(1)}, bf16[256,768]{1,0:T(8,128)(2,1)S(1)}, bf16[2,256,768]{2,1,0:T(8,128)(2,1)S(1)}, bf16[4,112,576]{2,1,0:T(8,128)(2,1)S(1)}, bf16[4,112,576]{2,1,0:T(8,128)(2,1)S(1)}) custom-call(s32[3]{0:T(128)S(1)} %pad_add_fusion.sc, bf16[256,192]{1,0:T(8,128)(2,1)S(1)} %get-tuple-element.232.refs_0_, ...), custom_call_target="tpu_custom_call" | custom-call | flops 240000000 | tf_op jit(solution)/shard_map/attend_back_body/pallas_call | solution.py:393
  159.3 1.6 collective-permute-start.47
  161.5 1.6 collective-permute-done.46
  163.2 2.2 collective-permute-done.47
  165.4 8.5 %collective-permute-done.48 = bf16[96,768]{1,0:T(8,128)(2,1)S(1)} collective-permute-done((bf16[96,768]{1,0:T(8,128)(2,1)S(1)}, bf16[96,768]{1,0:T(8,128)(2,1)S(1)}, u32[]{:S(2)}, u32[]{:S(2)}) %collective-permute-start.48) | collective-permute-done | bytes 147488 | tf_op jit(solution)/shard_map/ppermute | solution.py:350
  173.9 2.4 collective-permute-done.44.refs_4_
  176.4 2.8 %collective-permute-start.53 = (bf16[2,256,768]{2,1,0:T(8,128)(2,1)S(1)}, bf16[2,256,768]{2,1,0:T(8,128)(2,1)S(1)}, u32[]{:S(2)}, u32[]{:S(2)}) collective-permute-start(bf16[2,256,768]{2,1,0:T(8,128)(2,1)S(1)} %get-tuple-element.267), channel_id=1, source_target_pairs={{0,1},{1,0},{2,3},{3,2},{4,5},{5,4},{6,7},{7,6},{8,9},{9,8},{10,11... | collective-permute-start | bytes 2359304 | tf_op jit(solution)/shard_map/ppermute | solution.py:350
  181.3 1.7 collective-permute-start.51
  183.7 6.1 %collective-permute-done.50 = bf16[144,768]{1,0:T(8,128)(2,1)S(1)} collective-permute-done((bf16[144,768]{1,0:T(8,128)(2,1)S(1)}, bf16[144,768]{1,0:T(8,128)(2,1)S(1)}, u32[]{:S(2)}, u32[]{:S(2)}) %collective-permute-start.50) | collective-permute-done | bytes 221216 | tf_op jit(solution)/shard_map/ppermute | solution.py:350
  189.8 3.2 %collective-permute-done.51 = bf16[144,768]{1,0:T(8,128)(2,1)S(1)} collective-permute-done((bf16[144,768]{1,0:T(8,128)(2,1)S(1)}, bf16[144,768]{1,0:T(8,128)(2,1)S(1)}, u32[]{:S(2)}, u32[]{:S(2)}) %collective-permute-start.51) | collective-permute-done | bytes 221216 | tf_op jit(solution)/shard_map/ppermute | solution.py:350
  193.0 9.8 %collective-permute-done.52 = bf16[144,768]{1,0:T(8,128)(2,1)S(1)} collective-permute-done((bf16[144,768]{1,0:T(8,128)(2,1)S(1)}, bf16[144,768]{1,0:T(8,128)(2,1)S(1)}, u32[]{:S(2)}, u32[]{:S(2)}) %collective-permute-start.52) | collective-permute-done | bytes 221216 | tf_op jit(solution)/shard_map/ppermute | solution.py:350
  205.0 1.2 collective-permute-start.57
  207.1 2.0 collective-permute-start.55
  211.4 2.3 collective-permute-done.55
  213.7 8.2 %collective-permute-done.56 = bf16[112,576]{1,0:T(8,128)(2,1)S(1)} collective-permute-done((bf16[112,576]{1,0:T(8,128)(2,1)S(1)}, bf16[112,576]{1,0:T(8,128)(2,1)S(1)}, u32[]{:S(2)}, u32[]{:S(2)}) %collective-permute-start.56) | collective-permute-done | bytes 129056 | tf_op jit(solution)/shard_map/ppermute | solution.py:350
  221.9 2.6 %collective-permute-done.57 = bf16[256,768]{1,0:T(8,128)(2,1)} collective-permute-done((bf16[256,768]{1,0:T(8,128)(2,1)}, bf16[256,768]{1,0:T(8,128)(2,1)}, u32[]{:S(2)}, u32[]{:S(2)}) %collective-permute-start.57) | collective-permute-done | bytes 393248 | tf_op jit(solution)/shard_map/ppermute | solution.py:350
  224.6 1.6 slice_dynamic-update-slice_fusion.1
  226.1 1.6 constant_dynamic-update-slice_fusion
  227.8 1.6 fusion.10
  229.4 1.7 slice_bitcast_fusion.5
  231.1 2.3 collective-permute-start.61
  233.8 1.4 fusion.3
  235.3 1.5 fusion.14
  236.8 2.1 collective-permute-done.59
  248.0 1.2 slice_bitcast_fusion.1
  (163 shorter events, 45.1 us)
Async XLA Ops:
  0.6 11.2 %copy-start = (bf16[96,3072]{1,0:T(8,128)(2,1)S(1)}, bf16[96,3072]{1,0:T(8,128)(2,1)}, u32[]{:S(2)}) copy-start(bf16[96,3072]{1,0:T(8,128)(2,1)} %param.18) | copy-start | bytes 1769476
  5.3 7.4 %collective-permute-start = (bf16[96,640]{1,0:T(8,128)(2,1)S(1)}, bf16[96,640]{1,0:T(8,128)(2,1)S(1)}, u32[]{:S(2)}, u32[]{:S(2)}) collective-permute-start(bf16[96,640]{1,0:T(8,128)(2,1)S(1)} %pack_body.1), channel_id=1, source_target_pairs={{0,8},{1,9},{2,10},{3,11},{4,12},{5,13},{6,14},{7,15},{8,0},{9,1},... | collective-permute-start | bytes 368648 | tf_op jit(solution)/shard_map/ppermute | solution.py:350
  5.3 7.8 %collective-permute-start.1 = (bf16[96,640]{1,0:T(8,128)(2,1)S(1)}, bf16[96,640]{1,0:T(8,128)(2,1)S(1)}, u32[]{:S(2)}, u32[]{:S(2)}) collective-permute-start(bf16[96,640]{1,0:T(8,128)(2,1)S(1)} %pack_body.1), channel_id=1, source_target_pairs={{0,16},{1,17},{2,18},{3,19},{4,20},{5,21},{6,22},{7,23},{8,24},{9,... | collective-permute-start | bytes 368648 | tf_op jit(solution)/shard_map/ppermute | solution.py:350
  7.8 10.6 %collective-permute-start.2 = (bf16[96,640]{1,0:T(8,128)(2,1)S(1)}, bf16[96,640]{1,0:T(8,128)(2,1)S(1)}, u32[]{:S(2)}, u32[]{:S(2)}) collective-permute-start(bf16[96,640]{1,0:T(8,128)(2,1)S(1)} %pack_body.1), channel_id=1, source_target_pairs={{0,24},{1,25},{2,26},{3,27},{4,28},{5,29},{6,30},{7,31},{8,16},{9,... | collective-permute-start | bytes 368648 | tf_op jit(solution)/shard_map/ppermute | solution.py:350
  8.0 10.4 %collective-permute-start.3 = (bf16[256,768]{1,0:T(8,128)(2,1)}, bf16[256,768]{1,0:T(8,128)(2,1)S(1)}, u32[]{:S(2)}, u32[]{:S(2)}) collective-permute-start(bf16[256,768]{1,0:T(8,128)(2,1)} %bitcast.95), channel_id=1, source_target_pairs={{0,2},{1,3},{2,0},{3,1},{4,6},{5,7},{6,4},{7,5},{8,10},{9,11},{10,... | collective-permute-start | bytes 1179656 | tf_op jit(solution)/shard_map/ppermute | solution.py:350
  9.2 15.4 %collective-permute-start.8 = (bf16[256,768]{1,0:T(8,128)(2,1)}, bf16[256,768]{1,0:T(8,128)(2,1)S(1)}, u32[]{:S(2)}, u32[]{:S(2)}) collective-permute-start(bf16[256,768]{1,0:T(8,128)(2,1)} %bitcast.96), channel_id=1, source_target_pairs={{0,1},{1,0},{2,3},{3,2},{4,5},{5,4},{6,7},{7,6},{8,9},{9,8},{10,11... | collective-permute-start | bytes 1179656 | tf_op jit(solution)/shard_map/ppermute | solution.py:350
  18.5 27.4 %collective-permute-start.7 = (bf16[4,96,640]{2,1,0:T(8,128)(2,1)S(1)}, bf16[4,96,640]{2,1,0:T(8,128)(2,1)S(1)}, u32[]{:S(2)}, u32[]{:S(2)}) collective-permute-start(bf16[4,96,640]{2,1,0:T(8,128)(2,1)S(1)} %pad_maximum_fusion.7.refs_4_.refs_14_), channel_id=1, source_target_pairs={{0,4},{1,5},{2,6},{3,7},{4,0},{5,1},{6,2},{7,3},{8,12},{9,13},{10,... | collective-permute-start | bytes 1474568 | tf_op jit(solution)/shard_map/ppermute | solution.py:350
  19.8 26.1 %collective-permute-start.9 = (bf16[256,768]{1,0:T(8,128)(2,1)S(1)}, bf16[256,768]{1,0:T(8,128)(2,1)S(1)}, u32[]{:S(2)}, u32[]{:S(2)}) collective-permute-start(bf16[256,768]{1,0:T(8,128)(2,1)S(1)} %collective-permute-done.3.refs_2_.refs_12_), channel_id=1, source_target_pairs={{0,1},{1,0},{2,3},{3,2},{4,5},{5,4},{6,7},{7,6},{8,9},{9,8},{10,11... | collective-permute-start | bytes 1179656 | tf_op jit(solution)/shard_map/ppermute | solution.py:350
  21.8 10.5 %collective-permute-start.4 = (bf16[152,768]{1,0:T(8,128)(2,1)S(1)}, bf16[152,768]{1,0:T(8,128)(2,1)S(1)}, u32[]{:S(2)}, u32[]{:S(2)}) collective-permute-start(bf16[152,768]{1,0:T(8,128)(2,1)S(1)} %pad_maximum_fusion.9), channel_id=1, source_target_pairs={{0,8},{1,9},{2,10},{3,11},{4,12},{5,13},{6,14},{7,15},{8,0},{9,1},... | collective-permute-start | bytes 700424 | tf_op jit(solution)/shard_map/ppermute | solution.py:350
  22.5 17.2 %collective-permute-start.5 = (bf16[152,768]{1,0:T(8,128)(2,1)S(1)}, bf16[152,768]{1,0:T(8,128)(2,1)S(1)}, u32[]{:S(2)}, u32[]{:S(2)}) collective-permute-start(bf16[152,768]{1,0:T(8,128)(2,1)S(1)} %pad_maximum_fusion.9), channel_id=1, source_target_pairs={{0,16},{1,17},{2,18},{3,19},{4,20},{5,21},{6,22},{7,23},{8,24},{9,... | collective-permute-start | bytes 700424 | tf_op jit(solution)/shard_map/ppermute | solution.py:350
  24.6 21.3 %collective-permute-start.6 = (bf16[152,768]{1,0:T(8,128)(2,1)S(1)}, bf16[152,768]{1,0:T(8,128)(2,1)}, u32[]{:S(2)}, u32[]{:S(2)}) collective-permute-start(bf16[152,768]{1,0:T(8,128)(2,1)S(1)} %pad_maximum_fusion.9), channel_id=1, source_target_pairs={{0,24},{1,25},{2,26},{3,27},{4,28},{5,29},{6,30},{7,31},{8,16},{9,... | collective-permute-start | bytes 700424 | tf_op jit(solution)/shard_map/ppermute | solution.py:350
  45.9 10.9 %copy-start.2 = (bf16[1,256,768]{2,1,0:T(8,128)(2,1)S(1)}, bf16[1,256,768]{2,1,0:T(8,128)(2,1)}, u32[]{:S(2)}) copy-start(bf16[1,256,768]{2,1,0:T(8,128)(2,1)} %param.13) | copy-start | bytes 1179652
  47.0 21.5 %collective-permute-start.10 = (bf16[4,152,768]{2,1,0:T(8,128)(2,1)S(1)}, bf16[4,152,768]{2,1,0:T(8,128)(2,1)S(1)}, u32[]{:S(2)}, u32[]{:S(2)}) collective-permute-start(bf16[4,152,768]{2,1,0:T(8,128)(2,1)S(1)} %pad_maximum_fusion.refs_6_.refs_1_.refs_9_.refs_3_.refs_11_), channel_id=1, source_target_pairs={{0,4},{1,5},{2,6},{3,7},{4,0},{5,1},{6,2},{7,3},{8,12},{9,13},{10,... | collective-permute-start | bytes 2801672 | tf_op jit(solution)/shard_map/ppermute | solution.py:350
  47.4 19.2 %collective-permute-start.11 = (bf16[4,96,768]{2,1,0:T(8,128)(2,1)S(1)}, bf16[4,96,768]{2,1,0:T(8,128)(2,1)S(1)}, u32[]{:S(2)}, u32[]{:S(2)}) collective-permute-start(bf16[4,96,768]{2,1,0:T(8,128)(2,1)S(1)} %slice.180), channel_id=1, source_target_pairs={{0,2},{1,3},{2,0},{3,1},{4,6},{5,7},{6,4},{7,5},{8,10},{9,11},{10,... | collective-permute-start | bytes 1769480 | tf_op jit(solution)/shard_map/ppermute | solution.py:350
  48.6 4.3 %collective-permute-start.12 = (bf16[96,768]{1,0:T(8,128)(2,1)S(1)}, bf16[96,768]{1,0:T(8,128)(2,1)S(1)}, u32[]{:S(2)}, u32[]{:S(2)}) collective-permute-start(bf16[96,768]{1,0:T(8,128)(2,1)S(1)} %get-tuple-element.164), channel_id=1, source_target_pairs={{0,8},{1,9},{2,10},{3,11},{4,12},{5,13},{6,14},{7,15},{8,0},{9,1},... | collective-permute-start | bytes 442376 | tf_op jit(solution)/shard_map/ppermute | solution.py:350
  48.6 17.8 %collective-permute-start.13 = (bf16[96,768]{1,0:T(8,128)(2,1)S(1)}, bf16[96,768]{1,0:T(8,128)(2,1)S(1)}, u32[]{:S(2)}, u32[]{:S(2)}) collective-permute-start(bf16[96,768]{1,0:T(8,128)(2,1)S(1)} %get-tuple-element.164), channel_id=1, source_target_pairs={{0,16},{1,17},{2,18},{3,19},{4,20},{5,21},{6,22},{7,23},{8,24},{9,... | collective-permute-start | bytes 442376 | tf_op jit(solution)/shard_map/ppermute | solution.py:350
  51.0 15.5 %collective-permute-start.14 = (bf16[96,768]{1,0:T(8,128)(2,1)S(1)}, bf16[96,768]{1,0:T(8,128)(2,1)S(1)}, u32[]{:S(2)}, u32[]{:S(2)}) collective-permute-start(bf16[96,768]{1,0:T(8,128)(2,1)S(1)} %get-tuple-element.164), channel_id=1, source_target_pairs={{0,24},{1,25},{2,26},{3,27},{4,28},{5,29},{6,30},{7,31},{8,16},{9,... | collective-permute-start | bytes 442376 | tf_op jit(solution)/shard_map/ppermute | solution.py:350
  52.9 19.0 %collective-permute-start.18 = (bf16[4,152,768]{2,1,0:T(8,128)(2,1)S(1)}, bf16[4,152,768]{2,1,0:T(8,128)(2,1)S(1)}, u32[]{:S(2)}, u32[]{:S(2)}) collective-permute-start(bf16[4,152,768]{2,1,0:T(8,128)(2,1)S(1)} %pad_maximum_fusion.refs_6_.refs_1_.refs_9_.refs_3_.refs_11_), channel_id=1, source_target_pairs={{0,1},{1,0},{2,3},{3,2},{4,5},{5,4},{6,7},{7,6},{8,9},{9,8},{10,11... | collective-permute-start | bytes 2801672 | tf_op jit(solution)/shard_map/ppermute | solution.py:350
  68.5 11.7 %collective-permute-start.19 = (bf16[4,152,768]{2,1,0:T(8,128)(2,1)S(1)}, bf16[4,152,768]{2,1,0:T(8,128)(2,1)S(1)}, u32[]{:S(2)}, u32[]{:S(2)}) collective-permute-start(bf16[4,152,768]{2,1,0:T(8,128)(2,1)S(1)} %collective-permute-done.10.refs_7_.refs_2_.refs_10_.refs_4_.refs_12_), channel_id=1, source_target_pairs={{0,1},{1,0},{2,3},{3,2},{4,5},{5,4},{6,7},{7,6},{8,9},{9,8},{10,11... | collective-permute-start | bytes 2801672 | tf_op jit(solution)/shard_map/ppermute | solution.py:350
  70.2 19.0 %collective-permute-start.26 = (bf16[4,96,768]{2,1,0:T(8,128)(2,1)S(1)}, bf16[4,96,768]{2,1,0:T(8,128)(2,1)S(1)}, u32[]{:S(2)}, u32[]{:S(2)}) collective-permute-start(bf16[4,96,768]{2,1,0:T(8,128)(2,1)S(1)} %pad_maximum_fusion.1.refs_4_.refs_5_), channel_id=1, source_target_pairs={{0,4},{1,5},{2,6},{3,7},{4,0},{5,1},{6,2},{7,3},{8,12},{9,13},{10,... | collective-permute-start | bytes 1769480 | tf_op jit(solution)/shard_map/ppermute | solution.py:350
  70.4 2.1 collective-permute-start.15
  70.7 4.9 %collective-permute-start.16 = (bf16[256,192]{1,0:T(8,128)(2,1)S(1)}, bf16[256,192]{1,0:T(8,128)(2,1)S(1)}, u32[]{:S(2)}, u32[]{:S(2)}) collective-permute-start(bf16[256,192]{1,0:T(8,128)(2,1)S(1)} %get-tuple-element.181), channel_id=1, source_target_pairs={{0,2},{1,3},{2,0},{3,1},{4,6},{5,7},{6,4},{7,5},{8,10},{9,11},{10,... | collective-permute-start | bytes 294920 | tf_op jit(solution)/shard_map/ppermute | solution.py:350
  71.9 7.1 %collective-permute-start.17 = (bf16[256,192]{1,0:T(8,128)(2,1)S(1)}, bf16[256,192]{1,0:T(8,128)(2,1)S(1)}, u32[]{:S(2)}, u32[]{:S(2)}) collective-permute-start(bf16[256,192]{1,0:T(8,128)(2,1)S(1)} %get-tuple-element.182), channel_id=1, source_target_pairs={{0,3},{1,2},{2,1},{3,0},{4,7},{5,6},{6,5},{7,4},{8,11},{9,10},{10,... | collective-permute-start | bytes 294920 | tf_op jit(solution)/shard_map/ppermute | solution.py:350
  72.6 10.7 %collective-permute-start.23 = (bf16[96,768]{1,0:T(8,128)(2,1)S(1)}, bf16[96,768]{1,0:T(8,128)(2,1)S(1)}, u32[]{:S(2)}, u32[]{:S(2)}) collective-permute-start(bf16[96,768]{1,0:T(8,128)(2,1)S(1)} %get-tuple-element.187), channel_id=1, source_target_pairs={{0,8},{1,9},{2,10},{3,11},{4,12},{5,13},{6,14},{7,15},{8,0},{9,1},... | collective-permute-start | bytes 442376 | tf_op jit(solution)/shard_map/ppermute | solution.py:350
  75.6 8.1 %collective-permute-start.24 = (bf16[96,768]{1,0:T(8,128)(2,1)S(1)}, bf16[96,768]{1,0:T(8,128)(2,1)S(1)}, u32[]{:S(2)}, u32[]{:S(2)}) collective-permute-start(bf16[96,768]{1,0:T(8,128)(2,1)S(1)} %get-tuple-element.187), channel_id=1, source_target_pairs={{0,16},{1,17},{2,18},{3,19},{4,20},{5,21},{6,22},{7,23},{8,24},{9,... | collective-permute-start | bytes 442376 | tf_op jit(solution)/shard_map/ppermute | solution.py:350
  79.0 10.1 %collective-permute-start.25 = (bf16[96,768]{1,0:T(8,128)(2,1)S(1)}, bf16[96,768]{1,0:T(8,128)(2,1)S(1)}, u32[]{:S(2)}, u32[]{:S(2)}) collective-permute-start(bf16[96,768]{1,0:T(8,128)(2,1)S(1)} %get-tuple-element.187), channel_id=1, source_target_pairs={{0,24},{1,25},{2,26},{3,27},{4,28},{5,29},{6,30},{7,31},{8,16},{9,... | collective-permute-start | bytes 442376 | tf_op jit(solution)/shard_map/ppermute | solution.py:350
  80.3 15.0 %collective-permute-start.20 = (bf16[4,96,768]{2,1,0:T(8,128)(2,1)S(1)}, bf16[4,96,768]{2,1,0:T(8,128)(2,1)S(1)}, u32[]{:S(2)}, u32[]{:S(2)}) collective-permute-start(bf16[4,96,768]{2,1,0:T(8,128)(2,1)S(1)} %slice.138), channel_id=1, source_target_pairs={{0,2},{1,3},{2,0},{3,1},{4,6},{5,7},{6,4},{7,5},{8,10},{9,11},{10,... | collective-permute-start | bytes 1769480 | tf_op jit(solution)/shard_map/ppermute | solution.py:350
  83.3 13.3 %collective-permute-start.21 = (bf16[4,96,768]{2,1,0:T(8,128)(2,1)S(1)}, bf16[4,96,768]{2,1,0:T(8,128)(2,1)S(1)}, u32[]{:S(2)}, u32[]{:S(2)}) collective-permute-start(bf16[4,96,768]{2,1,0:T(8,128)(2,1)S(1)} %collective-permute-done.11.refs_5_.refs_7_), channel_id=1, source_target_pairs={{0,1},{1,0},{2,3},{3,2},{4,5},{5,4},{6,7},{7,6},{8,9},{9,8},{10,11... | collective-permute-start | bytes 1769480 | tf_op jit(solution)/shard_map/ppermute | solution.py:350
  89.2 13.0 %collective-permute-start.27 = (bf16[4,96,768]{2,1,0:T(8,128)(2,1)S(1)}, bf16[4,96,768]{2,1,0:T(8,128)(2,1)S(1)}, u32[]{:S(2)}, u32[]{:S(2)}) collective-permute-start(bf16[4,96,768]{2,1,0:T(8,128)(2,1)S(1)} %pad_maximum_fusion.2.refs_11_.refs_5_.refs_6_), channel_id=1, source_target_pairs={{0,4},{1,5},{2,6},{3,7},{4,0},{5,1},{6,2},{7,3},{8,12},{9,13},{10,... | collective-permute-start | bytes 1769480 | tf_op jit(solution)/shard_map/ppermute | solution.py:350
  95.3 9.8 %collective-permute-start.22 = (bf16[4,96,768]{2,1,0:T(8,128)(2,1)S(1)}, bf16[4,96,768]{2,1,0:T(8,128)(2,1)S(1)}, u32[]{:S(2)}, u32[]{:S(2)}) collective-permute-start(bf16[4,96,768]{2,1,0:T(8,128)(2,1)S(1)} %collective-permute-done.20.refs_6_.refs_8_), channel_id=1, source_target_pairs={{0,1},{1,0},{2,3},{3,2},{4,5},{5,4},{6,7},{7,6},{8,9},{9,8},{10,11... | collective-permute-start | bytes 1769480 | tf_op jit(solution)/shard_map/ppermute | solution.py:350
  96.1 13.2 %collective-permute-start.28 = (bf16[4,96,768]{2,1,0:T(8,128)(2,1)S(1)}, bf16[4,96,768]{2,1,0:T(8,128)(2,1)S(1)}, u32[]{:S(2)}, u32[]{:S(2)}) collective-permute-start(bf16[4,96,768]{2,1,0:T(8,128)(2,1)S(1)} %pad_maximum_fusion.1.refs_4_.refs_5_), channel_id=1, source_target_pairs={{0,1},{1,0},{2,3},{3,2},{4,5},{5,4},{6,7},{7,6},{8,9},{9,8},{10,11... | collective-permute-start | bytes 1769480 | tf_op jit(solution)/shard_map/ppermute | solution.py:350
  96.1 13.2 %collective-permute-start.29 = (bf16[4,96,768]{2,1,0:T(8,128)(2,1)S(1)}, bf16[4,96,768]{2,1,0:T(8,128)(2,1)S(1)}, u32[]{:S(2)}, u32[]{:S(2)}) collective-permute-start(bf16[4,96,768]{2,1,0:T(8,128)(2,1)S(1)} %pad_maximum_fusion.2.refs_11_.refs_5_.refs_6_), channel_id=1, source_target_pairs={{0,1},{1,0},{2,3},{3,2},{4,5},{5,4},{6,7},{7,6},{8,9},{9,8},{10,11... | collective-permute-start | bytes 1769480 | tf_op jit(solution)/shard_map/ppermute | solution.py:350
  96.6 12.7 %collective-permute-start.30 = (bf16[4,96,768]{2,1,0:T(8,128)(2,1)S(1)}, bf16[4,96,768]{2,1,0:T(8,128)(2,1)S(1)}, u32[]{:S(2)}, u32[]{:S(2)}) collective-permute-start(bf16[4,96,768]{2,1,0:T(8,128)(2,1)S(1)} %collective-permute-done.26.refs_6_.refs_7_), channel_id=1, source_target_pairs={{0,1},{1,0},{2,3},{3,2},{4,5},{5,4},{6,7},{7,6},{8,9},{9,8},{10,11... | collective-permute-start | bytes 1769480 | tf_op jit(solution)/shard_map/ppermute | solution.py:350
  102.3 7.0 %collective-permute-start.31 = (bf16[4,96,768]{2,1,0:T(8,128)(2,1)S(1)}, bf16[4,96,768]{2,1,0:T(8,128)(2,1)S(1)}, u32[]{:S(2)}, u32[]{:S(2)}) collective-permute-start(bf16[4,96,768]{2,1,0:T(8,128)(2,1)S(1)} %collective-permute-done.27.refs_7_.refs_8_), channel_id=1, source_target_pairs={{0,1},{1,0},{2,3},{3,2},{4,5},{5,4},{6,7},{7,6},{8,9},{9,8},{10,11... | collective-permute-start | bytes 1769480 | tf_op jit(solution)/shard_map/ppermute | solution.py:350
  114.8 4.6 %collective-permute-start.32 = (bf16[2,8,96,768]{3,2,1,0:T(8,128)(2,1)S(1)}, bf16[2,8,96,768]{3,2,1,0:T(8,128)(2,1)S(1)}, u32[]{:S(2)}, u32[]{:S(2)}) collective-permute-start(bf16[2,8,96,768]{3,2,1,0:T(8,128)(2,1)S(1)} %get-tuple-element.199), channel_id=1, source_target_pairs={{0,1},{1,0},{2,3},{3,2},{4,5},{5,4},{6,7},{7,6},{8,9},{9,8},{10,11... | collective-permute-start | bytes 7077896 | tf_op jit(solution)/shard_map/ppermute | solution.py:350
  122.8 5.6 %collective-permute-start.34 = (bf16[2,8,96,768]{3,2,1,0:T(8,128)(2,1)S(1)}, bf16[2,8,96,768]{3,2,1,0:T(8,128)(2,1)S(1)}, u32[]{:S(2)}, u32[]{:S(2)}) collective-permute-start(bf16[2,8,96,768]{3,2,1,0:T(8,128)(2,1)S(1)} %get-tuple-element.212), channel_id=1, source_target_pairs={{0,1},{1,0},{2,3},{3,2},{4,5},{5,4},{6,7},{7,6},{8,9},{9,8},{10,11... | collective-permute-start | bytes 7077896 | tf_op jit(solution)/shard_map/ppermute | solution.py:350
  123.2 14.7 %collective-permute-start.33 = (bf16[4,96,768]{2,1,0:T(8,128)(2,1)S(1)}, bf16[4,96,768]{2,1,0:T(8,128)(2,1)S(1)}, u32[]{:S(2)}, u32[]{:S(2)}) collective-permute-start(bf16[4,96,768]{2,1,0:T(8,128)(2,1)S(1)} %get-tuple-element.206), channel_id=1, source_target_pairs={{0,4},{1,5},{2,6},{3,7},{4,0},{5,1},{6,2},{7,3},{8,12},{9,13},{10,... | collective-permute-start | bytes 1769480 | tf_op jit(solution)/shard_map/ppermute | solution.py:350
  130.6 8.6 %collective-permute-start.38 = (bf16[8,48,768]{2,1,0:T(8,128)(2,1)S(1)}, bf16[8,48,768]{2,1,0:T(8,128)(2,1)S(1)}, u32[]{:S(2)}, u32[]{:S(2)}) collective-permute-start(bf16[8,48,768]{2,1,0:T(8,128)(2,1)S(1)} %get-tuple-element.225), channel_id=1, source_target_pairs={{0,1},{1,0},{2,3},{3,2},{4,5},{5,4},{6,7},{7,6},{8,9},{9,8},{10,11... | collective-permute-start | bytes 1769480 | tf_op jit(solution)/shard_map/ppermute | solution.py:350
  131.1 7.5 %collective-permute-start.35 = (bf16[256,192]{1,0:T(8,128)(2,1)S(1)}, bf16[256,192]{1,0:T(8,128)(2,1)S(1)}, u32[]{:S(2)}, u32[]{:S(2)}) collective-permute-start(bf16[256,192]{1,0:T(8,128)(2,1)S(1)} %get-tuple-element.222), channel_id=1, source_target_pairs={{0,1},{1,0},{2,3},{3,2},{4,5},{5,4},{6,7},{7,6},{8,9},{9,8},{10,11... | collective-permute-start | bytes 294920 | tf_op jit(solution)/shard_map/ppermute | solution.py:350
  131.2 7.4 %collective-permute-start.36 = (bf16[256,192]{1,0:T(8,128)(2,1)S(1)}, bf16[256,192]{1,0:T(8,128)(2,1)S(1)}, u32[]{:S(2)}, u32[]{:S(2)}) collective-permute-start(bf16[256,192]{1,0:T(8,128)(2,1)S(1)} %get-tuple-element.223), channel_id=1, source_target_pairs={{0,2},{1,3},{2,0},{3,1},{4,6},{5,7},{6,4},{7,5},{8,10},{9,11},{10,... | collective-permute-start | bytes 294920 | tf_op jit(solution)/shard_map/ppermute | solution.py:350
  132.4 6.8 %collective-permute-start.37 = (bf16[256,192]{1,0:T(8,128)(2,1)S(1)}, bf16[256,192]{1,0:T(8,128)(2,1)S(1)}, u32[]{:S(2)}, u32[]{:S(2)}) collective-permute-start(bf16[256,192]{1,0:T(8,128)(2,1)S(1)} %get-tuple-element.224), channel_id=1, source_target_pairs={{0,3},{1,2},{2,1},{3,0},{4,7},{5,6},{6,5},{7,4},{8,11},{9,10},{10,... | collective-permute-start | bytes 294920 | tf_op jit(solution)/shard_map/ppermute | solution.py:350
  139.3 17.0 %collective-permute-start.42 = (bf16[4,96,768]{2,1,0:T(8,128)(2,1)S(1)}, bf16[4,96,768]{2,1,0:T(8,128)(2,1)S(1)}, u32[]{:S(2)}, u32[]{:S(2)}) collective-permute-start(bf16[4,96,768]{2,1,0:T(8,128)(2,1)S(1)} %get-tuple-element.229), channel_id=1, source_target_pairs={{0,4},{1,5},{2,6},{3,7},{4,0},{5,1},{6,2},{7,3},{8,12},{9,13},{10,... | collective-permute-start | bytes 1769480 | tf_op jit(solution)/shard_map/ppermute | solution.py:350
  139.9 16.3 %collective-permute-start.43 = (bf16[4,96,768]{2,1,0:T(8,128)(2,1)S(1)}, bf16[4,96,768]{2,1,0:T(8,128)(2,1)S(1)}, u32[]{:S(2)}, u32[]{:S(2)}) collective-permute-start(bf16[4,96,768]{2,1,0:T(8,128)(2,1)S(1)} %get-tuple-element.230), channel_id=1, source_target_pairs={{0,2},{1,3},{2,0},{3,1},{4,6},{5,7},{6,4},{7,5},{8,10},{9,11},{10,... | collective-permute-start | bytes 1769480 | tf_op jit(solution)/shard_map/ppermute | solution.py:350
  141.2 14.5 %collective-permute-start.39 = (bf16[96,768]{1,0:T(8,128)(2,1)S(1)}, bf16[96,768]{1,0:T(8,128)(2,1)S(1)}, u32[]{:S(2)}, u32[]{:S(2)}) collective-permute-start(bf16[96,768]{1,0:T(8,128)(2,1)S(1)} %get-tuple-element.226), channel_id=1, source_target_pairs={{0,8},{1,9},{2,10},{3,11},{4,12},{5,13},{6,14},{7,15},{8,0},{9,1},... | collective-permute-start | bytes 442376 | tf_op jit(solution)/shard_map/ppermute | solution.py:350
  141.2 14.5 %collective-permute-start.40 = (bf16[96,768]{1,0:T(8,128)(2,1)S(1)}, bf16[96,768]{1,0:T(8,128)(2,1)S(1)}, u32[]{:S(2)}, u32[]{:S(2)}) collective-permute-start(bf16[96,768]{1,0:T(8,128)(2,1)S(1)} %get-tuple-element.227), channel_id=1, source_target_pairs={{0,16},{1,17},{2,18},{3,19},{4,20},{5,21},{6,22},{7,23},{8,24},{9,... | collective-permute-start | bytes 442376 | tf_op jit(solution)/shard_map/ppermute | solution.py:350
  143.1 13.1 %collective-permute-start.41 = (bf16[96,768]{1,0:T(8,128)(2,1)S(1)}, bf16[96,768]{1,0:T(8,128)(2,1)S(1)}, u32[]{:S(2)}, u32[]{:S(2)}) collective-permute-start(bf16[96,768]{1,0:T(8,128)(2,1)S(1)} %get-tuple-element.228), channel_id=1, source_target_pairs={{0,24},{1,25},{2,26},{3,27},{4,28},{5,29},{6,30},{7,31},{8,16},{9,... | collective-permute-start | bytes 442376 | tf_op jit(solution)/shard_map/ppermute | solution.py:350
  157.0 19.3 %collective-permute-start.44 = (bf16[4,144,768]{2,1,0:T(8,128)(2,1)S(1)}, bf16[4,144,768]{2,1,0:T(8,128)(2,1)S(1)}, u32[]{:S(2)}, u32[]{:S(2)}) collective-permute-start(bf16[4,144,768]{2,1,0:T(8,128)(2,1)S(1)} %join_far_body.1.refs_2_), channel_id=1, source_target_pairs={{0,4},{1,5},{2,6},{3,7},{4,0},{5,1},{6,2},{7,3},{8,12},{9,13},{10,... | collective-permute-start | bytes 2654216 | tf_op jit(solution)/shard_map/ppermute | solution.py:350
  157.9 16.0 %collective-permute-start.45 = (bf16[4,96,768]{2,1,0:T(8,128)(2,1)S(1)}, bf16[4,96,768]{2,1,0:T(8,128)(2,1)S(1)}, u32[]{:S(2)}, u32[]{:S(2)}) collective-permute-start(bf16[4,96,768]{2,1,0:T(8,128)(2,1)S(1)} %get-tuple-element.253), channel_id=1, source_target_pairs={{0,2},{1,3},{2,0},{3,1},{4,6},{5,7},{6,4},{7,5},{8,10},{9,11},{10,... | collective-permute-start | bytes 1769480 | tf_op jit(solution)/shard_map/ppermute | solution.py:350
  158.8 4.4 %collective-permute-start.46 = (bf16[96,768]{1,0:T(8,128)(2,1)S(1)}, bf16[96,768]{1,0:T(8,128)(2,1)S(1)}, u32[]{:S(2)}, u32[]{:S(2)}) collective-permute-start(bf16[96,768]{1,0:T(8,128)(2,1)S(1)} %get-tuple-element.256), channel_id=1, source_target_pairs={{0,8},{1,9},{2,10},{3,11},{4,12},{5,13},{6,14},{7,15},{8,0},{9,1},... | collective-permute-start | bytes 442376 | tf_op jit(solution)/shard_map/ppermute | solution.py:350
  159.3 6.1 %collective-permute-start.47 = (bf16[96,768]{1,0:T(8,128)(2,1)S(1)}, bf16[96,768]{1,0:T(8,128)(2,1)S(1)}, u32[]{:S(2)}, u32[]{:S(2)}) collective-permute-start(bf16[96,768]{1,0:T(8,128)(2,1)S(1)} %get-tuple-element.257), channel_id=1, source_target_pairs={{0,16},{1,17},{2,18},{3,19},{4,20},{5,21},{6,22},{7,23},{8,24},{9,... | collective-permute-start | bytes 442376 | tf_op jit(solution)/shard_map/ppermute | solution.py:350
  160.9 13.0 %collective-permute-start.48 = (bf16[96,768]{1,0:T(8,128)(2,1)S(1)}, bf16[96,768]{1,0:T(8,128)(2,1)S(1)}, u32[]{:S(2)}, u32[]{:S(2)}) collective-permute-start(bf16[96,768]{1,0:T(8,128)(2,1)S(1)} %get-tuple-element.258), channel_id=1, source_target_pairs={{0,24},{1,25},{2,26},{3,27},{4,28},{5,29},{6,30},{7,31},{8,16},{9,... | collective-permute-start | bytes 442376 | tf_op jit(solution)/shard_map/ppermute | solution.py:350
  176.4 26.5 %collective-permute-start.53 = (bf16[2,256,768]{2,1,0:T(8,128)(2,1)S(1)}, bf16[2,256,768]{2,1,0:T(8,128)(2,1)S(1)}, u32[]{:S(2)}, u32[]{:S(2)}) collective-permute-start(bf16[2,256,768]{2,1,0:T(8,128)(2,1)S(1)} %get-tuple-element.267), channel_id=1, source_target_pairs={{0,1},{1,0},{2,3},{3,2},{4,5},{5,4},{6,7},{7,6},{8,9},{9,8},{10,11... | collective-permute-start | bytes 2359304 | tf_op jit(solution)/shard_map/ppermute | solution.py:350
  179.2 23.7 %collective-permute-start.49 = (bf16[4,112,576]{2,1,0:T(8,128)(2,1)S(1)}, bf16[4,112,576]{2,1,0:T(8,128)(2,1)S(1)}, u32[]{:S(2)}, u32[]{:S(2)}) collective-permute-start(bf16[4,112,576]{2,1,0:T(8,128)(2,1)S(1)} %get-tuple-element.261), channel_id=1, source_target_pairs={{0,4},{1,5},{2,6},{3,7},{4,0},{5,1},{6,2},{7,3},{8,12},{9,13},{10,... | collective-permute-start | bytes 1548296 | tf_op jit(solution)/shard_map/ppermute | solution.py:350
  180.9 8.9 %collective-permute-start.50 = (bf16[144,768]{1,0:T(8,128)(2,1)S(1)}, bf16[144,768]{1,0:T(8,128)(2,1)S(1)}, u32[]{:S(2)}, u32[]{:S(2)}) collective-permute-start(bf16[144,768]{1,0:T(8,128)(2,1)S(1)} %get-tuple-element.264), channel_id=1, source_target_pairs={{0,8},{1,9},{2,10},{3,11},{4,12},{5,13},{6,14},{7,15},{8,0},{9,1},... | collective-permute-start | bytes 663560 | tf_op jit(solution)/shard_map/ppermute | solution.py:350
  181.3 11.7 %collective-permute-start.51 = (bf16[144,768]{1,0:T(8,128)(2,1)S(1)}, bf16[144,768]{1,0:T(8,128)(2,1)S(1)}, u32[]{:S(2)}, u32[]{:S(2)}) collective-permute-start(bf16[144,768]{1,0:T(8,128)(2,1)S(1)} %get-tuple-element.265), channel_id=1, source_target_pairs={{0,16},{1,17},{2,18},{3,19},{4,20},{5,21},{6,22},{7,23},{8,24},{9,... | collective-permute-start | bytes 663560 | tf_op jit(solution)/shard_map/ppermute | solution.py:350
  182.9 19.9 %collective-permute-start.52 = (bf16[144,768]{1,0:T(8,128)(2,1)S(1)}, bf16[144,768]{1,0:T(8,128)(2,1)S(1)}, u32[]{:S(2)}, u32[]{:S(2)}) collective-permute-start(bf16[144,768]{1,0:T(8,128)(2,1)S(1)} %get-tuple-element.266), channel_id=1, source_target_pairs={{0,24},{1,25},{2,26},{3,27},{4,28},{5,29},{6,30},{7,31},{8,16},{9,... | collective-permute-start | bytes 663560 | tf_op jit(solution)/shard_map/ppermute | solution.py:350
  203.9 20.6 %collective-permute-start.58 = (bf16[336,768]{1,0:T(8,128)(2,1)}, bf16[336,768]{1,0:T(8,128)(2,1)}, u32[]{:S(2)}, u32[]{:S(2)}) collective-permute-start(bf16[336,768]{1,0:T(8,128)(2,1)} %pad_maximum_fusion.6), channel_id=1, source_target_pairs={{0,2},{1,3},{2,0},{3,1},{4,6},{5,7},{6,4},{7,5},{8,10},{9,11},{10,... | collective-permute-start | bytes 1548296 | tf_op jit(solution)/shard_map/ppermute | solution.py:350
  205.0 19.5 %collective-permute-start.57 = (bf16[256,768]{1,0:T(8,128)(2,1)}, bf16[256,768]{1,0:T(8,128)(2,1)}, u32[]{:S(2)}, u32[]{:S(2)}) collective-permute-start(bf16[256,768]{1,0:T(8,128)(2,1)} %fusion.7), channel_id=1, source_target_pairs={{0,2},{1,3},{2,0},{3,1},{4,6},{5,7},{6,4},{7,5},{8,10},{9,11},{10,... | collective-permute-start | bytes 1179656 | tf_op jit(solution)/shard_map/ppermute | solution.py:350
  207.0 4.4 %collective-permute-start.54 = (bf16[112,576]{1,0:T(8,128)(2,1)S(1)}, bf16[112,576]{1,0:T(8,128)(2,1)S(1)}, u32[]{:S(2)}, u32[]{:S(2)}) collective-permute-start(bf16[112,576]{1,0:T(8,128)(2,1)S(1)} %get-tuple-element.276), channel_id=1, source_target_pairs={{0,8},{1,9},{2,10},{3,11},{4,12},{5,13},{6,14},{7,15},{8,0},{9,1},... | collective-permute-start | bytes 387080 | tf_op jit(solution)/shard_map/ppermute | solution.py:350
  207.1 6.6 %collective-permute-start.55 = (bf16[112,576]{1,0:T(8,128)(2,1)S(1)}, bf16[112,576]{1,0:T(8,128)(2,1)S(1)}, u32[]{:S(2)}, u32[]{:S(2)}) collective-permute-start(bf16[112,576]{1,0:T(8,128)(2,1)S(1)} %get-tuple-element.277), channel_id=1, source_target_pairs={{0,16},{1,17},{2,18},{3,19},{4,20},{5,21},{6,22},{7,23},{8,24},{9,... | collective-permute-start | bytes 387080 | tf_op jit(solution)/shard_map/ppermute | solution.py:350
  209.1 12.9 %collective-permute-start.56 = (bf16[112,576]{1,0:T(8,128)(2,1)S(1)}, bf16[112,576]{1,0:T(8,128)(2,1)S(1)}, u32[]{:S(2)}, u32[]{:S(2)}) collective-permute-start(bf16[112,576]{1,0:T(8,128)(2,1)S(1)} %get-tuple-element.278), channel_id=1, source_target_pairs={{0,24},{1,25},{2,26},{3,27},{4,28},{5,29},{6,30},{7,31},{8,16},{9,... | collective-permute-start | bytes 387080 | tf_op jit(solution)/shard_map/ppermute | solution.py:350
  231.1 16.9 %collective-permute-start.61 = (bf16[432,768]{1,0:T(8,128)(2,1)}, bf16[432,768]{1,0:T(8,128)(2,1)}, u32[]{:S(2)}, u32[]{:S(2)}) collective-permute-start(bf16[432,768]{1,0:T(8,128)(2,1)} %get-tuple-element.329), channel_id=1, source_target_pairs={{0,1},{1,0},{2,3},{3,2},{4,5},{5,4},{6,7},{7,6},{8,9},{9,8},{10,11... | collective-permute-start | bytes 1990664 | tf_op jit(solution)/shard_map/ppermute | solution.py:350
  233.5 5.5 %collective-permute-start.59 = (bf16[112,576]{1,0:T(8,128)(2,1)S(1)}, bf16[112,576]{1,0:T(8,128)(2,1)S(1)}, u32[]{:S(2)}, u32[]{:S(2)}) collective-permute-start(bf16[112,576]{1,0:T(8,128)(2,1)S(1)} %add_convert_fusion.5), channel_id=1, source_target_pairs={{0,2},{1,3},{2,0},{3,1},{4,6},{5,7},{6,4},{7,5},{8,10},{9,11},{10,... | collective-permute-start | bytes 387080 | tf_op jit(solution)/shard_map/ppermute | solution.py:350
  239.0 3.0 %collective-permute-start.60 = (bf16[2,112,576]{2,1,0:T(8,128)(2,1)S(1)}, bf16[2,112,576]{2,1,0:T(8,128)(2,1)S(1)}, u32[]{:S(2)}, u32[]{:S(2)}) collective-permute-start(bf16[2,112,576]{2,1,0:T(8,128)(2,1)S(1)} %pad_maximum_fusion.8), channel_id=1, source_target_pairs={{0,1},{1,0},{2,3},{3,2},{4,5},{5,4},{6,7},{7,6},{8,9},{9,8},{10,11... | collective-permute-start | bytes 774152 | tf_op jit(solution)/shard_map/ppermute | solution.py:350
  (13 other events, 35.2 us)
